TPU v7x, 32 devices: a whole 2x2x4 slice. The times are simulated.
32 devices in a mesh: band: 16 (over z, y, core), helper: 2 (over x).
Axes of the slice: x: 2, y: 2, z: 4, core: 2. Of those that a mesh axis runs over, the one named last changes fastest.
Arguments:
- node_latent: bfloat16 [2048, 256], P(('band', 'helper')), may hold values from -6 to 6
- edge_latent: bfloat16 [32768, 256], P(('band', 'helper')), may hold values from -6 to 6
- grad_out_node: bfloat16 [2048, 256], P(('band', 'helper')), may hold values from -6 to 6
- grad_out_edge: bfloat16 [32768, 256], P(('band', 'helper')), may hold values from -6 to 6
- senders: int32 [32768], P(('band', 'helper')), may hold values from 0 to 191
- receivers: int32 [32768], P(('band', 'helper')), may hold values from 0 to 127, as said below
- band_edges: int32 [16], replicated, may hold values from 2 to 16, as said below
- halo_list: int32 [16, 32], P('band'), may hold values from 0 to 127, as said below
- sea_mask: int32 [2048], P(('band', 'helper')), may hold values 0 or 1
- edge_w1: bfloat16 [768, 256], replicated, may hold values from -0.21875 to 0.21875
- edge_b1: float32 [256], replicated, may hold values from -3 to 3
- edge_w2: bfloat16 [256, 256], replicated, may hold values from -0.375 to 0.375
- edge_b2: float32 [256], replicated, may hold values from -3 to 3
- node_w1: bfloat16 [512, 256], replicated, may hold values from -0.25 to 0.25
- node_b1: float32 [256], replicated, may hold values from -3 to 3
- node_w2: bfloat16 [256, 256], replicated, may hold values from -0.375 to 0.375
- node_b2: float32 [256], replicated, may hold values from -3 to 3
Outputs:
- grad_node: float32 [2048, 256], P(('band', 'helper'))
- grad_edge: bfloat16 [32768, 256], P(('band', 'helper'))
- grad_edge_w1: float32 [768, 256], replicated
- grad_edge_b1: float32 [256], replicated
- grad_edge_w2: float32 [256, 256], replicated
- grad_edge_b2: float32 [256], replicated
- grad_node_w1: float32 [512, 256], replicated
- grad_node_b1: float32 [256], replicated
- grad_node_w2: float32 [256, 256], replicated
- grad_node_b2: float32 [256], replicated
Inputs may be any that keep to these rules, and one draw needn't show every extreme that they name: In every aligned block of 128 edge rows, all receivers lie in one aligned tile of 64 nodes. `band_edges`: A quarter of the bands, consecutive along the cycle, hold 16 live blocks; every other band holds between 2 and 6. `halo_list`: the 32 entries of a band are distinct.
All inputs are finite; a program needn't handle non-finite values. No bound on the sum of `sea_mask` on one device may be relied on, other than what follows from the above.
Results may differ from a plain program's by a relative error of at most 0.01.
Values may be sent and summed in bfloat16 or wider, within the bound.
No kernel may reach another device: no remote copies, remote signals or barrier semaphores. Data moves between devices by JAX's collectives and lax.ppermute only.
A program may use at most 64 MiB of HBM per device.

v0:
```python
import math

import jax
import jax.numpy as jnp
from jax import lax
from jax.experimental import pallas as pl
from jax.experimental.pallas import tpu as pltpu
from jax.sharding import PartitionSpec as P


EB = 128
LANES = 128
NORM_EPS = 1e-05
BF = jnp.bfloat16
F32 = jnp.float32
AXES = ("band", "helper")
VMEM_LIMIT = 24 * 1024 * 1024


def round_up(size, unit):
    return -(-size // unit) * unit


def dot(left, right):
    return jnp.dot(left, right, preferred_element_type=F32)


def dot_left_t(left, right):
    return lax.dot_general(left, right, (((0,), (0,)), ((), ())), preferred_element_type=F32)


def dot_right_t(left, right):
    return lax.dot_general(left, right, (((1,), (1,)), ((), ())), preferred_element_type=F32)


def normalise(pre):
    centre = pre - jnp.mean(pre, axis=-1, keepdims=True)
    inv = lax.rsqrt(jnp.mean(centre * centre, axis=-1, keepdims=True) + NORM_EPS)
    return centre * inv, inv


def norm_back(grad, normed, inv):
    return inv * (
        grad
        - jnp.mean(grad, axis=-1, keepdims=True)
        - normed * jnp.mean(grad * normed, axis=-1, keepdims=True)
    )


def ids_down_rows(ids_row):
    return jnp.broadcast_to(ids_row, (LANES, LANES)).T


def onehot_rows(ids_cols, width):
    rows = ids_cols[0].shape[0]
    lane = lax.broadcasted_iota(jnp.int32, (rows, LANES), 1)
    tiles = []
    for start in range(0, width, LANES):
        hit = ids_cols[0] == lane + start
        for more in ids_cols[1:]:
            hit = hit | (more == lane + start)
        tiles.append(jnp.where(hit, 1.0, 0.0).astype(BF))
    return jnp.concatenate(tiles, axis=1)


def onehot_cols(ids_rows, height):
    count = ids_rows[0].shape[1]
    down = lax.broadcasted_iota(jnp.int32, (height, count), 0)
    hit = ids_rows[0] == down
    for more in ids_rows[1:]:
        hit = hit | (more == down)
    return jnp.where(hit, 1.0, 0.0).astype(BF)


def call(kernel, out_shape, args, scratch=(), hbm_out=(), flops=0):
    in_specs = [pl.BlockSpec(memory_space=pltpu.VMEM)] * len(args)
    out_specs = [
        pl.BlockSpec(memory_space=pl.ANY if i in hbm_out else pltpu.VMEM)
        for i in range(len(out_shape))
    ]
    nbytes = sum(a.size * a.dtype.itemsize for a in args)
    nbytes += sum(math.prod(o.shape) * o.dtype.itemsize for o in out_shape)
    return pl.pallas_call(
        kernel,
        out_shape=out_shape,
        in_specs=in_specs,
        out_specs=out_specs,
        scratch_shapes=list(scratch),
        compiler_params=pltpu.CompilerParams(vmem_limit_bytes=VMEM_LIMIT),
        cost_estimate=pl.CostEstimate(flops=flops, bytes_accessed=nbytes, transcendentals=0),
    )(*args)


def sds(rows, cols, dtype):
    return jax.ShapeDtypeStruct((rows, cols), dtype)


class Groups:
    def __init__(self, bands, helpers):
        self.bands = bands
        self.helpers = helpers
        self.core = 2 if bands % 2 == 0 else 1
        rest = bands // self.core
        self.near = 2 if (helpers <= 2 and rest % 2 == 0) else 1
        self.group = self.near * helpers
        far = rest // self.near
        self.far_rounds = []
        stride = self.core * self.near
        while far > 1:
            size = 4 if far % 4 == 0 else 2
            self.far_rounds.append((stride, size))
            stride *= size
            far //= size

        self.crossed = (
            self.core == 2 and len(self.far_rounds) == 1 and self.far_rounds[0][1] == self.group
        )

    def permute(self, array, move):
        pairs = []
        for band in range(self.bands):
            for helper in range(self.helpers):
                to_band, to_helper = move(band, helper)
                pairs.append((band * self.helpers + helper, to_band * self.helpers + to_helper))
        return lax.ppermute(array, AXES, pairs)

    def core_swap(self, array):
        return self.permute(array, lambda b, h: (b ^ 1, h))

    def helper_swap(self, array, k):
        return self.permute(array, lambda b, h: (b, h ^ k))

    def near_move(self, band, helper, k):
        near, help_k = divmod(k, self.helpers)
        return band ^ (near * self.core), helper ^ help_k

    def first_swap(self, array, k):
        def move(band, helper):
            if self.crossed and band % 2:
                return band ^ (k * self.far_rounds[0][0]), helper
            return self.near_move(band, helper, k)

        return self.permute(array, move)

    def second_swap(self, array, stride, k):
        def move(band, helper):
            if self.crossed and band % 2:
                return self.near_move(band, helper, k)
            return band ^ (k * stride), helper

        return self.permute(array, move)

    def ring(self, array, by):
        return self.permute(array, lambda b, h: ((b + by) % self.bands, h))

    def core_id(self):
        return lax.rem(lax.axis_index("band"), self.core)

    def first_id(self, core):
        band = lax.axis_index("band")
        near = lax.rem(lax.div(band, self.core), self.near)
        near = near * self.helpers + lax.axis_index("helper")
        if not self.crossed:
            return near
        return jnp.where(core == 1, lax.div(band, self.core * self.near), near)


def tree_sum(parts):
    parts = list(parts)
    while len(parts) > 1:
        parts = [parts[i] + parts[i + 1] for i in range(0, len(parts), 2)]
    return parts[0]


def on_device(
    node_latent,
    edge_latent,
    grad_out_node,
    grad_out_edge,
    senders,
    receivers,
    band_edges,
    halo_list,
    sea_mask,
    edge_w1,
    edge_b1,
    edge_w2,
    edge_b2,
    node_w1,
    node_b1,
    node_w2,
    node_b2,
):
    helpers = lax.axis_size("helper")
    bands = lax.axis_size("band")
    groups = Groups(bands, helpers)
    own, feat = node_latent.shape
    band = own * helpers
    halo = halo_list.shape[1]
    edges = edge_latent.shape[0]
    slots = edges // EB
    look = band + 2 * halo
    chunk = 2 * EB if slots % 2 == 0 else EB
    per_chunk = chunk // EB
    edge_scale = 1.0 / math.sqrt(edges * helpers * bands)
    node_share = 1.0 / math.sqrt(own * helpers * bands) / helpers
    unit = edges * feat * feat * 2

    send_ids = senders.reshape(slots, EB)
    recv_ids = receivers.reshape(slots, EB)

    group = groups.group
    pieces = groups.core * group
    slices = [edge_w1.shape[0] // pieces, edge_w2.shape[0] // pieces, 8]
    n_slices = [node_w1.shape[0] // pieces, node_w2.shape[0] // pieces]
    e_piece, n_piece = sum(slices), sum(n_slices)
    piece = e_piece + n_piece
    half = piece * group
    starts = [0, slices[0], e_piece, e_piece + n_slices[0]]
    heights = [slices[0], slices[1], n_slices[0], n_slices[1]]
    at_bias = slices[0] + slices[1]

    def chunk_ids(ref, index):
        return jnp.concatenate(
            [
                ids_down_rows(ref[pl.ds(index * per_chunk + j, 1), :])
                for j in range(per_chunk)
            ],
            axis=0,
        )

    def chunk_row(ref, index):
        return jnp.concatenate(
            [ref[pl.ds(index * per_chunk + j, 1), :] for j in range(per_chunk)], axis=1
        )

    def chunk_live(ref, index):
        rows = [
            jnp.broadcast_to(ref[pl.ds(index * per_chunk + j, 1), :], (EB, feat))
            for j in range(per_chunk)
        ]
        return jnp.concatenate(rows, axis=0)

    b_width = round_up(2 * band, LANES)
    h_width = round_up(2 * halo, LANES)
    r_width = round_up(band, LANES)

    theirs = [groups.helper_swap(node_latent, k) for k in range(1, helpers)]

    def gather_kernel(halo_ref, *refs):
        parts, (band_ref, out_ref) = refs[:helpers], refs[helpers:]
        me = lax.axis_index("helper")
        for k in range(helpers):
            at = pl.multiple_of((me ^ k) * own, own)
            band_ref[pl.ds(at, own), :] = parts[k][...]
        pick = onehot_cols([halo_ref[...]], band)
        out_ref[...] = dot_left_t(pick, band_ref[...]).astype(BF)

    band_rows, outgoing = call(
        gather_kernel, [sds(band, feat, BF), sds(halo, feat, BF)], [halo_list, node_latent, *theirs]
    )
    from_prev = groups.ring(outgoing, 1)
    from_next = groups.ring(outgoing, -1)

    def split_store(table, height, at, proj):
        high = proj.astype(BF)
        table[at : at + proj.shape[0], :] = high
        table[height + at : height + at + proj.shape[0], :] = (proj - high.astype(F32)).astype(BF)

    def local_kernel(
        send_ref, recv_ref, band_ref, e_ref, w1_ref, b1_ref, b2_ref, nb1_ref, nb2_ref, be_ref,
        sea_ref, pre_ref, place_ref, recv_pick_ref, halo_pick_ref, et_ref, bias_ref, live_ref,
        sea_diag_ref, table,
    ):
        for i, ref in enumerate((b1_ref, b2_ref, nb1_ref, nb2_ref)):
            bias_ref[i, :] = ref[...]
        counts = be_ref[...][None, :]
        mine = lax.broadcasted_iota(jnp.int32, counts.shape, 1) == lax.axis_index("band")
        count = jnp.sum(jnp.where(mine, counts, 0), axis=1, keepdims=True)
        slot = lax.broadcasted_iota(jnp.int32, (slots, feat), 0)
        live_ref[...] = jnp.where(
            slot * helpers + lax.axis_index("helper") < count, 1.0, 0.0
        )
        down = lax.broadcasted_iota(jnp.int32, (own, own), 0)
        across = lax.broadcasted_iota(jnp.int32, (own, own), 1)
        sea_diag_ref[...] = jnp.where(
            (down == across) & (sea_ref[...][None, :] != 0), 1.0, 0.0
        ).astype(BF)
        if b_width > 2 * band:
            table[...] = jnp.zeros_like(table)
        for at, rows in ((0, slice(0, feat)), (band, slice(feat, 2 * feat))):
            split_store(table, b_width, at, dot(band_ref[...], w1_ref[rows, :]))
        for i in range(edges // chunk):
            rows = pl.ds(i * chunk, chunk)
            send_cols = chunk_ids(send_ref, i)
            recv_cols = chunk_ids(recv_ref, i)
            halo_pick_ref[rows, :] = onehot_rows([send_cols - band], h_width)
            recv_pick_ref[rows, :] = onehot_rows([recv_cols], r_width)
            place_ref[:, rows] = onehot_cols(
                [chunk_row(send_ref, i), chunk_row(recv_ref, i) + look], look + band
            )
            send_cols = jnp.where(send_cols < band, send_cols, -1)
            pick = onehot_rows([send_cols, recv_cols + band], b_width)
            pre = dot(jnp.concatenate([pick, pick], axis=1), table[...])
            e_rows = e_ref[rows, :]
            pre_ref[rows, :] = pre + dot(e_rows, w1_ref[2 * feat :, :]) + b1_ref[...][None, :]
            et_ref[:, rows] = e_rows.T

    pre_local, place, recv_pick, halo_pick, edge_t, biases, live, sea_diag = call(
        local_kernel,
        [
            sds(edges, feat, F32), sds(look + band, edges, BF), sds(edges, r_width, BF),
            sds(edges, h_width, BF), sds(feat, edges, BF), sds(4, feat, F32),
            sds(slots, feat, F32), sds(own, own, BF),
        ],
        [send_ids, recv_ids, band_rows, edge_latent, edge_w1, edge_b1, edge_b2, node_b1, node_b2,
         band_edges, sea_mask],
        scratch=[pltpu.VMEM((2 * b_width, feat), BF)],
        flops=4 * unit,
    )

    def forward_kernel(
        live_ref, pre_ref, place_ref, halo_pick_ref, prev_ref, next_ref, w1_ref, w2_ref, bias_ref,
        gon_ref, sea_ref, hid_ref, slope_ref, norm_ref, inv_ref, agg, swap_ref, table,
    ):
        if h_width > 2 * halo:
            table[...] = jnp.zeros_like(table)
        halo_rows = jnp.concatenate([prev_ref[...], next_ref[...]], axis=0)
        split_store(table, h_width, 0, dot(halo_rows, w1_ref[...]))
        for i in range(edges // chunk):
            rows = pl.ds(i * chunk, chunk)
            pick = halo_pick_ref[rows, :]
            pre = pre_ref[rows, :] + dot(jnp.concatenate([pick, pick], axis=1), table[...])
            sig = jax.nn.sigmoid(pre)
            hidden = (pre * sig).astype(BF)
            hid_ref[rows, :] = hidden
            slope_ref[rows, :] = sig * (1.0 + pre * (1.0 - sig))
            normed, inv = normalise(dot(hidden, w2_ref[...]) + bias_ref[1:2, :])
            norm_ref[rows, :] = normed
            inv_ref[rows, :] = inv
            message = (normed * chunk_live(live_ref, i)).astype(BF)
            part = dot(place_ref[look:, rows], message)
            if i == 0:
                agg[...] = part
            else:
                agg[...] += part
        swap_ref[:band, :] = agg[...].astype(BF)
        swap_ref[band:, :] = dot(sea_ref[...], gon_ref[...]).astype(BF)

    hidden, slope, normed, inv, agg_own, swap_own = call(
        forward_kernel,
        [sds(edges, feat, BF), sds(edges, feat, F32), sds(edges, feat, F32), sds(edges, 1, F32),
         sds(band, feat, F32), sds(band + own, feat, BF)],
        [live, pre_local, place, halo_pick, from_prev, from_next, edge_w1[:feat], edge_w2,
         biases, grad_out_node, sea_diag],
        scratch=[pltpu.VMEM((2 * h_width, feat), BF)],
        flops=3 * unit,
    )

    swaps = [swap_own] + [groups.helper_swap(swap_own, k) for k in range(1, helpers)]

    def backward_kernel(
        live_ref, place_ref, recv_pick_ref, band_ref, prev_ref, next_ref, et_ref, geo_ref,
        hid_ref, slope_ref, norm_ref, inv_ref, w1_ref, w2_ref, nw1_ref, nw2_ref, bias_ref,
        agg_ref, *refs,
    ):
        parts = refs[:helpers]
        edge_hbm, keep_ref, give_ref, lg_ref, din_ref, grads, sums, seed, edge_ref, sems = refs[helpers:]
        edge_copies = []
        band_v = band_ref[...]
        me = lax.axis_index("helper")
        for k in range(helpers):
            seed[pl.ds(pl.multiple_of((me ^ k) * own, own), own), :] = parts[k][band:, :]
        agg = tree_sum([agg_ref[...]] + [p[:band, :].astype(F32) for p in parts[1:]]).astype(BF)
        node_in = jnp.concatenate([band_v, agg], axis=1)
        n_pre = dot(node_in, nw1_ref[...]) + bias_ref[2:3, :]
        n_sig = jax.nn.sigmoid(n_pre)
        n_hidden = (n_pre * n_sig).astype(BF)
        n_normed, n_inv = normalise(dot(n_hidden, nw2_ref[...]) + bias_ref[3:4, :])
        n_dz = norm_back(seed[...].astype(F32), n_normed, n_inv)
        n_dzb = n_dz.astype(BF)
        n_dpre = dot_right_t(n_dzb, nw2_ref[...]) * (n_sig * (1.0 + n_pre * (1.0 - n_sig)))
        n_dpreb = n_dpre.astype(BF)
        din_ref[...] = dot_right_t(n_dpreb, nw1_ref[:feat, :])
        agg_grad = dot_right_t(n_dpreb, nw1_ref[feat:, :]).astype(BF)

        def put(which, first, value):
            high, row, count = heights[which], 0, value.shape[0]
            while row < count:
                spot, within = divmod(first + row, high)
                take = min(high - within, count - row)
                at = spot * piece + starts[which] + within
                grads[at : at + take, :] = value[row : row + take, :]
                row += take

        put(2, 0, dot_left_t(node_in, n_dpreb) * node_share)
        put(3, 0, dot_left_t(n_hidden, n_dzb) * node_share)
        gb_n1 = jnp.sum(n_dpre, axis=0, keepdims=True) * node_share
        gb_n2 = jnp.sum(n_dz, axis=0, keepdims=True) * node_share

        w1e = w1_ref[2 * feat :, :]
        gb_1 = jnp.zeros((1, feat), F32)
        gb_2 = jnp.zeros((1, feat), F32)
        gw_1 = jnp.zeros((feat, feat), F32)
        gw_2 = jnp.zeros((feat, feat), F32)
        for i in range(edges // chunk):
            rows = pl.ds(i * chunk, chunk)
            live = chunk_live(live_ref, i)
            geo = geo_ref[rows, :].astype(F32)
            at_recv = dot(recv_pick_ref[rows, :band], agg_grad)
            msg_grad = (geo + at_recv) * live
            dz = norm_back(msg_grad, norm_ref[rows, :], inv_ref[rows, :])
            gb_2 = gb_2 + jnp.sum(dz, axis=0, keepdims=True)
            dzb = dz.astype(BF)
            gw_2 = gw_2 + dot_left_t(hid_ref[rows, :], dzb)
            dpre = dot_right_t(dzb, w2_ref[...]) * slope_ref[rows, :]
            gb_1 = gb_1 + jnp.sum(dpre, axis=0, keepdims=True)
            dpreb = dpre.astype(BF)
            gw_1 = gw_1 + dot(et_ref[:, rows], dpreb)
            edge_ref[rows, :] = ((geo + dot_right_t(dpreb, w1e)) * live).astype(BF)
            edge_copies.append(
                pltpu.make_async_copy(edge_ref.at[rows, :], edge_hbm.at[rows, :], sems.at[i])
            )
            edge_copies[-1].start()
            part = dot(place_ref[:, rows], dpreb)
            if i == 0:
                sums[...] = part
            else:
                sums[...] += part
        at_send = sums[:look, :].astype(BF)
        at_recv = sums[look:, :].astype(BF)
        lookup = jnp.concatenate([band_v, prev_ref[...], next_ref[...]], axis=0)
        look_grad = dot_right_t(at_send, w1_ref[:feat, :])
        recv_grad = dot_right_t(at_recv, w1_ref[feat : 2 * feat, :])
        lg_ref[:band, :] = (look_grad[:band, :] + recv_grad).astype(BF)
        lg_ref[band:, :] = look_grad[band:, :].astype(BF)
        put(0, 0, dot_left_t(lookup, at_send) * edge_scale)
        put(0, feat, dot_left_t(band_v, at_recv) * edge_scale)
        put(0, 2 * feat, gw_1 * edge_scale)
        put(1, 0, gw_2 * edge_scale)
        bias = [gb_1 * edge_scale, gb_2 * edge_scale, gb_n1, gb_n2]
        grads[at_bias : at_bias + 8, :] = jnp.concatenate(bias + [jnp.zeros((4, feat), F32)], axis=0)
        for p in range(1, pieces):
            grads[p * piece + at_bias : p * piece + at_bias + 8, :] = jnp.zeros((8, feat), F32)
        core = groups.core_id()
        other = groups.core - 1 - core
        keep_ref[...] = grads[pl.ds(pl.multiple_of(core * half, 8), half), :]
        give_ref[...] = grads[pl.ds(pl.multiple_of(other * half, 8), half), :].astype(BF)
        for copy in edge_copies:
            copy.wait()

    grad_edge, keep, give, look_grad, node_din = call(
        backward_kernel,
        [sds(edges, feat, BF), sds(half, feat, F32), sds(half, feat, BF), sds(look, feat, BF),
         sds(band, feat, F32)],
        [live, place, recv_pick, band_rows, from_prev, from_next, edge_t, grad_out_edge,
         hidden, slope, normed, inv, edge_w1, edge_w2, node_w1, node_w2, biases, agg_own, *swaps],
        scratch=[pltpu.VMEM((half * groups.core, feat), F32), pltpu.VMEM((look + band, feat), F32),
                 pltpu.VMEM((band, feat), BF), pltpu.VMEM((edges, feat), BF),
                 pltpu.SemaphoreType.DMA((edges // chunk,))],
        hbm_out=(0,),
        flops=8 * unit,
    )

    got = groups.core_swap(give)
    looks = [look_grad] + [groups.helper_swap(look_grad, k) for k in range(1, helpers)]

    def split_kernel(keep_ref, got_ref, own_ref, *refs):
        outs, summed = refs[:-1], refs[-1]
        summed[...] = keep_ref[...] + got_ref[...].astype(F32)
        me = groups.first_id(groups.core_id())
        own_ref[...] = summed[pl.ds(pl.multiple_of(me * piece, 8), piece), :]
        for k in range(1, group):
            part = summed[pl.ds(pl.multiple_of((me ^ k) * piece, 8), piece), :]
            outs[k - 1][...] = part.astype(BF)

    own_part, *to_group = call(
        split_kernel,
        [sds(piece, feat, F32)] + [sds(piece, feat, BF)] * (group - 1),
        [keep, got],
        scratch=[pltpu.VMEM((half, feat), F32)],
    )
    from_group = [groups.first_swap(part, k) for k, part in enumerate(to_group, 1)]

    def look_kernel(*refs):
        parts, (mine_ref, prev_ref, next_ref) = refs[:helpers], refs[helpers:]
        at = pl.multiple_of(lax.axis_index("helper") * own, own)
        mine_ref[...] = tree_sum([g[pl.ds(at, own), :].astype(F32) for g in parts])
        halos = tree_sum([g[band:, :].astype(F32) for g in parts])
        prev_ref[...] = halos[:halo, :].astype(BF)
        next_ref[...] = halos[halo:, :].astype(BF)

    own_grad, prev_grad, next_grad = call(
        look_kernel, [sds(own, feat, F32), sds(halo, feat, BF), sds(halo, feat, BF)], looks
    )
    halo_back = groups.ring(prev_grad, -1)
    halo_forth = groups.ring(next_grad, 1)

    def join_kernel(own_ref, *refs):
        parts, piece_ref = refs[: group - 1], refs[group - 1]
        summed = own_ref[...]
        for part in parts:
            summed = summed + part[...].astype(F32)
        piece_ref[...] = summed.astype(BF)

    (piece_sum,) = call(join_kernel, [sds(piece, feat, BF)], [own_part, *from_group])

    halo_sums = None
    for stride, size in groups.far_rounds:
        swapped = [piece_sum] + [groups.second_swap(piece_sum, stride, k) for k in range(1, size)]
        first = halo_sums is None

        def far_kernel(*refs):
            parts, rest = refs[:size], refs[size:]
            rest[-1][...] = tree_sum([r[...].astype(F32) for r in parts]).astype(BF)
            if first:
                halo_ref, back_ref, forth_ref, out_ref, _ = rest
                at = lax.axis_index("helper") * own
                place = onehot_cols([halo_ref[...] - at], own)
                out_ref[...] = dot(place, back_ref[...]) + dot(place, forth_ref[...])

        if first:
            halo_sums, piece_sum = call(
                far_kernel,
                [sds(own, feat, F32), sds(piece, feat, BF)],
                swapped + [halo_list, halo_back, halo_forth],
            )
        else:
            (piece_sum,) = call(far_kernel, [sds(piece, feat, BF)], swapped)

    gathered = [piece_sum] + [groups.first_swap(piece_sum, k) for k in range(1, group)]
    vec = jax.ShapeDtypeStruct((feat,), F32)
    out_shape = [
        jax.ShapeDtypeStruct(edge_w1.shape, F32), vec, jax.ShapeDtypeStruct(edge_w2.shape, F32),
        vec, jax.ShapeDtypeStruct(node_w1.shape, F32), vec,
        jax.ShapeDtypeStruct(node_w2.shape, F32), vec,
    ]

    def place_pieces(parts, spots, outs, buf, row, sems):
        copies = []
        for i, (part, spot) in enumerate(zip(parts, spots)):
            buf[i * piece : (i + 1) * piece, :] = part[...].astype(F32)
            for j, (start, high, out) in enumerate(zip(starts, heights, outs[::2])):
                copies.append(
                    pltpu.make_async_copy(
                        buf.at[pl.ds(i * piece + start, high), :],
                        out.at[pl.ds(pl.multiple_of(spot * high, 8), high), :],
                        sems.at[i, j],
                    )
                )
                copies[-1].start()
        for i, spot in enumerate(spots):

            @pl.when(spot == 0)
            def _():
                for j, out in enumerate(outs[1::2]):
                    row[j][...] = buf[i * piece + at_bias + j, :]
                    pltpu.make_async_copy(row[j], out, sems.at[len(parts), j]).start()
                for j, out in enumerate(outs[1::2]):
                    pltpu.make_async_copy(row[j], out, sems.at[len(parts), j]).wait()

        for copy in copies:
            copy.wait()

    def place_call(keys, held, node=None):
        count = len(keys)
        parts = [sources[which, k] for which, k in keys]
        extra = [] if node is None else node

        def kernel(*refs):
            part_refs, refs = refs[:count], refs[count:]
            node_refs, refs = refs[: len(extra)], refs[len(extra) + len(held) :]
            if extra:
                node_out, *refs = refs
                halo_ref, mine_ref, din_ref, gon_ref = node_refs
                at = pl.multiple_of(lax.axis_index("helper") * own, own)
                node_out[...] = (
                    halo_ref[...] + mine_ref[...] + din_ref[pl.ds(at, own), :]
                    + gon_ref[...].astype(F32)
                )
            outs, (buf, *row, sems) = refs[:8], refs[8:]
            spots = []
            for which, k in keys:
                core = groups.core - 1 - groups.core_id() if which else groups.core_id()
                spots.append(core * group + (groups.first_id(core) ^ k))
            place_pieces(part_refs, spots, outs, buf, row, sems)

        vmem, hbm = pl.BlockSpec(memory_space=pltpu.VMEM), pl.BlockSpec(memory_space=pl.ANY)
        node_out = [sds(own, feat, F32)] if extra else []
        return pl.pallas_call(
            kernel,
            out_shape=node_out + out_shape,
            in_specs=[vmem] * (count + len(extra)) + [hbm] * len(held),
            out_specs=[vmem] * len(node_out) + [hbm] * 8,
            scratch_shapes=[pltpu.VMEM((count * piece, feat), F32)]
            + [pltpu.VMEM((feat,), F32)] * 4
            + [pltpu.SemaphoreType.DMA((count + 1, 4))],
            input_output_aliases={count + len(extra) + i: i for i in range(len(held))},
            compiler_params=pltpu.CompilerParams(vmem_limit_bytes=VMEM_LIMIT),
            cost_estimate=pl.CostEstimate(
                flops=0, bytes_accessed=6 * count * piece * feat, transcendentals=0
            ),
        )(*parts, *extra, *held)

    sources = {(0, k): part for k, part in enumerate(gathered)}
    sources[1, 0] = groups.core_swap(piece_sum)
    grad_node, *weight_grads = place_call(
        [(0, 0), (1, 0)], [], [halo_sums, own_grad, node_din, grad_out_node]
    )
    tops = range(group - 1, 0, -1)
    for i, k in enumerate(tops):
        if i < 2:
            sources[0, k], *weight_grads = lax.optimization_barrier(
                (sources[0, k], *weight_grads)
            )
        sources[1, k] = groups.core_swap(sources[0, k])
        if i == 0:
            weight_grads = place_call([(0, k)], weight_grads)
    third = [(0, k) for k in tops[1:]] + [(1, k) for k in tops[:1]]
    weight_grads = place_call(third, weight_grads)
    weight_grads = place_call([(1, k) for k in tops[1:]], weight_grads)
    return (grad_node, grad_edge, *weight_grads)


def solution(mesh):
    rows = P(AXES, None)
    flat = P(AXES)
    in_specs = (
        rows, rows, rows, rows, flat, flat, P(), P("band", None), flat,
        P(), P(), P(), P(), P(), P(), P(), P(),
    )
    out_specs = (rows, rows) + (P(),) * 8

    return jax.shard_map(
        on_device, mesh=mesh, in_specs=in_specs, out_specs=out_specs, check_vma=False
    )
```

profile of v0, /device:TPU:0, one launch (start us, length us, event | category | flops | bytes accessed | tf_op | source)
XLA Modules:
  0.0 61.3 jit_solution(5197957745444295227)
XLA Ops:
  0.7 3.0 %collective-permute-start = (bf16[64,256]{1,0:T(8,128)(2,1)}, bf16[64,256]{1,0:T(8,128)(2,1)S(1)}, u32[]{:S(2)}, u32[]{:S(2)}) collective-permute-start(bf16[64,256]{1,0:T(8,128)(2,1)} %refs_0_.1), channel_id=1, source_target_pairs={{0,1},{1,0},{2,3},{3,2},{4,5},{5,4},{6,7},{7,6},{8,9},{9,8},{10,11... | collective-permute-start | bytes 98312 | tf_op jit(solution)/shard_map/ppermute | solution.py:125
  3.7 0.9 %slice.3.w1_ref = bf16[256,256]{1,0:T(8,128)(2,1)S(1)} slice(bf16[768,256]{1,0:T(8,128)(2,1)} %w1_ref.3), slice={[0:256], [0:256]} | slice | bytes 262144 | tf_op jit(solution)/shard_map/slice | solution.py:354
  4.6 1.2 %collective-permute-done.refs_1_ = bf16[64,256]{1,0:T(8,128)(2,1)S(1)} collective-permute-done((bf16[64,256]{1,0:T(8,128)(2,1)}, bf16[64,256]{1,0:T(8,128)(2,1)S(1)}, u32[]{:S(2)}, u32[]{:S(2)}) %collective-permute-start) | collective-permute-done | bytes 32800 | tf_op jit(solution)/shard_map/ppermute | solution.py:125
  5.8 0.0 copy-start.16
  5.8 0.2 shard_map.240
  6.0 3.4 %collective-permute-start.2 = (bf16[32,256]{1,0:T(8,128)(2,1)S(1)}, bf16[32,256]{1,0:T(8,128)(2,1)S(1)}, u32[]{:S(2)}, u32[]{:S(2)}) collective-permute-start(bf16[32,256]{1,0:T(8,128)(2,1)S(1)} %get-tuple-element.95), channel_id=1, source_target_pairs={{0,30},{1,31},{2,0},{3,1},{4,2},{5,3},{6,4},{7,5},{8,6},{9,7},{10,... | collective-permute-start | bytes 49160 | tf_op jit(solution)/shard_map/ppermute | solution.py:125
  9.4 0.0 collective-permute-start.1
  9.4 0.0 copy-start.15
  9.4 0.0 copy-done.10
  9.4 0.0 copy-done.14
  9.5 0.6 %copy-done.12 = f32[256]{0:T(256)S(1)} copy-done((f32[256]{0:T(256)S(1)}, f32[256]{0:T(256)}, u32[]{:S(2)}) %copy-start.12) | copy-done | bytes 1048
  10.1 0.0 copy-done.13
  10.1 0.0 copy-done.11
  10.1 1.0 %copy-done = bf16[768,256]{1,0:T(8,128)(2,1)S(1)} copy-done((bf16[768,256]{1,0:T(8,128)(2,1)S(1)}, bf16[768,256]{1,0:T(8,128)(2,1)}, u32[]{:S(2)}) %copy-start) | copy-done | bytes 393240
  11.1 1.0 %copy-done.8 = bf16[1024,256]{1,0:T(8,128)(2,1)S(1)} copy-done((bf16[1024,256]{1,0:T(8,128)(2,1)S(1)}, bf16[1024,256]{1,0:T(8,128)(2,1)}, u32[]{:S(2)}) %copy-start.8) | copy-done | bytes 524312
  12.1 1.1 %shard_map.241 = (f32[1024,256]{1,0:T(8,128)S(1)}, bf16[320,1024]{1,0:T(8,128)(2,1)S(1)}, bf16[1024,128]{1,0:T(8,128)(2,1)S(1)}, bf16[1024,128]{1,0:T(8,128)(2,1...) custom-call(s32[8,128]{1,0:T(8,128)S(1)} %bitcast.2, ...), custom_call_target="tpu_custom_call" | custom-call | flops 536870912 | bytes 3768640 | tf_op jit(solution)/shard_map/pallas_call | solution.py:83
  13.3 0.0 collective-permute-done.2.next_ref
  13.3 2.0 %collective-permute-done.1.prev_ref = bf16[32,256]{1,0:T(8,128)(2,1)S(1)} collective-permute-done((bf16[32,256]{1,0:T(8,128)(2,1)S(1)}, bf16[32,256]{1,0:T(8,128)(2,1)S(1)}, u32[]{:S(2)}, u32[]{:S(2)}) %collective-permute-start.1) | collective-permute-done | bytes 16416 | tf_op jit(solution)/shard_map/ppermute | solution.py:125
  15.3 0.0 copy-start.5
  15.3 1.7 %shard_map.242 = (bf16[1024,256]{1,0:T(8,128)(2,1)S(1)}, f32[1024,256]{1,0:T(8,128)S(1)}, f32[1024,256]{1,0:T(8,128)S(1)}, f32[1024,1]{1,0:T(8,128)S(1)}, f32[12...) custom-call(f32[8,256]{1,0:T(8,128)S(1)} %get-tuple-element.92.live_ref, f32[1024,256]{1,0:T(8,128)S(1)} %get-tuple-element.97.pre_ref, ...), custom_call_target="tpu_custom_call" | custom-call | flops 402653184 | bytes 5169152 | tf_op jit(solution)/shard_map/pallas_call | solution.py:83
  17.0 1.6 %collective-permute-start.3 = (bf16[192,256]{1,0:T(8,128)(2,1)S(1)}, bf16[192,256]{1,0:T(8,128)(2,1)S(1)}, u32[]{:S(2)}, u32[]{:S(2)}) collective-permute-start(bf16[192,256]{1,0:T(8,128)(2,1)S(1)} %get-tuple-element.106.refs_0_), channel_id=1, source_target_pairs={{0,1},{1,0},{2,3},{3,2},{4,5},{5,4},{6,7},{7,6},{8,9},{9,8},{10,11... | collective-permute-start | bytes 294920 | tf_op jit(solution)/shard_map/ppermute | solution.py:125
  18.6 3.1 %collective-permute-done.3.refs_1_ = bf16[192,256]{1,0:T(8,128)(2,1)S(1)} collective-permute-done((bf16[192,256]{1,0:T(8,128)(2,1)S(1)}, bf16[192,256]{1,0:T(8,128)(2,1)S(1)}, u32[]{:S(2)}, u32[]{:S(2)}) %collective-permute-start.3) | collective-permute-done | bytes 98336 | tf_op jit(solution)/shard_map/ppermute | solution.py:125
  21.7 3.7 %shard_map.243 = (bf16[1024,256]{1,0:T(8,128)(2,1)}, f32[928,256]{1,0:T(8,128)S(1)}, bf16[928,256]{1,0:T(8,128)(2,1)S(1)}, bf16[192,256]{1,0:T(8,128)(2,1)S(1)}, f32[128,256]{1,0:T(8,128)S(1)}) custom-call(f32[8,256]{1,0:T(8,128)S(1)} %get-tuple-element.92.live_ref, bf16[320,1024]{1,0:T(8,128)(2,1)S(1)} %get-tuple-element.93.place_ref, ...), custom_call_target="tpu_custom_call" | custom-call | flops 1073741824 | bytes 8126464 | tf_op jit(solution)/shard_map/pallas_call | solution.py:83
  25.4 0.1 collective-permute-start.4
  25.4 1.8 %collective-permute-done.4.got_ref = bf16[928,256]{1,0:T(8,128)(2,1)S(1)} collective-permute-done((bf16[928,256]{1,0:T(8,128)(2,1)S(1)}, bf16[928,256]{1,0:T(8,128)(2,1)S(1)}, u32[]{:S(2)}, u32[]{:S(2)}) %collective-permute-start.4) | collective-permute-done | bytes 475168 | tf_op jit(solution)/shard_map/ppermute | solution.py:125
  27.3 0.2 shard_map.244
  27.4 1.6 %collective-permute-start.5 = (bf16[232,256]{1,0:T(8,128)(2,1)S(1)}, bf16[232,256]{1,0:T(8,128)(2,1)S(1)}, u32[]{:S(2)}, u32[]{:S(2)}) collective-permute-start(bf16[232,256]{1,0:T(8,128)(2,1)S(1)} %get-tuple-element.110), channel_id=1, source_target_pairs={{0,1},{1,0},{2,10},{3,11},{4,5},{5,4},{6,14},{7,15},{8,9},{9,8},{1... | collective-permute-start | bytes 356360 | tf_op jit(solution)/shard_map/ppermute | solution.py:125
  29.0 0.0 collective-permute-start.6
  29.0 2.0 %collective-permute-start.7 = (bf16[232,256]{1,0:T(8,128)(2,1)S(1)}, bf16[232,256]{1,0:T(8,128)(2,1)S(1)}, u32[]{:S(2)}, u32[]{:S(2)}) collective-permute-start(bf16[232,256]{1,0:T(8,128)(2,1)S(1)} %get-tuple-element.112), channel_id=1, source_target_pairs={{0,5},{1,4},{2,26},{3,27},{4,1},{5,0},{6,30},{7,31},{8,13},{9,12},... | collective-permute-start | bytes 356360 | tf_op jit(solution)/shard_map/ppermute | solution.py:125
  31.0 1.3 %collective-permute-done.5.refs_0_ = bf16[232,256]{1,0:T(8,128)(2,1)S(1)} collective-permute-done((bf16[232,256]{1,0:T(8,128)(2,1)S(1)}, bf16[232,256]{1,0:T(8,128)(2,1)S(1)}, u32[]{:S(2)}, u32[]{:S(2)}) %collective-permute-start.5) | collective-permute-done | bytes 118816 | tf_op jit(solution)/shard_map/ppermute | solution.py:125
  32.3 2.8 %collective-permute-done.6.refs_1_ = bf16[232,256]{1,0:T(8,128)(2,1)S(1)} collective-permute-done((bf16[232,256]{1,0:T(8,128)(2,1)S(1)}, bf16[232,256]{1,0:T(8,128)(2,1)S(1)}, u32[]{:S(2)}, u32[]{:S(2)}) %collective-permute-start.6) | collective-permute-done | bytes 118816 | tf_op jit(solution)/shard_map/ppermute | solution.py:125
  35.1 0.0 collective-permute-done.7.refs_2_
  35.1 0.1 shard_map.245.refs_0_
  35.2 1.7 %collective-permute-start.10 = (bf16[232,256]{1,0:T(8,128)(2,1)S(1)}, bf16[232,256]{1,0:T(8,128)(2,1)S(1)}, u32[]{:S(2)}, u32[]{:S(2)}) collective-permute-start(bf16[232,256]{1,0:T(8,128)(2,1)S(1)} %shard_map.245.refs_0_), channel_id=1, source_target_pairs={{0,24},{1,25},{2,7},{3,6},{4,28},{5,29},{6,3},{7,2},{8,16},{9,17},... | collective-permute-start | bytes 356360 | tf_op jit(solution)/shard_map/ppermute | solution.py:125
  36.8 0.0 collective-permute-start.9
  36.8 2.8 %collective-permute-start.8 = (bf16[232,256]{1,0:T(8,128)(2,1)S(1)}, bf16[232,256]{1,0:T(8,128)(2,1)S(1)}, u32[]{:S(2)}, u32[]{:S(2)}) collective-permute-start(bf16[232,256]{1,0:T(8,128)(2,1)S(1)} %shard_map.245.refs_0_), channel_id=1, source_target_pairs={{0,8},{1,9},{2,3},{3,2},{4,12},{5,13},{6,7},{7,6},{8,0},{9,1},{10,... | collective-permute-start | bytes 356360 | tf_op jit(solution)/shard_map/ppermute | solution.py:125
  39.6 0.5 collective-permute-start.11
  40.2 4.1 %collective-permute-done.11.refs_1_ = bf16[192,256]{1,0:T(8,128)(2,1)S(1)} collective-permute-done((bf16[192,256]{1,0:T(8,128)(2,1)S(1)}, bf16[192,256]{1,0:T(8,128)(2,1)S(1)}, u32[]{:S(2)}, u32[]{:S(2)}) %collective-permute-start.11) | collective-permute-done | bytes 98336 | tf_op jit(solution)/shard_map/ppermute | solution.py:125
  44.3 0.1 collective-permute-start.12
  44.3 0.5 collective-permute-start.13
  44.8 0.9 %collective-permute-done.12.refs_5_ = bf16[32,256]{1,0:T(8,128)(2,1)S(1)} collective-permute-done((bf16[32,256]{1,0:T(8,128)(2,1)S(1)}, bf16[32,256]{1,0:T(8,128)(2,1)S(1)}, u32[]{:S(2)}, u32[]{:S(2)}) %collective-permute-start.12) | collective-permute-done | bytes 16416 | tf_op jit(solution)/shard_map/ppermute | solution.py:125
  45.8 4.5 %collective-permute-done.13.refs_6_ = bf16[32,256]{1,0:T(8,128)(2,1)S(1)} collective-permute-done((bf16[32,256]{1,0:T(8,128)(2,1)S(1)}, bf16[32,256]{1,0:T(8,128)(2,1)S(1)}, u32[]{:S(2)}, u32[]{:S(2)}) %collective-permute-start.13) | collective-permute-done | bytes 16416 | tf_op jit(solution)/shard_map/ppermute | solution.py:125
  50.2 0.0 collective-permute-done.10.refs_3_
  50.2 0.0 collective-permute-done.9.refs_2_
  50.2 0.0 collective-permute-done.8.refs_1_
  50.3 0.2 shard_map.247
  50.5 0.1 collective-permute-start.14
  50.6 0.1 collective-permute-start.16
  50.6 3.4 %collective-permute-start.15 = (bf16[232,256]{1,0:T(8,128)(2,1)S(1)}, bf16[232,256]{1,0:T(8,128)(2,1)S(1)}, u32[]{:S(2)}, u32[]{:S(2)}) collective-permute-start(bf16[232,256]{1,0:T(8,128)(2,1)S(1)} %get-tuple-element.116.refs_0_), channel_id=1, source_target_pairs={{0,4},{1,5},{2,18},{3,19},{4,0},{5,1},{6,22},{7,23},{8,12},{9,13},... | collective-permute-start | bytes 356360 | tf_op jit(solution)/shard_map/ppermute | solution.py:125
  54.0 0.1 collective-permute-start.18
  54.1 0.0 collective-permute-done.14.refs_1_
  54.1 1.5 %shard_map.248 = (f32[64,256]{1,0:T(8,128)}, f32[768,256]{1,0:T(8,128)}, f32[256]{0:T(256)}, f32[256,256]{1,0:T(8,128)}, f32[256]{0:T(256)}, /*index=5*/f32[512,...) custom-call(bf16[232,256]{1,0:T(8,128)(2,1)S(1)} %get-tuple-element.116.refs_0_, ...), custom_call_target="tpu_custom_call" | custom-call | bytes 712704 | tf_op jit(solution)/shard_map/pallas_call | solution.py:590
  55.6 0.8 %collective-permute-done.16.refs_0_ = bf16[232,256]{1,0:T(8,128)(2,1)S(1)} collective-permute-done((bf16[232,256]{1,0:T(8,128)(2,1)S(1)}, bf16[232,256]{1,0:T(8,128)(2,1)S(1)}, u32[]{:S(2)}, u32[]{:S(2)}) %collective-permute-start.16) | collective-permute-done | bytes 118816 | tf_op jit(solution)/shard_map/ppermute | solution.py:125
  56.5 0.3 collective-permute-start.20
  56.7 0.8 %shard_map.249 = (f32[768,256]{1,0:T(8,128)}, f32[256]{0:T(256)}, f32[256,256]{1,0:T(8,128)}, f32[256]{0:T(256)}, f32[512,256]{1,0:T(8,128)}, /*index=5*/f32[256]{0:T(256)}, f32[256,256]{1,0:T(8,128)}, f32[256]{0:T(256)}) custom-call(bf16[232,256]{1,0:T(8,128)(2,1)S(1)} %collective-permute, ...), custom_call_target="tpu_custom_call", output_to_operand_aliasing={{0}: (1, {}), {1}: (2, {}), {2}: (3, {}), {3}: (4, {}), {4}... | custom-call | bytes 356352 | tf_op jit(solution)/shard_map/pallas_call | solution.py:590
  57.5 0.1 collective-permute-done.15.refs_0_
  57.6 1.2 %collective-permute-done.18.refs_1_ = bf16[232,256]{1,0:T(8,128)(2,1)S(1)} collective-permute-done((bf16[232,256]{1,0:T(8,128)(2,1)S(1)}, bf16[232,256]{1,0:T(8,128)(2,1)S(1)}, u32[]{:S(2)}, u32[]{:S(2)}) %collective-permute-start.18) | collective-permute-done | bytes 118816 | tf_op jit(solution)/shard_map/ppermute | solution.py:125
  58.8 0.0 collective-permute-start.19
  58.8 0.5 collective-permute-start.17
  59.3 0.0 collective-permute-done.20.refs_2_
  59.3 1.0 %shard_map.250 = (f32[768,256]{1,0:T(8,128)}, f32[256]{0:T(256)}, f32[256,256]{1,0:T(8,128)}, f32[256]{0:T(256)}, f32[512,256]{1,0:T(8,128)}, /*index=5*/f32[256]{0:T(256)}, f32[256,256]{1,0:T(8,128)}, f32[256]{0:T(256)}) custom-call(bf16[232,256]{1,0:T(8,128)(2,1)S(1)} %collective-permute, ...), custom_call_target="tpu_custom_call", output_to_operand_aliasing={{0}: (3, {}), {1}: (4, {}), {2}: (5, {}), {3}: (6, {}), {4}... | custom-call | bytes 1069056 | tf_op jit(solution)/shard_map/pallas_call | solution.py:590
  60.3 0.0 collective-permute-done.19.refs_1_
  60.4 0.0 collective-permute-done.17.refs_0_
  60.4 0.9 %shard_map.251 = (f32[768,256]{1,0:T(8,128)}, f32[256]{0:T(256)}, f32[256,256]{1,0:T(8,128)}, f32[256]{0:T(256)}, f32[512,256]{1,0:T(8,128)}, /*index=5*/f32[256]{0:T(256)}, f32[256,256]{1,0:T(8,128)}, f32[256]{0:T(256)}) custom-call(bf16[232,256]{1,0:T(8,128)(2,1)S(1)} %collective-permute, ...), custom_call_target="tpu_custom_call", output_to_operand_aliasing={{0}: (2, {}), {1}: (3, {}), {2}: (4, {}), {3}: (5, {}), {4}... | custom-call | bytes 712704 | tf_op jit(solution)/shard_map/pallas_call | solution.py:590
  (25 shorter events, 0.1 us)
Async XLA Ops:
  0.6 5.2 %copy-start.6 = (bf16[64,256]{1,0:T(8,128)(2,1)S(1)}, bf16[64,256]{1,0:T(8,128)(2,1)}, u32[]{:S(2)}) copy-start(bf16[64,256]{1,0:T(8,128)(2,1)} %refs_0_.1) | copy-start | bytes 98308
  0.7 5.2 %copy-start.7 = (s32[1,32]{1,0:T(1,128)S(1)}, s32[1,32]{1,0:T(1,128)}, u32[]{:S(2)}) copy-start(s32[1,32]{1,0:T(1,128)} %refs_4_.1) | copy-start | bytes 388
  0.7 5.1 %collective-permute-start = (bf16[64,256]{1,0:T(8,128)(2,1)}, bf16[64,256]{1,0:T(8,128)(2,1)S(1)}, u32[]{:S(2)}, u32[]{:S(2)}) collective-permute-start(bf16[64,256]{1,0:T(8,128)(2,1)} %refs_0_.1), channel_id=1, source_target_pairs={{0,1},{1,0},{2,3},{3,2},{4,5},{5,4},{6,7},{7,6},{8,9},{9,8},{10,11... | collective-permute-start | bytes 98312 | tf_op jit(solution)/shard_map/ppermute | solution.py:125
  5.8 3.6 %copy-start.10 = (s32[1024]{0:T(1024)S(1)}, s32[1024]{0:T(1024)}, u32[]{:S(2)}) copy-start(s32[1024]{0:T(1024)} %param.22) | copy-start | bytes 12292
  5.8 3.6 %copy-start.14 = (f32[256]{0:T(256)S(1)}, f32[256]{0:T(256)}, u32[]{:S(2)}) copy-start(f32[256]{0:T(256)} %nb2_ref.1) | copy-start | bytes 3076
  5.8 3.6 %copy-start.16 = (s32[64]{0:T(128)S(1)}, s32[64]{0:T(128)}, u32[]{:S(2)}) copy-start(s32[64]{0:T(128)} %sea_ref.1) | copy-start | bytes 772
  6.0 3.4 %copy-start.9 = (s32[1024]{0:T(1024)S(1)}, s32[1024]{0:T(1024)}, u32[]{:S(2)}) copy-start(s32[1024]{0:T(1024)} %param.21) | copy-start | bytes 12292
  6.0 7.3 %collective-permute-start.2 = (bf16[32,256]{1,0:T(8,128)(2,1)S(1)}, bf16[32,256]{1,0:T(8,128)(2,1)S(1)}, u32[]{:S(2)}, u32[]{:S(2)}) collective-permute-start(bf16[32,256]{1,0:T(8,128)(2,1)S(1)} %get-tuple-element.95), channel_id=1, source_target_pairs={{0,30},{1,31},{2,0},{3,1},{4,2},{5,3},{6,4},{7,5},{8,6},{9,7},{10,... | collective-permute-start | bytes 49160 | tf_op jit(solution)/shard_map/ppermute | solution.py:125
  9.4 5.9 %collective-permute-start.1 = (bf16[32,256]{1,0:T(8,128)(2,1)S(1)}, bf16[32,256]{1,0:T(8,128)(2,1)S(1)}, u32[]{:S(2)}, u32[]{:S(2)}) collective-permute-start(bf16[32,256]{1,0:T(8,128)(2,1)S(1)} %get-tuple-element.95), channel_id=1, source_target_pairs={{0,2},{1,3},{2,4},{3,5},{4,6},{5,7},{6,8},{7,9},{8,10},{9,11},{10,... | collective-permute-start | bytes 49160 | tf_op jit(solution)/shard_map/ppermute | solution.py:125
  9.4 0.7 %copy-start.12 = (f32[256]{0:T(256)S(1)}, f32[256]{0:T(256)}, u32[]{:S(2)}) copy-start(f32[256]{0:T(256)} %b2_ref.1) | copy-start | bytes 3076
  9.4 0.7 %copy-start.13 = (f32[256]{0:T(256)S(1)}, f32[256]{0:T(256)}, u32[]{:S(2)}) copy-start(f32[256]{0:T(256)} %nb1_ref.1) | copy-start | bytes 3076
  9.4 0.7 %copy-start.11 = (f32[256]{0:T(256)S(1)}, f32[256]{0:T(256)}, u32[]{:S(2)}) copy-start(f32[256]{0:T(256)} %b1_ref.1) | copy-start | bytes 3076
  9.4 0.7 %copy-start.15 = (s32[16]{0:T(128)S(1)}, s32[16]{0:T(128)}, u32[]{:S(2)}) copy-start(s32[16]{0:T(128)} %be_ref.1) | copy-start | bytes 196
  10.1 1.0 %copy-start = (bf16[768,256]{1,0:T(8,128)(2,1)S(1)}, bf16[768,256]{1,0:T(8,128)(2,1)}, u32[]{:S(2)}) copy-start(bf16[768,256]{1,0:T(8,128)(2,1)} %w1_ref.3) | copy-start | bytes 1179652
  11.1 1.0 %copy-start.8 = (bf16[1024,256]{1,0:T(8,128)(2,1)S(1)}, bf16[1024,256]{1,0:T(8,128)(2,1)}, u32[]{:S(2)}) copy-start(bf16[1024,256]{1,0:T(8,128)(2,1)} %e_ref.1) | copy-start | bytes 1572868
  12.1 3.1 %copy-start.1 = (bf16[256,256]{1,0:T(8,128)(2,1)S(1)}, bf16[256,256]{1,0:T(8,128)(2,1)}, u32[]{:S(2)}) copy-start(bf16[256,256]{1,0:T(8,128)(2,1)} %w2_ref.3) | copy-start | bytes 393220
  12.1 3.1 %copy-start.4 = (bf16[64,256]{1,0:T(8,128)(2,1)S(1)}, bf16[64,256]{1,0:T(8,128)(2,1)}, u32[]{:S(2)}) copy-start(bf16[64,256]{1,0:T(8,128)(2,1)} %refs_5_.1) | copy-start | bytes 98308
  15.3 6.4 %copy-start.2 = (bf16[1024,256]{1,0:T(8,128)(2,1)S(1)}, bf16[1024,256]{1,0:T(8,128)(2,1)}, u32[]{:S(2)}) copy-start(bf16[1024,256]{1,0:T(8,128)(2,1)} %geo_ref.1) | copy-start | bytes 1572868
  15.3 6.4 %copy-start.3 = (bf16[512,256]{1,0:T(8,128)(2,1)S(1)}, bf16[512,256]{1,0:T(8,128)(2,1)}, u32[]{:S(2)}) copy-start(bf16[512,256]{1,0:T(8,128)(2,1)} %nw1_ref.1) | copy-start | bytes 786436
  15.3 6.4 %copy-start.5 = (bf16[256,256]{1,0:T(8,128)(2,1)S(1)}, bf16[256,256]{1,0:T(8,128)(2,1)}, u32[]{:S(2)}) copy-start(bf16[256,256]{1,0:T(8,128)(2,1)} %nw2_ref.1) | copy-start | bytes 393220
  17.0 4.7 %collective-permute-start.3 = (bf16[192,256]{1,0:T(8,128)(2,1)S(1)}, bf16[192,256]{1,0:T(8,128)(2,1)S(1)}, u32[]{:S(2)}, u32[]{:S(2)}) collective-permute-start(bf16[192,256]{1,0:T(8,128)(2,1)S(1)} %get-tuple-element.106.refs_0_), channel_id=1, source_target_pairs={{0,1},{1,0},{2,3},{3,2},{4,5},{5,4},{6,7},{7,6},{8,9},{9,8},{10,11... | collective-permute-start | bytes 294920 | tf_op jit(solution)/shard_map/ppermute | solution.py:125
  25.4 1.9 %collective-permute-start.4 = (bf16[928,256]{1,0:T(8,128)(2,1)S(1)}, bf16[928,256]{1,0:T(8,128)(2,1)S(1)}, u32[]{:S(2)}, u32[]{:S(2)}) collective-permute-start(bf16[928,256]{1,0:T(8,128)(2,1)S(1)} %get-tuple-element.108), channel_id=1, source_target_pairs={{0,2},{1,3},{2,0},{3,1},{4,6},{5,7},{6,4},{7,5},{8,10},{9,11},{10,... | collective-permute-start | bytes 1425416 | tf_op jit(solution)/shard_map/ppermute | solution.py:125
  27.4 4.9 %collective-permute-start.5 = (bf16[232,256]{1,0:T(8,128)(2,1)S(1)}, bf16[232,256]{1,0:T(8,128)(2,1)S(1)}, u32[]{:S(2)}, u32[]{:S(2)}) collective-permute-start(bf16[232,256]{1,0:T(8,128)(2,1)S(1)} %get-tuple-element.110), channel_id=1, source_target_pairs={{0,1},{1,0},{2,10},{3,11},{4,5},{5,4},{6,14},{7,15},{8,9},{9,8},{1... | collective-permute-start | bytes 356360 | tf_op jit(solution)/shard_map/ppermute | solution.py:125
  29.0 6.1 %collective-permute-start.6 = (bf16[232,256]{1,0:T(8,128)(2,1)S(1)}, bf16[232,256]{1,0:T(8,128)(2,1)S(1)}, u32[]{:S(2)}, u32[]{:S(2)}) collective-permute-start(bf16[232,256]{1,0:T(8,128)(2,1)S(1)} %get-tuple-element.111), channel_id=1, source_target_pairs={{0,4},{1,5},{2,18},{3,19},{4,0},{5,1},{6,22},{7,23},{8,12},{9,13},... | collective-permute-start | bytes 356360 | tf_op jit(solution)/shard_map/ppermute | solution.py:125
  29.0 6.1 %collective-permute-start.7 = (bf16[232,256]{1,0:T(8,128)(2,1)S(1)}, bf16[232,256]{1,0:T(8,128)(2,1)S(1)}, u32[]{:S(2)}, u32[]{:S(2)}) collective-permute-start(bf16[232,256]{1,0:T(8,128)(2,1)S(1)} %get-tuple-element.112), channel_id=1, source_target_pairs={{0,5},{1,4},{2,26},{3,27},{4,1},{5,0},{6,30},{7,31},{8,13},{9,12},... | collective-permute-start | bytes 356360 | tf_op jit(solution)/shard_map/ppermute | solution.py:125
  35.2 15.1 %collective-permute-start.10 = (bf16[232,256]{1,0:T(8,128)(2,1)S(1)}, bf16[232,256]{1,0:T(8,128)(2,1)S(1)}, u32[]{:S(2)}, u32[]{:S(2)}) collective-permute-start(bf16[232,256]{1,0:T(8,128)(2,1)S(1)} %shard_map.245.refs_0_), channel_id=1, source_target_pairs={{0,24},{1,25},{2,7},{3,6},{4,28},{5,29},{6,3},{7,2},{8,16},{9,17},... | collective-permute-start | bytes 356360 | tf_op jit(solution)/shard_map/ppermute | solution.py:125
  36.8 13.4 %collective-permute-start.9 = (bf16[232,256]{1,0:T(8,128)(2,1)S(1)}, bf16[232,256]{1,0:T(8,128)(2,1)S(1)}, u32[]{:S(2)}, u32[]{:S(2)}) collective-permute-start(bf16[232,256]{1,0:T(8,128)(2,1)S(1)} %shard_map.245.refs_0_), channel_id=1, source_target_pairs={{0,16},{1,17},{2,6},{3,7},{4,20},{5,21},{6,2},{7,3},{8,24},{9,25},... | collective-permute-start | bytes 356360 | tf_op jit(solution)/shard_map/ppermute | solution.py:125
  36.8 13.4 %collective-permute-start.8 = (bf16[232,256]{1,0:T(8,128)(2,1)S(1)}, bf16[232,256]{1,0:T(8,128)(2,1)S(1)}, u32[]{:S(2)}, u32[]{:S(2)}) collective-permute-start(bf16[232,256]{1,0:T(8,128)(2,1)S(1)} %shard_map.245.refs_0_), channel_id=1, source_target_pairs={{0,8},{1,9},{2,3},{3,2},{4,12},{5,13},{6,7},{7,6},{8,0},{9,1},{10,... | collective-permute-start | bytes 356360 | tf_op jit(solution)/shard_map/ppermute | solution.py:125
  39.6 4.6 %collective-permute-start.11 = (bf16[192,256]{1,0:T(8,128)(2,1)S(1)}, bf16[192,256]{1,0:T(8,128)(2,1)S(1)}, u32[]{:S(2)}, u32[]{:S(2)}) collective-permute-start(bf16[192,256]{1,0:T(8,128)(2,1)S(1)} %get-tuple-element.113.refs_0_), channel_id=1, source_target_pairs={{0,1},{1,0},{2,3},{3,2},{4,5},{5,4},{6,7},{7,6},{8,9},{9,8},{10,11... | collective-permute-start | bytes 294920 | tf_op jit(solution)/shard_map/ppermute | solution.py:125
  44.3 1.5 %collective-permute-start.12 = (bf16[32,256]{1,0:T(8,128)(2,1)S(1)}, bf16[32,256]{1,0:T(8,128)(2,1)S(1)}, u32[]{:S(2)}, u32[]{:S(2)}) collective-permute-start(bf16[32,256]{1,0:T(8,128)(2,1)S(1)} %get-tuple-element.114), channel_id=1, source_target_pairs={{0,30},{1,31},{2,0},{3,1},{4,2},{5,3},{6,4},{7,5},{8,6},{9,7},{10,... | collective-permute-start | bytes 49160 | tf_op jit(solution)/shard_map/ppermute | solution.py:125
  44.3 5.9 %collective-permute-start.13 = (bf16[32,256]{1,0:T(8,128)(2,1)S(1)}, bf16[32,256]{1,0:T(8,128)(2,1)S(1)}, u32[]{:S(2)}, u32[]{:S(2)}) collective-permute-start(bf16[32,256]{1,0:T(8,128)(2,1)S(1)} %get-tuple-element.115), channel_id=1, source_target_pairs={{0,2},{1,3},{2,4},{3,5},{4,6},{5,7},{6,8},{7,9},{8,10},{9,11},{10,... | collective-permute-start | bytes 49160 | tf_op jit(solution)/shard_map/ppermute | solution.py:125
  50.5 3.6 %collective-permute-start.14 = (bf16[232,256]{1,0:T(8,128)(2,1)S(1)}, bf16[232,256]{1,0:T(8,128)(2,1)S(1)}, u32[]{:S(2)}, u32[]{:S(2)}) collective-permute-start(bf16[232,256]{1,0:T(8,128)(2,1)S(1)} %get-tuple-element.116.refs_0_), channel_id=1, source_target_pairs={{0,2},{1,3},{2,0},{3,1},{4,6},{5,7},{6,4},{7,5},{8,10},{9,11},{10,... | collective-permute-start | bytes 356360 | tf_op jit(solution)/shard_map/ppermute | solution.py:125
  50.6 5.9 %collective-permute-start.16 = (bf16[232,256]{1,0:T(8,128)(2,1)S(1)}, bf16[232,256]{1,0:T(8,128)(2,1)S(1)}, u32[]{:S(2)}, u32[]{:S(2)}) collective-permute-start(bf16[232,256]{1,0:T(8,128)(2,1)S(1)} %get-tuple-element.116.refs_0_), channel_id=1, source_target_pairs={{0,5},{1,4},{2,26},{3,27},{4,1},{5,0},{6,30},{7,31},{8,13},{9,12},... | collective-permute-start | bytes 356360 | tf_op jit(solution)/shard_map/ppermute | solution.py:125
  50.6 7.0 %collective-permute-start.15 = (bf16[232,256]{1,0:T(8,128)(2,1)S(1)}, bf16[232,256]{1,0:T(8,128)(2,1)S(1)}, u32[]{:S(2)}, u32[]{:S(2)}) collective-permute-start(bf16[232,256]{1,0:T(8,128)(2,1)S(1)} %get-tuple-element.116.refs_0_), channel_id=1, source_target_pairs={{0,4},{1,5},{2,18},{3,19},{4,0},{5,1},{6,22},{7,23},{8,12},{9,13},... | collective-permute-start | bytes 356360 | tf_op jit(solution)/shard_map/ppermute | solution.py:125
  54.0 4.8 %collective-permute-start.18 = (bf16[232,256]{1,0:T(8,128)(2,1)S(1)}, bf16[232,256]{1,0:T(8,128)(2,1)S(1)}, u32[]{:S(2)}, u32[]{:S(2)}) collective-permute-start(bf16[232,256]{1,0:T(8,128)(2,1)S(1)} %get-tuple-element.116.refs_0_), channel_id=1, source_target_pairs={{0,1},{1,0},{2,10},{3,11},{4,5},{5,4},{6,14},{7,15},{8,9},{9,8},{1... | collective-permute-start | bytes 356360 | tf_op jit(solution)/shard_map/ppermute | solution.py:125
  56.5 2.9 %collective-permute-start.20 = (bf16[232,256]{1,0:T(8,128)(2,1)S(1)}, bf16[232,256]{1,0:T(8,128)(2,1)S(1)}, u32[]{:S(2)}, u32[]{:S(2)}) collective-permute-start(bf16[232,256]{1,0:T(8,128)(2,1)S(1)} %collective-permute-done.16.refs_0_), channel_id=1, source_target_pairs={{0,2},{1,3},{2,0},{3,1},{4,6},{5,7},{6,4},{7,5},{8,10},{9,11},{10,... | collective-permute-start | bytes 356360 | tf_op jit(solution)/shard_map/ppermute | solution.py:125
  58.8 1.5 %collective-permute-start.19 = (bf16[232,256]{1,0:T(8,128)(2,1)S(1)}, bf16[232,256]{1,0:T(8,128)(2,1)S(1)}, u32[]{:S(2)}, u32[]{:S(2)}) collective-permute-start(bf16[232,256]{1,0:T(8,128)(2,1)S(1)} %collective-permute-done.18.refs_1_), channel_id=1, source_target_pairs={{0,2},{1,3},{2,0},{3,1},{4,6},{5,7},{6,4},{7,5},{8,10},{9,11},{10,... | collective-permute-start | bytes 356360 | tf_op jit(solution)/shard_map/ppermute | solution.py:125
  58.8 1.5 %collective-permute-start.17 = (bf16[232,256]{1,0:T(8,128)(2,1)S(1)}, bf16[232,256]{1,0:T(8,128)(2,1)S(1)}, u32[]{:S(2)}, u32[]{:S(2)}) collective-permute-start(bf16[232,256]{1,0:T(8,128)(2,1)S(1)} %collective-permute-done.15.refs_0_), channel_id=1, source_target_pairs={{0,2},{1,3},{2,0},{3,1},{4,6},{5,7},{6,4},{7,5},{8,10},{9,11},{10,... | collective-permute-start | bytes 356360 | tf_op jit(solution)/shard_map/ppermute | solution.py:125
where the time goes:
time: 61.5 us; the launch traced here: 61.3 us
  waiting for transfers between devices  23.8 us (39%)
  starting transfers between devices  21.6 us (35%)
  Pallas kernels  11.3 us (18%)
  local copies, waits for them, and re-layouts  3.65 us (6%)
  between operations  0.88 us (1%)
    ppermute x21, waiting for transfers between devices, permute(): return lax.ppermute(array, AXES, pairs)  23.8 us
    ppermute x21, starting transfers between devices, permute(): return lax.ppermute(array, AXES, pairs)  21.6 us
    pallas_call x8, Pallas kernels, call(): pl.pallas_call(kernel, out_shape=out_shape, in_specs=in_specs, out_specs=...  7.15 us
    pallas_call x4, Pallas kernels, place_call(): pl.pallas_call(kernel, out_shape=node_out + out_shape, in_specs=[vmem] *...  4.16 us
    unnamed x34, local copies, waits for them, and re-layouts  2.74 us
  transfers between devices with their start and end apart: 21, of which 12 were waited for; matrix products, arithmetic and copies ran while one was open for 1% of the time, Pallas kernels for 7%

commit v1 on v0

--- a/solution.py
+++ b/solution.py
@@ -150,8 +150,10 @@
 
         return self.permute(array, move)
 
-    def ring(self, array, by):
-        return self.permute(array, lambda b, h: ((b + by) % self.bands, h))
+    def ring_swap(self, array):
+        return self.permute(
+            array, lambda b, h: ((b + (1 if b % 2 else -1)) % self.bands, h)
+        )
 
     def core_id(self):
         return lax.rem(lax.axis_index("band"), self.core)
@@ -259,8 +261,8 @@
     band_rows, outgoing = call(
         gather_kernel, [sds(band, feat, BF), sds(halo, feat, BF)], [halo_list, node_latent, *theirs]
     )
-    from_prev = groups.ring(outgoing, 1)
-    from_next = groups.ring(outgoing, -1)
+    from_ring = groups.ring_swap(outgoing)
+    from_core = groups.core_swap(outgoing)
 
     def split_store(table, height, at, proj):
         high = proj.astype(BF)
@@ -320,13 +322,16 @@
     )
 
     def forward_kernel(
-        live_ref, pre_ref, place_ref, halo_pick_ref, prev_ref, next_ref, w1_ref, w2_ref, bias_ref,
-        gon_ref, sea_ref, hid_ref, slope_ref, norm_ref, inv_ref, agg, swap_ref, table,
+        live_ref, pre_ref, place_ref, halo_pick_ref, ring_ref, core_ref, w1_ref, w2_ref, bias_ref,
+        gon_ref, sea_ref, hid_ref, slope_ref, norm_ref, inv_ref, agg, swap_ref, halo_ref,
+        table,
     ):
         if h_width > 2 * halo:
             table[...] = jnp.zeros_like(table)
-        halo_rows = jnp.concatenate([prev_ref[...], next_ref[...]], axis=0)
-        split_store(table, h_width, 0, dot(halo_rows, w1_ref[...]))
+        odd = lax.rem(lax.axis_index("band"), 2)
+        halo_ref[pl.ds(pl.multiple_of(odd * halo, halo), halo), :] = ring_ref[...]
+        halo_ref[pl.ds(pl.multiple_of((1 - odd) * halo, halo), halo), :] = core_ref[...]
+        split_store(table, h_width, 0, dot(halo_ref[...], w1_ref[...]))
         for i in range(edges // chunk):
             rows = pl.ds(i * chunk, chunk)
             pick = halo_pick_ref[rows, :]
@@ -347,11 +352,11 @@
         swap_ref[:band, :] = agg[...].astype(BF)
         swap_ref[band:, :] = dot(sea_ref[...], gon_ref[...]).astype(BF)
 
-    hidden, slope, normed, inv, agg_own, swap_own = call(
+    hidden, slope, normed, inv, agg_own, swap_own, halo_rows = call(
         forward_kernel,
         [sds(edges, feat, BF), sds(edges, feat, F32), sds(edges, feat, F32), sds(edges, 1, F32),
-         sds(band, feat, F32), sds(band + own, feat, BF)],
-        [live, pre_local, place, halo_pick, from_prev, from_next, edge_w1[:feat], edge_w2,
+         sds(band, feat, F32), sds(band + own, feat, BF), sds(2 * halo, feat, BF)],
+        [live, pre_local, place, halo_pick, from_ring, from_core, edge_w1[:feat], edge_w2,
          biases, grad_out_node, sea_diag],
         scratch=[pltpu.VMEM((2 * h_width, feat), BF)],
         flops=3 * unit,
@@ -360,7 +365,7 @@
     swaps = [swap_own] + [groups.helper_swap(swap_own, k) for k in range(1, helpers)]
 
     def backward_kernel(
-        live_ref, place_ref, recv_pick_ref, band_ref, prev_ref, next_ref, et_ref, geo_ref,
+        live_ref, place_ref, recv_pick_ref, band_ref, halo_ref, et_ref, geo_ref,
         hid_ref, slope_ref, norm_ref, inv_ref, w1_ref, w2_ref, nw1_ref, nw2_ref, bias_ref,
         agg_ref, *refs,
     ):
@@ -429,7 +434,7 @@
                 sums[...] += part
         at_send = sums[:look, :].astype(BF)
         at_recv = sums[look:, :].astype(BF)
-        lookup = jnp.concatenate([band_v, prev_ref[...], next_ref[...]], axis=0)
+        lookup = jnp.concatenate([band_v, halo_ref[...]], axis=0)
         look_grad = dot_right_t(at_send, w1_ref[:feat, :])
         recv_grad = dot_right_t(at_recv, w1_ref[feat : 2 * feat, :])
         lg_ref[:band, :] = (look_grad[:band, :] + recv_grad).astype(BF)
@@ -453,7 +458,7 @@
         backward_kernel,
         [sds(edges, feat, BF), sds(half, feat, F32), sds(half, feat, BF), sds(look, feat, BF),
          sds(band, feat, F32)],
-        [live, place, recv_pick, band_rows, from_prev, from_next, edge_t, grad_out_edge,
+        [live, place, recv_pick, band_rows, halo_rows, edge_t, grad_out_edge,
          hidden, slope, normed, inv, edge_w1, edge_w2, node_w1, node_w2, biases, agg_own, *swaps],
         scratch=[pltpu.VMEM((half * groups.core, feat), F32), pltpu.VMEM((look + band, feat), F32),
                  pltpu.VMEM((band, feat), BF), pltpu.VMEM((edges, feat), BF),
@@ -483,18 +488,22 @@
     from_group = [groups.first_swap(part, k) for k, part in enumerate(to_group, 1)]
 
     def look_kernel(*refs):
-        parts, (mine_ref, prev_ref, next_ref) = refs[:helpers], refs[helpers:]
+        parts, (mine_ref, ring_ref, core_ref, halos) = refs[:helpers], refs[helpers:]
         at = pl.multiple_of(lax.axis_index("helper") * own, own)
         mine_ref[...] = tree_sum([g[pl.ds(at, own), :].astype(F32) for g in parts])
-        halos = tree_sum([g[band:, :].astype(F32) for g in parts])
-        prev_ref[...] = halos[:halo, :].astype(BF)
-        next_ref[...] = halos[halo:, :].astype(BF)
-
-    own_grad, prev_grad, next_grad = call(
-        look_kernel, [sds(own, feat, F32), sds(halo, feat, BF), sds(halo, feat, BF)], looks
-    )
-    halo_back = groups.ring(prev_grad, -1)
-    halo_forth = groups.ring(next_grad, 1)
+        halos[...] = tree_sum([g[band:, :].astype(F32) for g in parts])
+        odd = lax.rem(lax.axis_index("band"), 2)
+        ring_ref[...] = halos[pl.ds(pl.multiple_of(odd * halo, halo), halo), :].astype(BF)
+        core_ref[...] = halos[pl.ds(pl.multiple_of((1 - odd) * halo, halo), halo), :].astype(BF)
+
+    own_grad, ring_grad, core_grad = call(
+        look_kernel,
+        [sds(own, feat, F32), sds(halo, feat, BF), sds(halo, feat, BF)],
+        looks,
+        scratch=[pltpu.VMEM((2 * halo, feat), F32)],
+    )
+    ring_back = groups.ring_swap(ring_grad)
+    core_back = groups.core_swap(core_grad)
 
     def join_kernel(own_ref, *refs):
         parts, piece_ref = refs[: group - 1], refs[group - 1]
@@ -523,7 +532,7 @@
             halo_sums, piece_sum = call(
                 far_kernel,
                 [sds(own, feat, F32), sds(piece, feat, BF)],
-                swapped + [halo_list, halo_back, halo_forth],
+                swapped + [halo_list, ring_back, core_back],
             )
         else:
             (piece_sum,) = call(far_kernel, [sds(piece, feat, BF)], swapped)

time: 61.5 us -> 60.5 us (0.984)
  waiting for transfers between devices: 23.8 us -> 19.6 us
  starting transfers between devices: 21.6 us -> 24.8 us
    ppermute x21, waiting for transfers between devices: 23.8 us -> 19.6 us  [permute(): return lax.ppermute(array, AXES, pairs)]
    ppermute x21, starting transfers between devices: 21.6 us -> 24.8 us  [permute(): return lax.ppermute(array, AXES, pairs)]
  transfers between devices with their start and end apart: 21 -> 21, of which waited for: 12 -> 9; matrix products, arithmetic and copies ran while one was open for 1% -> 2% of each run, Pallas kernels for 7% -> 7%
where the time goes in v1:
time: 60.5 us; the launch traced here: 60.3 us
  starting transfers between devices  24.8 us (41%)
  waiting for transfers between devices  19.6 us (32%)
  Pallas kernels  11.3 us (19%)
  local copies, waits for them, and re-layouts  3.67 us (6%)
  between operations  0.93 us (2%)
    ppermute x21, starting transfers between devices, permute(): return lax.ppermute(array, AXES, pairs)  24.8 us
    ppermute x21, waiting for transfers between devices, permute(): return lax.ppermute(array, AXES, pairs)  19.6 us
    pallas_call x8, Pallas kernels, call(): pl.pallas_call(kernel, out_shape=out_shape, in_specs=in_specs, out_specs=...  7.15 us
    pallas_call x4, Pallas kernels, place_call(): pl.pallas_call(kernel, out_shape=node_out + out_shape, in_specs=[vmem] *...  4.15 us
    unnamed x34, local copies, waits for them, and re-layouts  2.76 us
  transfers between devices with their start and end apart: 21, of which 9 were waited for; matrix products, arithmetic and copies ran while one was open for 2% of the time, Pallas kernels for 7%

profile of v1, /device:TPU:0, one launch (start us, length us, event | category | flops | bytes accessed | tf_op | source)
XLA Modules:
  0.0 60.3 jit_solution(4926373328852126811)
XLA Ops:
  0.7 3.0 %collective-permute-start = (bf16[64,256]{1,0:T(8,128)(2,1)}, bf16[64,256]{1,0:T(8,128)(2,1)S(1)}, u32[]{:S(2)}, u32[]{:S(2)}) collective-permute-start(bf16[64,256]{1,0:T(8,128)(2,1)} %refs_0_.1), channel_id=1, source_target_pairs={{0,1},{1,0},{2,3},{3,2},{4,5},{5,4},{6,7},{7,6},{8,9},{9,8},{10,11... | collective-permute-start | bytes 98312 | tf_op jit(solution)/shard_map/ppermute | solution.py:125
  3.7 0.9 %slice.3.w1_ref = bf16[256,256]{1,0:T(8,128)(2,1)S(1)} slice(bf16[768,256]{1,0:T(8,128)(2,1)} %w1_ref.3), slice={[0:256], [0:256]} | slice | bytes 262144 | tf_op jit(solution)/shard_map/slice | solution.py:359
  4.6 1.2 %collective-permute-done.refs_1_ = bf16[64,256]{1,0:T(8,128)(2,1)S(1)} collective-permute-done((bf16[64,256]{1,0:T(8,128)(2,1)}, bf16[64,256]{1,0:T(8,128)(2,1)S(1)}, u32[]{:S(2)}, u32[]{:S(2)}) %collective-permute-start) | collective-permute-done | bytes 32800 | tf_op jit(solution)/shard_map/ppermute | solution.py:125
  5.8 0.0 copy-start.16
  5.8 0.2 shard_map.240
  6.0 0.0 collective-permute-start.2
  6.0 5.2 %collective-permute-start.1 = (bf16[32,256]{1,0:T(8,128)(2,1)S(1)}, bf16[32,256]{1,0:T(8,128)(2,1)S(1)}, u32[]{:S(2)}, u32[]{:S(2)}) collective-permute-start(bf16[32,256]{1,0:T(8,128)(2,1)S(1)} %get-tuple-element.98), channel_id=1, source_target_pairs={{0,30},{1,31},{2,4},{3,5},{4,2},{5,3},{6,8},{7,9},{8,6},{9,7},{10,... | collective-permute-start | bytes 49160 | tf_op jit(solution)/shard_map/ppermute | solution.py:125
  11.3 0.6 %copy-done.12 = f32[256]{0:T(256)S(1)} copy-done((f32[256]{0:T(256)S(1)}, f32[256]{0:T(256)}, u32[]{:S(2)}) %copy-start.12) | copy-done | bytes 1048
  11.9 0.0 copy-done.13
  11.9 0.0 copy-done.11
  11.9 1.0 %copy-done = bf16[768,256]{1,0:T(8,128)(2,1)S(1)} copy-done((bf16[768,256]{1,0:T(8,128)(2,1)S(1)}, bf16[768,256]{1,0:T(8,128)(2,1)}, u32[]{:S(2)}) %copy-start) | copy-done | bytes 393240
  12.9 1.0 %copy-done.8 = bf16[1024,256]{1,0:T(8,128)(2,1)S(1)} copy-done((bf16[1024,256]{1,0:T(8,128)(2,1)S(1)}, bf16[1024,256]{1,0:T(8,128)(2,1)}, u32[]{:S(2)}) %copy-start.8) | copy-done | bytes 524312
  14.0 1.1 %shard_map.241 = (f32[1024,256]{1,0:T(8,128)S(1)}, bf16[320,1024]{1,0:T(8,128)(2,1)S(1)}, bf16[1024,128]{1,0:T(8,128)(2,1)S(1)}, bf16[1024,128]{1,0:T(8,128)(2,1...) custom-call(s32[8,128]{1,0:T(8,128)S(1)} %bitcast.2, ...), custom_call_target="tpu_custom_call" | custom-call | flops 536870912 | bytes 3768640 | tf_op jit(solution)/shard_map/pallas_call | solution.py:83
  15.1 0.0 collective-permute-done.2.core_ref
  15.1 0.0 collective-permute-done.1.ring_ref
  15.1 0.0 copy-start.2
  15.2 0.0 copy-start.3
  15.2 0.0 copy-start.5
  15.2 1.7 %shard_map.242 = (bf16[1024,256]{1,0:T(8,128)(2,1)S(1)}, f32[1024,256]{1,0:T(8,128)S(1)}, f32[1024,256]{1,0:T(8,128)S(1)}, f32[1024,1]{1,0:T(8,128)S(1)}, f32[12...) custom-call(f32[8,256]{1,0:T(8,128)S(1)} %get-tuple-element.93.live_ref, ...), custom_call_target="tpu_custom_call" | custom-call | flops 402653184 | bytes 5201920 | tf_op jit(solution)/shard_map/pallas_call | solution.py:83
  16.9 1.6 %collective-permute-start.3 = (bf16[192,256]{1,0:T(8,128)(2,1)S(1)}, bf16[192,256]{1,0:T(8,128)(2,1)S(1)}, u32[]{:S(2)}, u32[]{:S(2)}) collective-permute-start(bf16[192,256]{1,0:T(8,128)(2,1)S(1)} %get-tuple-element.108.refs_0_), channel_id=1, source_target_pairs={{0,1},{1,0},{2,3},{3,2},{4,5},{5,4},{6,7},{7,6},{8,9},{9,8},{10,11... | collective-permute-start | bytes 294920 | tf_op jit(solution)/shard_map/ppermute | solution.py:125
  18.5 3.1 %collective-permute-done.3.refs_1_ = bf16[192,256]{1,0:T(8,128)(2,1)S(1)} collective-permute-done((bf16[192,256]{1,0:T(8,128)(2,1)S(1)}, bf16[192,256]{1,0:T(8,128)(2,1)S(1)}, u32[]{:S(2)}, u32[]{:S(2)}) %collective-permute-start.3) | collective-permute-done | bytes 98336 | tf_op jit(solution)/shard_map/ppermute | solution.py:125
  21.6 0.0 copy-done.2
  21.6 3.7 %shard_map.243 = (bf16[1024,256]{1,0:T(8,128)(2,1)}, f32[928,256]{1,0:T(8,128)S(1)}, bf16[928,256]{1,0:T(8,128)(2,1)S(1)}, bf16[192,256]{1,0:T(8,128)(2,1)S(1)}, f32[128,256]{1,0:T(8,128)S(1)}) custom-call(f32[8,256]{1,0:T(8,128)S(1)} %get-tuple-element.93.live_ref, bf16[320,1024]{1,0:T(8,128)(2,1)S(1)} %get-tuple-element.94.place_ref, ...), custom_call_target="tpu_custom_call" | custom-call | flops 1073741824 | bytes 8126464 | tf_op jit(solution)/shard_map/pallas_call | solution.py:83
  25.3 0.1 collective-permute-start.4
  25.3 1.8 %collective-permute-done.4.got_ref = bf16[928,256]{1,0:T(8,128)(2,1)S(1)} collective-permute-done((bf16[928,256]{1,0:T(8,128)(2,1)S(1)}, bf16[928,256]{1,0:T(8,128)(2,1)S(1)}, u32[]{:S(2)}, u32[]{:S(2)}) %collective-permute-start.4) | collective-permute-done | bytes 475168 | tf_op jit(solution)/shard_map/ppermute | solution.py:125
  27.2 0.2 shard_map.244
  27.3 1.6 %collective-permute-start.5 = (bf16[232,256]{1,0:T(8,128)(2,1)S(1)}, bf16[232,256]{1,0:T(8,128)(2,1)S(1)}, u32[]{:S(2)}, u32[]{:S(2)}) collective-permute-start(bf16[232,256]{1,0:T(8,128)(2,1)S(1)} %get-tuple-element.112), channel_id=1, source_target_pairs={{0,1},{1,0},{2,10},{3,11},{4,5},{5,4},{6,14},{7,15},{8,9},{9,8},{1... | collective-permute-start | bytes 356360 | tf_op jit(solution)/shard_map/ppermute | solution.py:125
  28.9 0.0 collective-permute-start.6
  28.9 2.0 %collective-permute-start.7 = (bf16[232,256]{1,0:T(8,128)(2,1)S(1)}, bf16[232,256]{1,0:T(8,128)(2,1)S(1)}, u32[]{:S(2)}, u32[]{:S(2)}) collective-permute-start(bf16[232,256]{1,0:T(8,128)(2,1)S(1)} %get-tuple-element.114), channel_id=1, source_target_pairs={{0,5},{1,4},{2,26},{3,27},{4,1},{5,0},{6,30},{7,31},{8,13},{9,12},... | collective-permute-start | bytes 356360 | tf_op jit(solution)/shard_map/ppermute | solution.py:125
  30.9 1.3 %collective-permute-done.5.refs_0_ = bf16[232,256]{1,0:T(8,128)(2,1)S(1)} collective-permute-done((bf16[232,256]{1,0:T(8,128)(2,1)S(1)}, bf16[232,256]{1,0:T(8,128)(2,1)S(1)}, u32[]{:S(2)}, u32[]{:S(2)}) %collective-permute-start.5) | collective-permute-done | bytes 118816 | tf_op jit(solution)/shard_map/ppermute | solution.py:125
  32.2 2.8 %collective-permute-done.6.refs_1_ = bf16[232,256]{1,0:T(8,128)(2,1)S(1)} collective-permute-done((bf16[232,256]{1,0:T(8,128)(2,1)S(1)}, bf16[232,256]{1,0:T(8,128)(2,1)S(1)}, u32[]{:S(2)}, u32[]{:S(2)}) %collective-permute-start.6) | collective-permute-done | bytes 118816 | tf_op jit(solution)/shard_map/ppermute | solution.py:125
  35.0 0.0 collective-permute-done.7.refs_2_
  35.0 0.1 shard_map.245.refs_0_
  35.1 1.3 %collective-permute-start.10 = (bf16[232,256]{1,0:T(8,128)(2,1)S(1)}, bf16[232,256]{1,0:T(8,128)(2,1)S(1)}, u32[]{:S(2)}, u32[]{:S(2)}) collective-permute-start(bf16[232,256]{1,0:T(8,128)(2,1)S(1)} %shard_map.245.refs_0_), channel_id=1, source_target_pairs={{0,24},{1,25},{2,7},{3,6},{4,28},{5,29},{6,3},{7,2},{8,16},{9,17},... | collective-permute-start | bytes 356360 | tf_op jit(solution)/shard_map/ppermute | solution.py:125
  36.3 0.0 collective-permute-start.9
  36.4 3.2 %collective-permute-start.8 = (bf16[232,256]{1,0:T(8,128)(2,1)S(1)}, bf16[232,256]{1,0:T(8,128)(2,1)S(1)}, u32[]{:S(2)}, u32[]{:S(2)}) collective-permute-start(bf16[232,256]{1,0:T(8,128)(2,1)S(1)} %shard_map.245.refs_0_), channel_id=1, source_target_pairs={{0,8},{1,9},{2,3},{3,2},{4,12},{5,13},{6,7},{7,6},{8,0},{9,1},{10,... | collective-permute-start | bytes 356360 | tf_op jit(solution)/shard_map/ppermute | solution.py:125
  39.5 0.5 collective-permute-start.11
  40.1 4.1 %collective-permute-done.11.refs_1_ = bf16[192,256]{1,0:T(8,128)(2,1)S(1)} collective-permute-done((bf16[192,256]{1,0:T(8,128)(2,1)S(1)}, bf16[192,256]{1,0:T(8,128)(2,1)S(1)}, u32[]{:S(2)}, u32[]{:S(2)}) %collective-permute-start.11) | collective-permute-done | bytes 98336 | tf_op jit(solution)/shard_map/ppermute | solution.py:125
  44.2 0.1 collective-permute-start.12
  44.3 1.8 %collective-permute-start.13 = (bf16[32,256]{1,0:T(8,128)(2,1)S(1)}, bf16[32,256]{1,0:T(8,128)(2,1)S(1)}, u32[]{:S(2)}, u32[]{:S(2)}) collective-permute-start(bf16[32,256]{1,0:T(8,128)(2,1)S(1)} %get-tuple-element.117), channel_id=1, source_target_pairs={{0,2},{1,3},{2,0},{3,1},{4,6},{5,7},{6,4},{7,5},{8,10},{9,11},{10,... | collective-permute-start | bytes 49160 | tf_op jit(solution)/shard_map/ppermute | solution.py:125
  46.0 4.1 %collective-permute-done.12.refs_5_ = bf16[32,256]{1,0:T(8,128)(2,1)S(1)} collective-permute-done((bf16[32,256]{1,0:T(8,128)(2,1)S(1)}, bf16[32,256]{1,0:T(8,128)(2,1)S(1)}, u32[]{:S(2)}, u32[]{:S(2)}) %collective-permute-start.12) | collective-permute-done | bytes 16416 | tf_op jit(solution)/shard_map/ppermute | solution.py:125
  50.1 0.0 collective-permute-done.13.refs_6_
  50.1 0.0 collective-permute-done.10.refs_3_
  50.1 0.0 collective-permute-done.9.refs_2_
  50.1 0.0 collective-permute-done.8.refs_1_
  50.1 0.2 shard_map.247
  50.4 0.1 collective-permute-start.14
  50.4 0.1 collective-permute-start.16
  50.5 2.0 %collective-permute-start.15 = (bf16[232,256]{1,0:T(8,128)(2,1)S(1)}, bf16[232,256]{1,0:T(8,128)(2,1)S(1)}, u32[]{:S(2)}, u32[]{:S(2)}) collective-permute-start(bf16[232,256]{1,0:T(8,128)(2,1)S(1)} %get-tuple-element.118.refs_0_), channel_id=1, source_target_pairs={{0,4},{1,5},{2,18},{3,19},{4,0},{5,1},{6,22},{7,23},{8,12},{9,13},... | collective-permute-start | bytes 356360 | tf_op jit(solution)/shard_map/ppermute | solution.py:125
  52.5 1.5 %collective-permute-start.18 = (bf16[232,256]{1,0:T(8,128)(2,1)S(1)}, bf16[232,256]{1,0:T(8,128)(2,1)S(1)}, u32[]{:S(2)}, u32[]{:S(2)}) collective-permute-start(bf16[232,256]{1,0:T(8,128)(2,1)S(1)} %get-tuple-element.118.refs_0_), channel_id=1, source_target_pairs={{0,1},{1,0},{2,10},{3,11},{4,5},{5,4},{6,14},{7,15},{8,9},{9,8},{1... | collective-permute-start | bytes 356360 | tf_op jit(solution)/shard_map/ppermute | solution.py:125
  54.0 0.0 collective-permute-done.14.refs_1_
  54.0 1.5 %shard_map.248 = (f32[64,256]{1,0:T(8,128)}, f32[768,256]{1,0:T(8,128)}, f32[256]{0:T(256)}, f32[256,256]{1,0:T(8,128)}, f32[256]{0:T(256)}, /*index=5*/f32[512,...) custom-call(bf16[232,256]{1,0:T(8,128)(2,1)S(1)} %get-tuple-element.118.refs_0_, ...), custom_call_target="tpu_custom_call" | custom-call | bytes 712704 | tf_op jit(solution)/shard_map/pallas_call | solution.py:599
  55.5 0.8 %collective-permute-done.16.refs_0_ = bf16[232,256]{1,0:T(8,128)(2,1)S(1)} collective-permute-done((bf16[232,256]{1,0:T(8,128)(2,1)S(1)}, bf16[232,256]{1,0:T(8,128)(2,1)S(1)}, u32[]{:S(2)}, u32[]{:S(2)}) %collective-permute-start.16) | collective-permute-done | bytes 118816 | tf_op jit(solution)/shard_map/ppermute | solution.py:125
  56.3 0.3 collective-permute-start.20
  56.6 0.8 %shard_map.249 = (f32[768,256]{1,0:T(8,128)}, f32[256]{0:T(256)}, f32[256,256]{1,0:T(8,128)}, f32[256]{0:T(256)}, f32[512,256]{1,0:T(8,128)}, /*index=5*/f32[256]{0:T(256)}, f32[256,256]{1,0:T(8,128)}, f32[256]{0:T(256)}) custom-call(bf16[232,256]{1,0:T(8,128)(2,1)S(1)} %collective-permute, ...), custom_call_target="tpu_custom_call", output_to_operand_aliasing={{0}: (1, {}), {1}: (2, {}), {2}: (3, {}), {3}: (4, {}), {4}... | custom-call | bytes 356352 | tf_op jit(solution)/shard_map/pallas_call | solution.py:599
  57.4 0.0 collective-permute-done.15.refs_0_
  57.4 0.0 collective-permute-done.18.refs_1_
  57.4 0.7 %collective-permute-start.19 = (bf16[232,256]{1,0:T(8,128)(2,1)S(1)}, bf16[232,256]{1,0:T(8,128)(2,1)S(1)}, u32[]{:S(2)}, u32[]{:S(2)}) collective-permute-start(bf16[232,256]{1,0:T(8,128)(2,1)S(1)} %collective-permute-done.18.refs_1_), channel_id=1, source_target_pairs={{0,2},{1,3},{2,0},{3,1},{4,6},{5,7},{6,4},{7,5},{8,10},{9,11},{10,... | collective-permute-start | bytes 356360 | tf_op jit(solution)/shard_map/ppermute | solution.py:125
  58.1 0.0 collective-permute-start.17
  58.1 0.0 collective-permute-done.20.refs_2_
  58.1 1.0 %shard_map.250 = (f32[768,256]{1,0:T(8,128)}, f32[256]{0:T(256)}, f32[256,256]{1,0:T(8,128)}, f32[256]{0:T(256)}, f32[512,256]{1,0:T(8,128)}, /*index=5*/f32[256]{0:T(256)}, f32[256,256]{1,0:T(8,128)}, f32[256]{0:T(256)}) custom-call(bf16[232,256]{1,0:T(8,128)(2,1)S(1)} %collective-permute, ...), custom_call_target="tpu_custom_call", output_to_operand_aliasing={{0}: (3, {}), {1}: (4, {}), {2}: (5, {}), {3}: (6, {}), {4}... | custom-call | bytes 1069056 | tf_op jit(solution)/shard_map/pallas_call | solution.py:599
  59.1 0.0 collective-permute-done.19.refs_1_
  59.1 0.3 collective-permute-done.17.refs_0_
  59.4 0.9 %shard_map.251 = (f32[768,256]{1,0:T(8,128)}, f32[256]{0:T(256)}, f32[256,256]{1,0:T(8,128)}, f32[256]{0:T(256)}, f32[512,256]{1,0:T(8,128)}, /*index=5*/f32[256]{0:T(256)}, f32[256,256]{1,0:T(8,128)}, f32[256]{0:T(256)}) custom-call(bf16[232,256]{1,0:T(8,128)(2,1)S(1)} %collective-permute, ...), custom_call_target="tpu_custom_call", output_to_operand_aliasing={{0}: (2, {}), {1}: (3, {}), {2}: (4, {}), {3}: (5, {}), {4}... | custom-call | bytes 712704 | tf_op jit(solution)/shard_map/pallas_call | solution.py:599
  (25 shorter events, 0.1 us)
Async XLA Ops:
  0.6 5.2 %copy-start.6 = (bf16[64,256]{1,0:T(8,128)(2,1)S(1)}, bf16[64,256]{1,0:T(8,128)(2,1)}, u32[]{:S(2)}) copy-start(bf16[64,256]{1,0:T(8,128)(2,1)} %refs_0_.1) | copy-start | bytes 98308
  0.7 5.2 %copy-start.7 = (s32[1,32]{1,0:T(1,128)S(1)}, s32[1,32]{1,0:T(1,128)}, u32[]{:S(2)}) copy-start(s32[1,32]{1,0:T(1,128)} %refs_4_.1) | copy-start | bytes 388
  0.7 5.1 %collective-permute-start = (bf16[64,256]{1,0:T(8,128)(2,1)}, bf16[64,256]{1,0:T(8,128)(2,1)S(1)}, u32[]{:S(2)}, u32[]{:S(2)}) collective-permute-start(bf16[64,256]{1,0:T(8,128)(2,1)} %refs_0_.1), channel_id=1, source_target_pairs={{0,1},{1,0},{2,3},{3,2},{4,5},{5,4},{6,7},{7,6},{8,9},{9,8},{10,11... | collective-permute-start | bytes 98312 | tf_op jit(solution)/shard_map/ppermute | solution.py:125
  5.8 5.4 %copy-start.10 = (s32[1024]{0:T(1024)S(1)}, s32[1024]{0:T(1024)}, u32[]{:S(2)}) copy-start(s32[1024]{0:T(1024)} %param.22) | copy-start | bytes 12292
  5.8 5.4 %copy-start.14 = (f32[256]{0:T(256)S(1)}, f32[256]{0:T(256)}, u32[]{:S(2)}) copy-start(f32[256]{0:T(256)} %nb2_ref.1) | copy-start | bytes 3076
  5.8 5.4 %copy-start.16 = (s32[64]{0:T(128)S(1)}, s32[64]{0:T(128)}, u32[]{:S(2)}) copy-start(s32[64]{0:T(128)} %sea_ref.1) | copy-start | bytes 772
  6.0 5.3 %copy-start.9 = (s32[1024]{0:T(1024)S(1)}, s32[1024]{0:T(1024)}, u32[]{:S(2)}) copy-start(s32[1024]{0:T(1024)} %param.21) | copy-start | bytes 12292
  6.0 9.1 %collective-permute-start.2 = (bf16[32,256]{1,0:T(8,128)(2,1)S(1)}, bf16[32,256]{1,0:T(8,128)(2,1)S(1)}, u32[]{:S(2)}, u32[]{:S(2)}) collective-permute-start(bf16[32,256]{1,0:T(8,128)(2,1)S(1)} %get-tuple-element.98), channel_id=1, source_target_pairs={{0,2},{1,3},{2,0},{3,1},{4,6},{5,7},{6,4},{7,5},{8,10},{9,11},{10,... | collective-permute-start | bytes 49160 | tf_op jit(solution)/shard_map/ppermute | solution.py:125
  6.0 9.1 %collective-permute-start.1 = (bf16[32,256]{1,0:T(8,128)(2,1)S(1)}, bf16[32,256]{1,0:T(8,128)(2,1)S(1)}, u32[]{:S(2)}, u32[]{:S(2)}) collective-permute-start(bf16[32,256]{1,0:T(8,128)(2,1)S(1)} %get-tuple-element.98), channel_id=1, source_target_pairs={{0,30},{1,31},{2,4},{3,5},{4,2},{5,3},{6,8},{7,9},{8,6},{9,7},{10,... | collective-permute-start | bytes 49160 | tf_op jit(solution)/shard_map/ppermute | solution.py:125
  11.2 0.7 %copy-start.12 = (f32[256]{0:T(256)S(1)}, f32[256]{0:T(256)}, u32[]{:S(2)}) copy-start(f32[256]{0:T(256)} %b2_ref.1) | copy-start | bytes 3076
  11.2 0.7 %copy-start.13 = (f32[256]{0:T(256)S(1)}, f32[256]{0:T(256)}, u32[]{:S(2)}) copy-start(f32[256]{0:T(256)} %nb1_ref.1) | copy-start | bytes 3076
  11.2 0.7 %copy-start.11 = (f32[256]{0:T(256)S(1)}, f32[256]{0:T(256)}, u32[]{:S(2)}) copy-start(f32[256]{0:T(256)} %b1_ref.1) | copy-start | bytes 3076
  11.2 0.7 %copy-start.15 = (s32[16]{0:T(128)S(1)}, s32[16]{0:T(128)}, u32[]{:S(2)}) copy-start(s32[16]{0:T(128)} %be_ref.1) | copy-start | bytes 196
  11.9 1.0 %copy-start = (bf16[768,256]{1,0:T(8,128)(2,1)S(1)}, bf16[768,256]{1,0:T(8,128)(2,1)}, u32[]{:S(2)}) copy-start(bf16[768,256]{1,0:T(8,128)(2,1)} %w1_ref.3) | copy-start | bytes 1179652
  12.9 1.0 %copy-start.8 = (bf16[1024,256]{1,0:T(8,128)(2,1)S(1)}, bf16[1024,256]{1,0:T(8,128)(2,1)}, u32[]{:S(2)}) copy-start(bf16[1024,256]{1,0:T(8,128)(2,1)} %e_ref.1) | copy-start | bytes 1572868
  14.0 1.2 %copy-start.1 = (bf16[256,256]{1,0:T(8,128)(2,1)S(1)}, bf16[256,256]{1,0:T(8,128)(2,1)}, u32[]{:S(2)}) copy-start(bf16[256,256]{1,0:T(8,128)(2,1)} %w2_ref.3) | copy-start | bytes 393220
  14.0 1.2 %copy-start.4 = (bf16[64,256]{1,0:T(8,128)(2,1)S(1)}, bf16[64,256]{1,0:T(8,128)(2,1)}, u32[]{:S(2)}) copy-start(bf16[64,256]{1,0:T(8,128)(2,1)} %refs_5_.1) | copy-start | bytes 98308
  15.1 6.4 %copy-start.2 = (bf16[1024,256]{1,0:T(8,128)(2,1)S(1)}, bf16[1024,256]{1,0:T(8,128)(2,1)}, u32[]{:S(2)}) copy-start(bf16[1024,256]{1,0:T(8,128)(2,1)} %geo_ref.1) | copy-start | bytes 1572868
  15.2 6.4 %copy-start.3 = (bf16[512,256]{1,0:T(8,128)(2,1)S(1)}, bf16[512,256]{1,0:T(8,128)(2,1)}, u32[]{:S(2)}) copy-start(bf16[512,256]{1,0:T(8,128)(2,1)} %nw1_ref.1) | copy-start | bytes 786436
  15.2 6.4 %copy-start.5 = (bf16[256,256]{1,0:T(8,128)(2,1)S(1)}, bf16[256,256]{1,0:T(8,128)(2,1)}, u32[]{:S(2)}) copy-start(bf16[256,256]{1,0:T(8,128)(2,1)} %nw2_ref.1) | copy-start | bytes 393220
  16.9 4.7 %collective-permute-start.3 = (bf16[192,256]{1,0:T(8,128)(2,1)S(1)}, bf16[192,256]{1,0:T(8,128)(2,1)S(1)}, u32[]{:S(2)}, u32[]{:S(2)}) collective-permute-start(bf16[192,256]{1,0:T(8,128)(2,1)S(1)} %get-tuple-element.108.refs_0_), channel_id=1, source_target_pairs={{0,1},{1,0},{2,3},{3,2},{4,5},{5,4},{6,7},{7,6},{8,9},{9,8},{10,11... | collective-permute-start | bytes 294920 | tf_op jit(solution)/shard_map/ppermute | solution.py:125
  25.3 1.9 %collective-permute-start.4 = (bf16[928,256]{1,0:T(8,128)(2,1)S(1)}, bf16[928,256]{1,0:T(8,128)(2,1)S(1)}, u32[]{:S(2)}, u32[]{:S(2)}) collective-permute-start(bf16[928,256]{1,0:T(8,128)(2,1)S(1)} %get-tuple-element.110), channel_id=1, source_target_pairs={{0,2},{1,3},{2,0},{3,1},{4,6},{5,7},{6,4},{7,5},{8,10},{9,11},{10,... | collective-permute-start | bytes 1425416 | tf_op jit(solution)/shard_map/ppermute | solution.py:125
  27.3 4.9 %collective-permute-start.5 = (bf16[232,256]{1,0:T(8,128)(2,1)S(1)}, bf16[232,256]{1,0:T(8,128)(2,1)S(1)}, u32[]{:S(2)}, u32[]{:S(2)}) collective-permute-start(bf16[232,256]{1,0:T(8,128)(2,1)S(1)} %get-tuple-element.112), channel_id=1, source_target_pairs={{0,1},{1,0},{2,10},{3,11},{4,5},{5,4},{6,14},{7,15},{8,9},{9,8},{1... | collective-permute-start | bytes 356360 | tf_op jit(solution)/shard_map/ppermute | solution.py:125
  28.9 6.1 %collective-permute-start.6 = (bf16[232,256]{1,0:T(8,128)(2,1)S(1)}, bf16[232,256]{1,0:T(8,128)(2,1)S(1)}, u32[]{:S(2)}, u32[]{:S(2)}) collective-permute-start(bf16[232,256]{1,0:T(8,128)(2,1)S(1)} %get-tuple-element.113), channel_id=1, source_target_pairs={{0,4},{1,5},{2,18},{3,19},{4,0},{5,1},{6,22},{7,23},{8,12},{9,13},... | collective-permute-start | bytes 356360 | tf_op jit(solution)/shard_map/ppermute | solution.py:125
  28.9 6.1 %collective-permute-start.7 = (bf16[232,256]{1,0:T(8,128)(2,1)S(1)}, bf16[232,256]{1,0:T(8,128)(2,1)S(1)}, u32[]{:S(2)}, u32[]{:S(2)}) collective-permute-start(bf16[232,256]{1,0:T(8,128)(2,1)S(1)} %get-tuple-element.114), channel_id=1, source_target_pairs={{0,5},{1,4},{2,26},{3,27},{4,1},{5,0},{6,30},{7,31},{8,13},{9,12},... | collective-permute-start | bytes 356360 | tf_op jit(solution)/shard_map/ppermute | solution.py:125
  35.1 15.0 %collective-permute-start.10 = (bf16[232,256]{1,0:T(8,128)(2,1)S(1)}, bf16[232,256]{1,0:T(8,128)(2,1)S(1)}, u32[]{:S(2)}, u32[]{:S(2)}) collective-permute-start(bf16[232,256]{1,0:T(8,128)(2,1)S(1)} %shard_map.245.refs_0_), channel_id=1, source_target_pairs={{0,24},{1,25},{2,7},{3,6},{4,28},{5,29},{6,3},{7,2},{8,16},{9,17},... | collective-permute-start | bytes 356360 | tf_op jit(solution)/shard_map/ppermute | solution.py:125
  36.3 13.8 %collective-permute-start.9 = (bf16[232,256]{1,0:T(8,128)(2,1)S(1)}, bf16[232,256]{1,0:T(8,128)(2,1)S(1)}, u32[]{:S(2)}, u32[]{:S(2)}) collective-permute-start(bf16[232,256]{1,0:T(8,128)(2,1)S(1)} %shard_map.245.refs_0_), channel_id=1, source_target_pairs={{0,16},{1,17},{2,6},{3,7},{4,20},{5,21},{6,2},{7,3},{8,24},{9,25},... | collective-permute-start | bytes 356360 | tf_op jit(solution)/shard_map/ppermute | solution.py:125
  36.4 13.8 %collective-permute-start.8 = (bf16[232,256]{1,0:T(8,128)(2,1)S(1)}, bf16[232,256]{1,0:T(8,128)(2,1)S(1)}, u32[]{:S(2)}, u32[]{:S(2)}) collective-permute-start(bf16[232,256]{1,0:T(8,128)(2,1)S(1)} %shard_map.245.refs_0_), channel_id=1, source_target_pairs={{0,8},{1,9},{2,3},{3,2},{4,12},{5,13},{6,7},{7,6},{8,0},{9,1},{10,... | collective-permute-start | bytes 356360 | tf_op jit(solution)/shard_map/ppermute | solution.py:125
  39.5 4.6 %collective-permute-start.11 = (bf16[192,256]{1,0:T(8,128)(2,1)S(1)}, bf16[192,256]{1,0:T(8,128)(2,1)S(1)}, u32[]{:S(2)}, u32[]{:S(2)}) collective-permute-start(bf16[192,256]{1,0:T(8,128)(2,1)S(1)} %get-tuple-element.115.refs_0_), channel_id=1, source_target_pairs={{0,1},{1,0},{2,3},{3,2},{4,5},{5,4},{6,7},{7,6},{8,9},{9,8},{10,11... | collective-permute-start | bytes 294920 | tf_op jit(solution)/shard_map/ppermute | solution.py:125
  44.2 5.9 %collective-permute-start.12 = (bf16[32,256]{1,0:T(8,128)(2,1)S(1)}, bf16[32,256]{1,0:T(8,128)(2,1)S(1)}, u32[]{:S(2)}, u32[]{:S(2)}) collective-permute-start(bf16[32,256]{1,0:T(8,128)(2,1)S(1)} %get-tuple-element.116), channel_id=1, source_target_pairs={{0,30},{1,31},{2,4},{3,5},{4,2},{5,3},{6,8},{7,9},{8,6},{9,7},{10,... | collective-permute-start | bytes 49160 | tf_op jit(solution)/shard_map/ppermute | solution.py:125
  44.3 5.9 %collective-permute-start.13 = (bf16[32,256]{1,0:T(8,128)(2,1)S(1)}, bf16[32,256]{1,0:T(8,128)(2,1)S(1)}, u32[]{:S(2)}, u32[]{:S(2)}) collective-permute-start(bf16[32,256]{1,0:T(8,128)(2,1)S(1)} %get-tuple-element.117), channel_id=1, source_target_pairs={{0,2},{1,3},{2,0},{3,1},{4,6},{5,7},{6,4},{7,5},{8,10},{9,11},{10,... | collective-permute-start | bytes 49160 | tf_op jit(solution)/shard_map/ppermute | solution.py:125
  50.4 3.6 %collective-permute-start.14 = (bf16[232,256]{1,0:T(8,128)(2,1)S(1)}, bf16[232,256]{1,0:T(8,128)(2,1)S(1)}, u32[]{:S(2)}, u32[]{:S(2)}) collective-permute-start(bf16[232,256]{1,0:T(8,128)(2,1)S(1)} %get-tuple-element.118.refs_0_), channel_id=1, source_target_pairs={{0,2},{1,3},{2,0},{3,1},{4,6},{5,7},{6,4},{7,5},{8,10},{9,11},{10,... | collective-permute-start | bytes 356360 | tf_op jit(solution)/shard_map/ppermute | solution.py:125
  50.4 5.9 %collective-permute-start.16 = (bf16[232,256]{1,0:T(8,128)(2,1)S(1)}, bf16[232,256]{1,0:T(8,128)(2,1)S(1)}, u32[]{:S(2)}, u32[]{:S(2)}) collective-permute-start(bf16[232,256]{1,0:T(8,128)(2,1)S(1)} %get-tuple-element.118.refs_0_), channel_id=1, source_target_pairs={{0,5},{1,4},{2,26},{3,27},{4,1},{5,0},{6,30},{7,31},{8,13},{9,12},... | collective-permute-start | bytes 356360 | tf_op jit(solution)/shard_map/ppermute | solution.py:125
  50.5 6.9 %collective-permute-start.15 = (bf16[232,256]{1,0:T(8,128)(2,1)S(1)}, bf16[232,256]{1,0:T(8,128)(2,1)S(1)}, u32[]{:S(2)}, u32[]{:S(2)}) collective-permute-start(bf16[232,256]{1,0:T(8,128)(2,1)S(1)} %get-tuple-element.118.refs_0_), channel_id=1, source_target_pairs={{0,4},{1,5},{2,18},{3,19},{4,0},{5,1},{6,22},{7,23},{8,12},{9,13},... | collective-permute-start | bytes 356360 | tf_op jit(solution)/shard_map/ppermute | solution.py:125
  52.5 4.9 %collective-permute-start.18 = (bf16[232,256]{1,0:T(8,128)(2,1)S(1)}, bf16[232,256]{1,0:T(8,128)(2,1)S(1)}, u32[]{:S(2)}, u32[]{:S(2)}) collective-permute-start(bf16[232,256]{1,0:T(8,128)(2,1)S(1)} %get-tuple-element.118.refs_0_), channel_id=1, source_target_pairs={{0,1},{1,0},{2,10},{3,11},{4,5},{5,4},{6,14},{7,15},{8,9},{9,8},{1... | collective-permute-start | bytes 356360 | tf_op jit(solution)/shard_map/ppermute | solution.py:125
  56.3 1.7 %collective-permute-start.20 = (bf16[232,256]{1,0:T(8,128)(2,1)S(1)}, bf16[232,256]{1,0:T(8,128)(2,1)S(1)}, u32[]{:S(2)}, u32[]{:S(2)}) collective-permute-start(bf16[232,256]{1,0:T(8,128)(2,1)S(1)} %collective-permute-done.16.refs_0_), channel_id=1, source_target_pairs={{0,2},{1,3},{2,0},{3,1},{4,6},{5,7},{6,4},{7,5},{8,10},{9,11},{10,... | collective-permute-start | bytes 356360 | tf_op jit(solution)/shard_map/ppermute | solution.py:125
  57.4 1.7 %collective-permute-start.19 = (bf16[232,256]{1,0:T(8,128)(2,1)S(1)}, bf16[232,256]{1,0:T(8,128)(2,1)S(1)}, u32[]{:S(2)}, u32[]{:S(2)}) collective-permute-start(bf16[232,256]{1,0:T(8,128)(2,1)S(1)} %collective-permute-done.18.refs_1_), channel_id=1, source_target_pairs={{0,2},{1,3},{2,0},{3,1},{4,6},{5,7},{6,4},{7,5},{8,10},{9,11},{10,... | collective-permute-start | bytes 356360 | tf_op jit(solution)/shard_map/ppermute | solution.py:125
  58.1 1.3 %collective-permute-start.17 = (bf16[232,256]{1,0:T(8,128)(2,1)S(1)}, bf16[232,256]{1,0:T(8,128)(2,1)S(1)}, u32[]{:S(2)}, u32[]{:S(2)}) collective-permute-start(bf16[232,256]{1,0:T(8,128)(2,1)S(1)} %collective-permute-done.15.refs_0_), channel_id=1, source_target_pairs={{0,2},{1,3},{2,0},{3,1},{4,6},{5,7},{6,4},{7,5},{8,10},{9,11},{10,... | collective-permute-start | bytes 356360 | tf_op jit(solution)/shard_map/ppermute | solution.py:125

commit v2 on v1

--- a/solution.py
+++ b/solution.py
@@ -10,6 +10,7 @@
 
 EB = 128
 LANES = 128
+WIDE = 8
 NORM_EPS = 1e-05
 BF = jnp.bfloat16
 F32 = jnp.float32
@@ -236,16 +237,17 @@
             [ref[pl.ds(index * per_chunk + j, 1), :] for j in range(per_chunk)], axis=1
         )
 
-    def chunk_live(ref, index):
-        rows = [
-            jnp.broadcast_to(ref[pl.ds(index * per_chunk + j, 1), :], (EB, feat))
-            for j in range(per_chunk)
-        ]
-        return jnp.concatenate(rows, axis=0)
-
     b_width = round_up(2 * band, LANES)
     h_width = round_up(2 * halo, LANES)
     r_width = round_up(band, LANES)
+    wide = WIDE * EB if slots % WIDE == 0 else EB
+
+    def wide_live(ref, index):
+        rows = [
+            jnp.broadcast_to(ref[pl.ds(index * (wide // EB) + j, 1), :], (EB, feat))
+            for j in range(wide // EB)
+        ]
+        return jnp.concatenate(rows, axis=0)
 
     theirs = [groups.helper_swap(node_latent, k) for k in range(1, helpers)]
 
@@ -332,8 +334,8 @@
         halo_ref[pl.ds(pl.multiple_of(odd * halo, halo), halo), :] = ring_ref[...]
         halo_ref[pl.ds(pl.multiple_of((1 - odd) * halo, halo), halo), :] = core_ref[...]
         split_store(table, h_width, 0, dot(halo_ref[...], w1_ref[...]))
-        for i in range(edges // chunk):
-            rows = pl.ds(i * chunk, chunk)
+        for i in range(edges // wide):
+            rows = pl.ds(i * wide, wide)
             pick = halo_pick_ref[rows, :]
             pre = pre_ref[rows, :] + dot(jnp.concatenate([pick, pick], axis=1), table[...])
             sig = jax.nn.sigmoid(pre)
@@ -343,7 +345,7 @@
             normed, inv = normalise(dot(hidden, w2_ref[...]) + bias_ref[1:2, :])
             norm_ref[rows, :] = normed
             inv_ref[rows, :] = inv
-            message = (normed * chunk_live(live_ref, i)).astype(BF)
+            message = (normed * wide_live(live_ref, i)).astype(BF)
             part = dot(place_ref[look:, rows], message)
             if i == 0:
                 agg[...] = part
@@ -408,9 +410,9 @@
         gb_2 = jnp.zeros((1, feat), F32)
         gw_1 = jnp.zeros((feat, feat), F32)
         gw_2 = jnp.zeros((feat, feat), F32)
-        for i in range(edges // chunk):
-            rows = pl.ds(i * chunk, chunk)
-            live = chunk_live(live_ref, i)
+        for i in range(edges // wide):
+            rows = pl.ds(i * wide, wide)
+            live = wide_live(live_ref, i)
             geo = geo_ref[rows, :].astype(F32)
             at_recv = dot(recv_pick_ref[rows, :band], agg_grad)
             msg_grad = (geo + at_recv) * live
@@ -462,7 +464,7 @@
          hidden, slope, normed, inv, edge_w1, edge_w2, node_w1, node_w2, biases, agg_own, *swaps],
         scratch=[pltpu.VMEM((half * groups.core, feat), F32), pltpu.VMEM((look + band, feat), F32),
                  pltpu.VMEM((band, feat), BF), pltpu.VMEM((edges, feat), BF),
-                 pltpu.SemaphoreType.DMA((edges // chunk,))],
+                 pltpu.SemaphoreType.DMA((edges // wide,))],
         hbm_out=(0,),
         flops=8 * unit,
     )

time: 60.5 us -> 59.5 us (0.983)
  Pallas kernels: 11.3 us -> 10.3 us
    pallas_call x8, Pallas kernels: 7.15 us -> 6.15 us  [call(): pl.pallas_call(kernel, out_shape=out_shape, in_specs=in_specs, out_specs=...]
where the time goes in v2:
time: 59.5 us; the launch traced here: 59.3 us
  starting transfers between devices  24.8 us (42%)
  waiting for transfers between devices  19.6 us (33%)
  Pallas kernels  10.3 us (17%)
  local copies, waits for them, and re-layouts  3.67 us (6%)
  between operations  0.93 us (2%)
    ppermute x21, starting transfers between devices, permute(): return lax.ppermute(array, AXES, pairs)  24.8 us
    ppermute x21, waiting for transfers between devices, permute(): return lax.ppermute(array, AXES, pairs)  19.6 us
    pallas_call x8, Pallas kernels, call(): pl.pallas_call(kernel, out_shape=out_shape, in_specs=in_specs, out_specs=...  6.15 us
    pallas_call x4, Pallas kernels, place_call(): pl.pallas_call(kernel, out_shape=node_out + out_shape, in_specs=[vmem] *...  4.15 us
    unnamed x34, local copies, waits for them, and re-layouts  2.76 us
  transfers between devices with their start and end apart: 21, of which 9 were waited for; matrix products, arithmetic and copies ran while one was open for 2% of the time, Pallas kernels for 7%

profile of v2, /device:TPU:0, one launch (start us, length us, event | category | flops | bytes accessed | tf_op | source)
XLA Modules:
  0.0 59.3 jit_solution(4069682858891524008)
XLA Ops:
  0.7 3.0 %collective-permute-start = (bf16[64,256]{1,0:T(8,128)(2,1)}, bf16[64,256]{1,0:T(8,128)(2,1)S(1)}, u32[]{:S(2)}, u32[]{:S(2)}) collective-permute-start(bf16[64,256]{1,0:T(8,128)(2,1)} %refs_0_.1), channel_id=1, source_target_pairs={{0,1},{1,0},{2,3},{3,2},{4,5},{5,4},{6,7},{7,6},{8,9},{9,8},{10,11... | collective-permute-start | bytes 98312 | tf_op jit(solution)/shard_map/ppermute | solution.py:126
  3.7 0.9 %slice.3.w1_ref = bf16[256,256]{1,0:T(8,128)(2,1)S(1)} slice(bf16[768,256]{1,0:T(8,128)(2,1)} %w1_ref.3), slice={[0:256], [0:256]} | slice | bytes 262144 | tf_op jit(solution)/shard_map/slice | solution.py:361
  4.6 1.2 %collective-permute-done.refs_1_ = bf16[64,256]{1,0:T(8,128)(2,1)S(1)} collective-permute-done((bf16[64,256]{1,0:T(8,128)(2,1)}, bf16[64,256]{1,0:T(8,128)(2,1)S(1)}, u32[]{:S(2)}, u32[]{:S(2)}) %collective-permute-start) | collective-permute-done | bytes 32800 | tf_op jit(solution)/shard_map/ppermute | solution.py:126
  5.8 0.0 copy-start.16
  5.8 0.2 shard_map.240
  6.0 0.0 collective-permute-start.2
  6.0 5.2 %collective-permute-start.1 = (bf16[32,256]{1,0:T(8,128)(2,1)S(1)}, bf16[32,256]{1,0:T(8,128)(2,1)S(1)}, u32[]{:S(2)}, u32[]{:S(2)}) collective-permute-start(bf16[32,256]{1,0:T(8,128)(2,1)S(1)} %get-tuple-element.98), channel_id=1, source_target_pairs={{0,30},{1,31},{2,4},{3,5},{4,2},{5,3},{6,8},{7,9},{8,6},{9,7},{10,... | collective-permute-start | bytes 49160 | tf_op jit(solution)/shard_map/ppermute | solution.py:126
  11.3 0.6 %copy-done.12 = f32[256]{0:T(256)S(1)} copy-done((f32[256]{0:T(256)S(1)}, f32[256]{0:T(256)}, u32[]{:S(2)}) %copy-start.12) | copy-done | bytes 1048
  11.9 0.0 copy-done.13
  11.9 0.0 copy-done.11
  11.9 1.0 %copy-done = bf16[768,256]{1,0:T(8,128)(2,1)S(1)} copy-done((bf16[768,256]{1,0:T(8,128)(2,1)S(1)}, bf16[768,256]{1,0:T(8,128)(2,1)}, u32[]{:S(2)}) %copy-start) | copy-done | bytes 393240
  12.9 1.0 %copy-done.8 = bf16[1024,256]{1,0:T(8,128)(2,1)S(1)} copy-done((bf16[1024,256]{1,0:T(8,128)(2,1)S(1)}, bf16[1024,256]{1,0:T(8,128)(2,1)}, u32[]{:S(2)}) %copy-start.8) | copy-done | bytes 524312
  14.0 1.1 %shard_map.241 = (f32[1024,256]{1,0:T(8,128)S(1)}, bf16[320,1024]{1,0:T(8,128)(2,1)S(1)}, bf16[1024,128]{1,0:T(8,128)(2,1)S(1)}, bf16[1024,128]{1,0:T(8,128)(2,1...) custom-call(s32[8,128]{1,0:T(8,128)S(1)} %bitcast.2, ...), custom_call_target="tpu_custom_call" | custom-call | flops 536870912 | bytes 3768640 | tf_op jit(solution)/shard_map/pallas_call | solution.py:84
  15.1 0.0 collective-permute-done.2.core_ref
  15.1 0.0 collective-permute-done.1.ring_ref
  15.1 0.0 copy-start.2
  15.2 0.0 copy-start.3
  15.2 0.0 copy-start.5
  15.2 1.2 %shard_map.242 = (bf16[1024,256]{1,0:T(8,128)(2,1)S(1)}, f32[1024,256]{1,0:T(8,128)S(1)}, f32[1024,256]{1,0:T(8,128)S(1)}, f32[1024,1]{1,0:T(8,128)S(1)}, f32[12...) custom-call(f32[8,256]{1,0:T(8,128)S(1)} %get-tuple-element.93.live_ref, ...), custom_call_target="tpu_custom_call" | custom-call | flops 402653184 | bytes 5201920 | tf_op jit(solution)/shard_map/pallas_call | solution.py:84
  16.4 1.6 %collective-permute-start.3 = (bf16[192,256]{1,0:T(8,128)(2,1)S(1)}, bf16[192,256]{1,0:T(8,128)(2,1)S(1)}, u32[]{:S(2)}, u32[]{:S(2)}) collective-permute-start(bf16[192,256]{1,0:T(8,128)(2,1)S(1)} %get-tuple-element.108.refs_0_), channel_id=1, source_target_pairs={{0,1},{1,0},{2,3},{3,2},{4,5},{5,4},{6,7},{7,6},{8,9},{9,8},{10,11... | collective-permute-start | bytes 294920 | tf_op jit(solution)/shard_map/ppermute | solution.py:126
  17.9 3.1 %collective-permute-done.3.refs_1_ = bf16[192,256]{1,0:T(8,128)(2,1)S(1)} collective-permute-done((bf16[192,256]{1,0:T(8,128)(2,1)S(1)}, bf16[192,256]{1,0:T(8,128)(2,1)S(1)}, u32[]{:S(2)}, u32[]{:S(2)}) %collective-permute-start.3) | collective-permute-done | bytes 98336 | tf_op jit(solution)/shard_map/ppermute | solution.py:126
  21.1 0.0 copy-done.3
  21.1 3.2 %shard_map.243 = (bf16[1024,256]{1,0:T(8,128)(2,1)}, f32[928,256]{1,0:T(8,128)S(1)}, bf16[928,256]{1,0:T(8,128)(2,1)S(1)}, bf16[192,256]{1,0:T(8,128)(2,1)S(1)}, f32[128,256]{1,0:T(8,128)S(1)}) custom-call(f32[8,256]{1,0:T(8,128)S(1)} %get-tuple-element.93.live_ref, bf16[320,1024]{1,0:T(8,128)(2,1)S(1)} %get-tuple-element.94.place_ref, ...), custom_call_target="tpu_custom_call" | custom-call | flops 1073741824 | bytes 8126464 | tf_op jit(solution)/shard_map/pallas_call | solution.py:84
  24.3 0.1 collective-permute-start.4
  24.3 1.8 %collective-permute-done.4.got_ref = bf16[928,256]{1,0:T(8,128)(2,1)S(1)} collective-permute-done((bf16[928,256]{1,0:T(8,128)(2,1)S(1)}, bf16[928,256]{1,0:T(8,128)(2,1)S(1)}, u32[]{:S(2)}, u32[]{:S(2)}) %collective-permute-start.4) | collective-permute-done | bytes 475168 | tf_op jit(solution)/shard_map/ppermute | solution.py:126
  26.2 0.2 shard_map.244
  26.3 1.6 %collective-permute-start.5 = (bf16[232,256]{1,0:T(8,128)(2,1)S(1)}, bf16[232,256]{1,0:T(8,128)(2,1)S(1)}, u32[]{:S(2)}, u32[]{:S(2)}) collective-permute-start(bf16[232,256]{1,0:T(8,128)(2,1)S(1)} %get-tuple-element.112), channel_id=1, source_target_pairs={{0,1},{1,0},{2,10},{3,11},{4,5},{5,4},{6,14},{7,15},{8,9},{9,8},{1... | collective-permute-start | bytes 356360 | tf_op jit(solution)/shard_map/ppermute | solution.py:126
  27.9 0.0 collective-permute-start.6
  27.9 2.0 %collective-permute-start.7 = (bf16[232,256]{1,0:T(8,128)(2,1)S(1)}, bf16[232,256]{1,0:T(8,128)(2,1)S(1)}, u32[]{:S(2)}, u32[]{:S(2)}) collective-permute-start(bf16[232,256]{1,0:T(8,128)(2,1)S(1)} %get-tuple-element.114), channel_id=1, source_target_pairs={{0,5},{1,4},{2,26},{3,27},{4,1},{5,0},{6,30},{7,31},{8,13},{9,12},... | collective-permute-start | bytes 356360 | tf_op jit(solution)/shard_map/ppermute | solution.py:126
  29.9 1.3 %collective-permute-done.5.refs_0_ = bf16[232,256]{1,0:T(8,128)(2,1)S(1)} collective-permute-done((bf16[232,256]{1,0:T(8,128)(2,1)S(1)}, bf16[232,256]{1,0:T(8,128)(2,1)S(1)}, u32[]{:S(2)}, u32[]{:S(2)}) %collective-permute-start.5) | collective-permute-done | bytes 118816 | tf_op jit(solution)/shard_map/ppermute | solution.py:126
  31.2 2.8 %collective-permute-done.6.refs_1_ = bf16[232,256]{1,0:T(8,128)(2,1)S(1)} collective-permute-done((bf16[232,256]{1,0:T(8,128)(2,1)S(1)}, bf16[232,256]{1,0:T(8,128)(2,1)S(1)}, u32[]{:S(2)}, u32[]{:S(2)}) %collective-permute-start.6) | collective-permute-done | bytes 118816 | tf_op jit(solution)/shard_map/ppermute | solution.py:126
  34.0 0.0 collective-permute-done.7.refs_2_
  34.0 0.1 shard_map.245.refs_0_
  34.1 1.3 %collective-permute-start.10 = (bf16[232,256]{1,0:T(8,128)(2,1)S(1)}, bf16[232,256]{1,0:T(8,128)(2,1)S(1)}, u32[]{:S(2)}, u32[]{:S(2)}) collective-permute-start(bf16[232,256]{1,0:T(8,128)(2,1)S(1)} %shard_map.245.refs_0_), channel_id=1, source_target_pairs={{0,24},{1,25},{2,7},{3,6},{4,28},{5,29},{6,3},{7,2},{8,16},{9,17},... | collective-permute-start | bytes 356360 | tf_op jit(solution)/shard_map/ppermute | solution.py:126
  35.3 0.0 collective-permute-start.9
  35.3 3.2 %collective-permute-start.8 = (bf16[232,256]{1,0:T(8,128)(2,1)S(1)}, bf16[232,256]{1,0:T(8,128)(2,1)S(1)}, u32[]{:S(2)}, u32[]{:S(2)}) collective-permute-start(bf16[232,256]{1,0:T(8,128)(2,1)S(1)} %shard_map.245.refs_0_), channel_id=1, source_target_pairs={{0,8},{1,9},{2,3},{3,2},{4,12},{5,13},{6,7},{7,6},{8,0},{9,1},{10,... | collective-permute-start | bytes 356360 | tf_op jit(solution)/shard_map/ppermute | solution.py:126
  38.5 0.5 collective-permute-start.11
  39.1 4.1 %collective-permute-done.11.refs_1_ = bf16[192,256]{1,0:T(8,128)(2,1)S(1)} collective-permute-done((bf16[192,256]{1,0:T(8,128)(2,1)S(1)}, bf16[192,256]{1,0:T(8,128)(2,1)S(1)}, u32[]{:S(2)}, u32[]{:S(2)}) %collective-permute-start.11) | collective-permute-done | bytes 98336 | tf_op jit(solution)/shard_map/ppermute | solution.py:126
  43.2 0.1 collective-permute-start.12
  43.2 1.8 %collective-permute-start.13 = (bf16[32,256]{1,0:T(8,128)(2,1)S(1)}, bf16[32,256]{1,0:T(8,128)(2,1)S(1)}, u32[]{:S(2)}, u32[]{:S(2)}) collective-permute-start(bf16[32,256]{1,0:T(8,128)(2,1)S(1)} %get-tuple-element.117), channel_id=1, source_target_pairs={{0,2},{1,3},{2,0},{3,1},{4,6},{5,7},{6,4},{7,5},{8,10},{9,11},{10,... | collective-permute-start | bytes 49160 | tf_op jit(solution)/shard_map/ppermute | solution.py:126
  45.0 4.1 %collective-permute-done.12.refs_5_ = bf16[32,256]{1,0:T(8,128)(2,1)S(1)} collective-permute-done((bf16[32,256]{1,0:T(8,128)(2,1)S(1)}, bf16[32,256]{1,0:T(8,128)(2,1)S(1)}, u32[]{:S(2)}, u32[]{:S(2)}) %collective-permute-start.12) | collective-permute-done | bytes 16416 | tf_op jit(solution)/shard_map/ppermute | solution.py:126
  49.1 0.0 collective-permute-done.13.refs_6_
  49.1 0.0 collective-permute-done.10.refs_3_
  49.1 0.0 collective-permute-done.9.refs_2_
  49.1 0.0 collective-permute-done.8.refs_1_
  49.1 0.2 shard_map.247
  49.4 0.1 collective-permute-start.14
  49.4 0.1 collective-permute-start.16
  49.5 2.0 %collective-permute-start.15 = (bf16[232,256]{1,0:T(8,128)(2,1)S(1)}, bf16[232,256]{1,0:T(8,128)(2,1)S(1)}, u32[]{:S(2)}, u32[]{:S(2)}) collective-permute-start(bf16[232,256]{1,0:T(8,128)(2,1)S(1)} %get-tuple-element.118.refs_0_), channel_id=1, source_target_pairs={{0,4},{1,5},{2,18},{3,19},{4,0},{5,1},{6,22},{7,23},{8,12},{9,13},... | collective-permute-start | bytes 356360 | tf_op jit(solution)/shard_map/ppermute | solution.py:126
  51.5 1.5 %collective-permute-start.18 = (bf16[232,256]{1,0:T(8,128)(2,1)S(1)}, bf16[232,256]{1,0:T(8,128)(2,1)S(1)}, u32[]{:S(2)}, u32[]{:S(2)}) collective-permute-start(bf16[232,256]{1,0:T(8,128)(2,1)S(1)} %get-tuple-element.118.refs_0_), channel_id=1, source_target_pairs={{0,1},{1,0},{2,10},{3,11},{4,5},{5,4},{6,14},{7,15},{8,9},{9,8},{1... | collective-permute-start | bytes 356360 | tf_op jit(solution)/shard_map/ppermute | solution.py:126
  53.0 0.0 collective-permute-done.14.refs_1_
  53.0 1.5 %shard_map.248 = (f32[64,256]{1,0:T(8,128)}, f32[768,256]{1,0:T(8,128)}, f32[256]{0:T(256)}, f32[256,256]{1,0:T(8,128)}, f32[256]{0:T(256)}, /*index=5*/f32[512,...) custom-call(bf16[232,256]{1,0:T(8,128)(2,1)S(1)} %get-tuple-element.118.refs_0_, ...), custom_call_target="tpu_custom_call" | custom-call | bytes 712704 | tf_op jit(solution)/shard_map/pallas_call | solution.py:601
  54.5 0.8 %collective-permute-done.16.refs_0_ = bf16[232,256]{1,0:T(8,128)(2,1)S(1)} collective-permute-done((bf16[232,256]{1,0:T(8,128)(2,1)S(1)}, bf16[232,256]{1,0:T(8,128)(2,1)S(1)}, u32[]{:S(2)}, u32[]{:S(2)}) %collective-permute-start.16) | collective-permute-done | bytes 118816 | tf_op jit(solution)/shard_map/ppermute | solution.py:126
  55.3 0.3 collective-permute-start.20
  55.6 0.8 %shard_map.249 = (f32[768,256]{1,0:T(8,128)}, f32[256]{0:T(256)}, f32[256,256]{1,0:T(8,128)}, f32[256]{0:T(256)}, f32[512,256]{1,0:T(8,128)}, /*index=5*/f32[256]{0:T(256)}, f32[256,256]{1,0:T(8,128)}, f32[256]{0:T(256)}) custom-call(bf16[232,256]{1,0:T(8,128)(2,1)S(1)} %collective-permute, ...), custom_call_target="tpu_custom_call", output_to_operand_aliasing={{0}: (1, {}), {1}: (2, {}), {2}: (3, {}), {3}: (4, {}), {4}... | custom-call | bytes 356352 | tf_op jit(solution)/shard_map/pallas_call | solution.py:601
  56.4 0.0 collective-permute-done.15.refs_0_
  56.4 0.0 collective-permute-done.18.refs_1_
  56.4 0.7 %collective-permute-start.19 = (bf16[232,256]{1,0:T(8,128)(2,1)S(1)}, bf16[232,256]{1,0:T(8,128)(2,1)S(1)}, u32[]{:S(2)}, u32[]{:S(2)}) collective-permute-start(bf16[232,256]{1,0:T(8,128)(2,1)S(1)} %collective-permute-done.18.refs_1_), channel_id=1, source_target_pairs={{0,2},{1,3},{2,0},{3,1},{4,6},{5,7},{6,4},{7,5},{8,10},{9,11},{10,... | collective-permute-start | bytes 356360 | tf_op jit(solution)/shard_map/ppermute | solution.py:126
  57.1 0.0 collective-permute-start.17
  57.1 0.0 collective-permute-done.20.refs_2_
  57.1 1.0 %shard_map.250 = (f32[768,256]{1,0:T(8,128)}, f32[256]{0:T(256)}, f32[256,256]{1,0:T(8,128)}, f32[256]{0:T(256)}, f32[512,256]{1,0:T(8,128)}, /*index=5*/f32[256]{0:T(256)}, f32[256,256]{1,0:T(8,128)}, f32[256]{0:T(256)}) custom-call(bf16[232,256]{1,0:T(8,128)(2,1)S(1)} %collective-permute, ...), custom_call_target="tpu_custom_call", output_to_operand_aliasing={{0}: (3, {}), {1}: (4, {}), {2}: (5, {}), {3}: (6, {}), {4}... | custom-call | bytes 1069056 | tf_op jit(solution)/shard_map/pallas_call | solution.py:601
  58.1 0.0 collective-permute-done.19.refs_1_
  58.1 0.3 collective-permute-done.17.refs_0_
  58.4 0.9 %shard_map.251 = (f32[768,256]{1,0:T(8,128)}, f32[256]{0:T(256)}, f32[256,256]{1,0:T(8,128)}, f32[256]{0:T(256)}, f32[512,256]{1,0:T(8,128)}, /*index=5*/f32[256]{0:T(256)}, f32[256,256]{1,0:T(8,128)}, f32[256]{0:T(256)}) custom-call(bf16[232,256]{1,0:T(8,128)(2,1)S(1)} %collective-permute, ...), custom_call_target="tpu_custom_call", output_to_operand_aliasing={{0}: (2, {}), {1}: (3, {}), {2}: (4, {}), {3}: (5, {}), {4}... | custom-call | bytes 712704 | tf_op jit(solution)/shard_map/pallas_call | solution.py:601
  (25 shorter events, 0.1 us)
Async XLA Ops:
  0.6 5.2 %copy-start.6 = (bf16[64,256]{1,0:T(8,128)(2,1)S(1)}, bf16[64,256]{1,0:T(8,128)(2,1)}, u32[]{:S(2)}) copy-start(bf16[64,256]{1,0:T(8,128)(2,1)} %refs_0_.1) | copy-start | bytes 98308
  0.7 5.2 %copy-start.7 = (s32[1,32]{1,0:T(1,128)S(1)}, s32[1,32]{1,0:T(1,128)}, u32[]{:S(2)}) copy-start(s32[1,32]{1,0:T(1,128)} %refs_4_.1) | copy-start | bytes 388
  0.7 5.1 %collective-permute-start = (bf16[64,256]{1,0:T(8,128)(2,1)}, bf16[64,256]{1,0:T(8,128)(2,1)S(1)}, u32[]{:S(2)}, u32[]{:S(2)}) collective-permute-start(bf16[64,256]{1,0:T(8,128)(2,1)} %refs_0_.1), channel_id=1, source_target_pairs={{0,1},{1,0},{2,3},{3,2},{4,5},{5,4},{6,7},{7,6},{8,9},{9,8},{10,11... | collective-permute-start | bytes 98312 | tf_op jit(solution)/shard_map/ppermute | solution.py:126
  5.8 5.4 %copy-start.10 = (s32[1024]{0:T(1024)S(1)}, s32[1024]{0:T(1024)}, u32[]{:S(2)}) copy-start(s32[1024]{0:T(1024)} %param.22) | copy-start | bytes 12292
  5.8 5.4 %copy-start.14 = (f32[256]{0:T(256)S(1)}, f32[256]{0:T(256)}, u32[]{:S(2)}) copy-start(f32[256]{0:T(256)} %nb2_ref.1) | copy-start | bytes 3076
  5.8 5.4 %copy-start.16 = (s32[64]{0:T(128)S(1)}, s32[64]{0:T(128)}, u32[]{:S(2)}) copy-start(s32[64]{0:T(128)} %sea_ref.1) | copy-start | bytes 772
  6.0 5.3 %copy-start.9 = (s32[1024]{0:T(1024)S(1)}, s32[1024]{0:T(1024)}, u32[]{:S(2)}) copy-start(s32[1024]{0:T(1024)} %param.21) | copy-start | bytes 12292
  6.0 9.1 %collective-permute-start.2 = (bf16[32,256]{1,0:T(8,128)(2,1)S(1)}, bf16[32,256]{1,0:T(8,128)(2,1)S(1)}, u32[]{:S(2)}, u32[]{:S(2)}) collective-permute-start(bf16[32,256]{1,0:T(8,128)(2,1)S(1)} %get-tuple-element.98), channel_id=1, source_target_pairs={{0,2},{1,3},{2,0},{3,1},{4,6},{5,7},{6,4},{7,5},{8,10},{9,11},{10,... | collective-permute-start | bytes 49160 | tf_op jit(solution)/shard_map/ppermute | solution.py:126
  6.0 9.1 %collective-permute-start.1 = (bf16[32,256]{1,0:T(8,128)(2,1)S(1)}, bf16[32,256]{1,0:T(8,128)(2,1)S(1)}, u32[]{:S(2)}, u32[]{:S(2)}) collective-permute-start(bf16[32,256]{1,0:T(8,128)(2,1)S(1)} %get-tuple-element.98), channel_id=1, source_target_pairs={{0,30},{1,31},{2,4},{3,5},{4,2},{5,3},{6,8},{7,9},{8,6},{9,7},{10,... | collective-permute-start | bytes 49160 | tf_op jit(solution)/shard_map/ppermute | solution.py:126
  11.2 0.7 %copy-start.12 = (f32[256]{0:T(256)S(1)}, f32[256]{0:T(256)}, u32[]{:S(2)}) copy-start(f32[256]{0:T(256)} %b2_ref.1) | copy-start | bytes 3076
  11.2 0.7 %copy-start.13 = (f32[256]{0:T(256)S(1)}, f32[256]{0:T(256)}, u32[]{:S(2)}) copy-start(f32[256]{0:T(256)} %nb1_ref.1) | copy-start | bytes 3076
  11.2 0.7 %copy-start.11 = (f32[256]{0:T(256)S(1)}, f32[256]{0:T(256)}, u32[]{:S(2)}) copy-start(f32[256]{0:T(256)} %b1_ref.1) | copy-start | bytes 3076
  11.2 0.7 %copy-start.15 = (s32[16]{0:T(128)S(1)}, s32[16]{0:T(128)}, u32[]{:S(2)}) copy-start(s32[16]{0:T(128)} %be_ref.1) | copy-start | bytes 196
  11.9 1.0 %copy-start = (bf16[768,256]{1,0:T(8,128)(2,1)S(1)}, bf16[768,256]{1,0:T(8,128)(2,1)}, u32[]{:S(2)}) copy-start(bf16[768,256]{1,0:T(8,128)(2,1)} %w1_ref.3) | copy-start | bytes 1179652
  12.9 1.0 %copy-start.8 = (bf16[1024,256]{1,0:T(8,128)(2,1)S(1)}, bf16[1024,256]{1,0:T(8,128)(2,1)}, u32[]{:S(2)}) copy-start(bf16[1024,256]{1,0:T(8,128)(2,1)} %e_ref.1) | copy-start | bytes 1572868
  14.0 1.2 %copy-start.1 = (bf16[256,256]{1,0:T(8,128)(2,1)S(1)}, bf16[256,256]{1,0:T(8,128)(2,1)}, u32[]{:S(2)}) copy-start(bf16[256,256]{1,0:T(8,128)(2,1)} %w2_ref.3) | copy-start | bytes 393220
  14.0 1.2 %copy-start.4 = (bf16[64,256]{1,0:T(8,128)(2,1)S(1)}, bf16[64,256]{1,0:T(8,128)(2,1)}, u32[]{:S(2)}) copy-start(bf16[64,256]{1,0:T(8,128)(2,1)} %refs_5_.1) | copy-start | bytes 98308
  15.1 5.9 %copy-start.2 = (bf16[1024,256]{1,0:T(8,128)(2,1)S(1)}, bf16[1024,256]{1,0:T(8,128)(2,1)}, u32[]{:S(2)}) copy-start(bf16[1024,256]{1,0:T(8,128)(2,1)} %geo_ref.1) | copy-start | bytes 1572868
  15.2 5.9 %copy-start.3 = (bf16[512,256]{1,0:T(8,128)(2,1)S(1)}, bf16[512,256]{1,0:T(8,128)(2,1)}, u32[]{:S(2)}) copy-start(bf16[512,256]{1,0:T(8,128)(2,1)} %nw1_ref.1) | copy-start | bytes 786436
  15.2 5.9 %copy-start.5 = (bf16[256,256]{1,0:T(8,128)(2,1)S(1)}, bf16[256,256]{1,0:T(8,128)(2,1)}, u32[]{:S(2)}) copy-start(bf16[256,256]{1,0:T(8,128)(2,1)} %nw2_ref.1) | copy-start | bytes 393220
  16.4 4.7 %collective-permute-start.3 = (bf16[192,256]{1,0:T(8,128)(2,1)S(1)}, bf16[192,256]{1,0:T(8,128)(2,1)S(1)}, u32[]{:S(2)}, u32[]{:S(2)}) collective-permute-start(bf16[192,256]{1,0:T(8,128)(2,1)S(1)} %get-tuple-element.108.refs_0_), channel_id=1, source_target_pairs={{0,1},{1,0},{2,3},{3,2},{4,5},{5,4},{6,7},{7,6},{8,9},{9,8},{10,11... | collective-permute-start | bytes 294920 | tf_op jit(solution)/shard_map/ppermute | solution.py:126
  24.3 1.9 %collective-permute-start.4 = (bf16[928,256]{1,0:T(8,128)(2,1)S(1)}, bf16[928,256]{1,0:T(8,128)(2,1)S(1)}, u32[]{:S(2)}, u32[]{:S(2)}) collective-permute-start(bf16[928,256]{1,0:T(8,128)(2,1)S(1)} %get-tuple-element.110), channel_id=1, source_target_pairs={{0,2},{1,3},{2,0},{3,1},{4,6},{5,7},{6,4},{7,5},{8,10},{9,11},{10,... | collective-permute-start | bytes 1425416 | tf_op jit(solution)/shard_map/ppermute | solution.py:126
  26.3 4.9 %collective-permute-start.5 = (bf16[232,256]{1,0:T(8,128)(2,1)S(1)}, bf16[232,256]{1,0:T(8,128)(2,1)S(1)}, u32[]{:S(2)}, u32[]{:S(2)}) collective-permute-start(bf16[232,256]{1,0:T(8,128)(2,1)S(1)} %get-tuple-element.112), channel_id=1, source_target_pairs={{0,1},{1,0},{2,10},{3,11},{4,5},{5,4},{6,14},{7,15},{8,9},{9,8},{1... | collective-permute-start | bytes 356360 | tf_op jit(solution)/shard_map/ppermute | solution.py:126
  27.9 6.1 %collective-permute-start.6 = (bf16[232,256]{1,0:T(8,128)(2,1)S(1)}, bf16[232,256]{1,0:T(8,128)(2,1)S(1)}, u32[]{:S(2)}, u32[]{:S(2)}) collective-permute-start(bf16[232,256]{1,0:T(8,128)(2,1)S(1)} %get-tuple-element.113), channel_id=1, source_target_pairs={{0,4},{1,5},{2,18},{3,19},{4,0},{5,1},{6,22},{7,23},{8,12},{9,13},... | collective-permute-start | bytes 356360 | tf_op jit(solution)/shard_map/ppermute | solution.py:126
  27.9 6.1 %collective-permute-start.7 = (bf16[232,256]{1,0:T(8,128)(2,1)S(1)}, bf16[232,256]{1,0:T(8,128)(2,1)S(1)}, u32[]{:S(2)}, u32[]{:S(2)}) collective-permute-start(bf16[232,256]{1,0:T(8,128)(2,1)S(1)} %get-tuple-element.114), channel_id=1, source_target_pairs={{0,5},{1,4},{2,26},{3,27},{4,1},{5,0},{6,30},{7,31},{8,13},{9,12},... | collective-permute-start | bytes 356360 | tf_op jit(solution)/shard_map/ppermute | solution.py:126
  34.1 15.0 %collective-permute-start.10 = (bf16[232,256]{1,0:T(8,128)(2,1)S(1)}, bf16[232,256]{1,0:T(8,128)(2,1)S(1)}, u32[]{:S(2)}, u32[]{:S(2)}) collective-permute-start(bf16[232,256]{1,0:T(8,128)(2,1)S(1)} %shard_map.245.refs_0_), channel_id=1, source_target_pairs={{0,24},{1,25},{2,7},{3,6},{4,28},{5,29},{6,3},{7,2},{8,16},{9,17},... | collective-permute-start | bytes 356360 | tf_op jit(solution)/shard_map/ppermute | solution.py:126
  35.3 13.8 %collective-permute-start.9 = (bf16[232,256]{1,0:T(8,128)(2,1)S(1)}, bf16[232,256]{1,0:T(8,128)(2,1)S(1)}, u32[]{:S(2)}, u32[]{:S(2)}) collective-permute-start(bf16[232,256]{1,0:T(8,128)(2,1)S(1)} %shard_map.245.refs_0_), channel_id=1, source_target_pairs={{0,16},{1,17},{2,6},{3,7},{4,20},{5,21},{6,2},{7,3},{8,24},{9,25},... | collective-permute-start | bytes 356360 | tf_op jit(solution)/shard_map/ppermute | solution.py:126
  35.3 13.8 %collective-permute-start.8 = (bf16[232,256]{1,0:T(8,128)(2,1)S(1)}, bf16[232,256]{1,0:T(8,128)(2,1)S(1)}, u32[]{:S(2)}, u32[]{:S(2)}) collective-permute-start(bf16[232,256]{1,0:T(8,128)(2,1)S(1)} %shard_map.245.refs_0_), channel_id=1, source_target_pairs={{0,8},{1,9},{2,3},{3,2},{4,12},{5,13},{6,7},{7,6},{8,0},{9,1},{10,... | collective-permute-start | bytes 356360 | tf_op jit(solution)/shard_map/ppermute | solution.py:126
  38.5 4.6 %collective-permute-start.11 = (bf16[192,256]{1,0:T(8,128)(2,1)S(1)}, bf16[192,256]{1,0:T(8,128)(2,1)S(1)}, u32[]{:S(2)}, u32[]{:S(2)}) collective-permute-start(bf16[192,256]{1,0:T(8,128)(2,1)S(1)} %get-tuple-element.115.refs_0_), channel_id=1, source_target_pairs={{0,1},{1,0},{2,3},{3,2},{4,5},{5,4},{6,7},{7,6},{8,9},{9,8},{10,11... | collective-permute-start | bytes 294920 | tf_op jit(solution)/shard_map/ppermute | solution.py:126
  43.2 5.9 %collective-permute-start.12 = (bf16[32,256]{1,0:T(8,128)(2,1)S(1)}, bf16[32,256]{1,0:T(8,128)(2,1)S(1)}, u32[]{:S(2)}, u32[]{:S(2)}) collective-permute-start(bf16[32,256]{1,0:T(8,128)(2,1)S(1)} %get-tuple-element.116), channel_id=1, source_target_pairs={{0,30},{1,31},{2,4},{3,5},{4,2},{5,3},{6,8},{7,9},{8,6},{9,7},{10,... | collective-permute-start | bytes 49160 | tf_op jit(solution)/shard_map/ppermute | solution.py:126
  43.2 5.9 %collective-permute-start.13 = (bf16[32,256]{1,0:T(8,128)(2,1)S(1)}, bf16[32,256]{1,0:T(8,128)(2,1)S(1)}, u32[]{:S(2)}, u32[]{:S(2)}) collective-permute-start(bf16[32,256]{1,0:T(8,128)(2,1)S(1)} %get-tuple-element.117), channel_id=1, source_target_pairs={{0,2},{1,3},{2,0},{3,1},{4,6},{5,7},{6,4},{7,5},{8,10},{9,11},{10,... | collective-permute-start | bytes 49160 | tf_op jit(solution)/shard_map/ppermute | solution.py:126
  49.4 3.6 %collective-permute-start.14 = (bf16[232,256]{1,0:T(8,128)(2,1)S(1)}, bf16[232,256]{1,0:T(8,128)(2,1)S(1)}, u32[]{:S(2)}, u32[]{:S(2)}) collective-permute-start(bf16[232,256]{1,0:T(8,128)(2,1)S(1)} %get-tuple-element.118.refs_0_), channel_id=1, source_target_pairs={{0,2},{1,3},{2,0},{3,1},{4,6},{5,7},{6,4},{7,5},{8,10},{9,11},{10,... | collective-permute-start | bytes 356360 | tf_op jit(solution)/shard_map/ppermute | solution.py:126
  49.4 5.9 %collective-permute-start.16 = (bf16[232,256]{1,0:T(8,128)(2,1)S(1)}, bf16[232,256]{1,0:T(8,128)(2,1)S(1)}, u32[]{:S(2)}, u32[]{:S(2)}) collective-permute-start(bf16[232,256]{1,0:T(8,128)(2,1)S(1)} %get-tuple-element.118.refs_0_), channel_id=1, source_target_pairs={{0,5},{1,4},{2,26},{3,27},{4,1},{5,0},{6,30},{7,31},{8,13},{9,12},... | collective-permute-start | bytes 356360 | tf_op jit(solution)/shard_map/ppermute | solution.py:126
  49.5 6.9 %collective-permute-start.15 = (bf16[232,256]{1,0:T(8,128)(2,1)S(1)}, bf16[232,256]{1,0:T(8,128)(2,1)S(1)}, u32[]{:S(2)}, u32[]{:S(2)}) collective-permute-start(bf16[232,256]{1,0:T(8,128)(2,1)S(1)} %get-tuple-element.118.refs_0_), channel_id=1, source_target_pairs={{0,4},{1,5},{2,18},{3,19},{4,0},{5,1},{6,22},{7,23},{8,12},{9,13},... | collective-permute-start | bytes 356360 | tf_op jit(solution)/shard_map/ppermute | solution.py:126
  51.5 4.9 %collective-permute-start.18 = (bf16[232,256]{1,0:T(8,128)(2,1)S(1)}, bf16[232,256]{1,0:T(8,128)(2,1)S(1)}, u32[]{:S(2)}, u32[]{:S(2)}) collective-permute-start(bf16[232,256]{1,0:T(8,128)(2,1)S(1)} %get-tuple-element.118.refs_0_), channel_id=1, source_target_pairs={{0,1},{1,0},{2,10},{3,11},{4,5},{5,4},{6,14},{7,15},{8,9},{9,8},{1... | collective-permute-start | bytes 356360 | tf_op jit(solution)/shard_map/ppermute | solution.py:126
  55.3 1.7 %collective-permute-start.20 = (bf16[232,256]{1,0:T(8,128)(2,1)S(1)}, bf16[232,256]{1,0:T(8,128)(2,1)S(1)}, u32[]{:S(2)}, u32[]{:S(2)}) collective-permute-start(bf16[232,256]{1,0:T(8,128)(2,1)S(1)} %collective-permute-done.16.refs_0_), channel_id=1, source_target_pairs={{0,2},{1,3},{2,0},{3,1},{4,6},{5,7},{6,4},{7,5},{8,10},{9,11},{10,... | collective-permute-start | bytes 356360 | tf_op jit(solution)/shard_map/ppermute | solution.py:126
  56.4 1.7 %collective-permute-start.19 = (bf16[232,256]{1,0:T(8,128)(2,1)S(1)}, bf16[232,256]{1,0:T(8,128)(2,1)S(1)}, u32[]{:S(2)}, u32[]{:S(2)}) collective-permute-start(bf16[232,256]{1,0:T(8,128)(2,1)S(1)} %collective-permute-done.18.refs_1_), channel_id=1, source_target_pairs={{0,2},{1,3},{2,0},{3,1},{4,6},{5,7},{6,4},{7,5},{8,10},{9,11},{10,... | collective-permute-start | bytes 356360 | tf_op jit(solution)/shard_map/ppermute | solution.py:126
  57.1 1.3 %collective-permute-start.17 = (bf16[232,256]{1,0:T(8,128)(2,1)S(1)}, bf16[232,256]{1,0:T(8,128)(2,1)S(1)}, u32[]{:S(2)}, u32[]{:S(2)}) collective-permute-start(bf16[232,256]{1,0:T(8,128)(2,1)S(1)} %collective-permute-done.15.refs_0_), channel_id=1, source_target_pairs={{0,2},{1,3},{2,0},{3,1},{4,6},{5,7},{6,4},{7,5},{8,10},{9,11},{10,... | collective-permute-start | bytes 356360 | tf_op jit(solution)/shard_map/ppermute | solution.py:126

commit v3 on v2

--- a/solution.py
+++ b/solution.py
@@ -250,6 +250,7 @@
         return jnp.concatenate(rows, axis=0)
 
     theirs = [groups.helper_swap(node_latent, k) for k in range(1, helpers)]
+    w1_send, w1_rest = edge_w1[:feat], edge_w1[feat:]
 
     def gather_kernel(halo_ref, *refs):
         parts, (band_ref, out_ref) = refs[:helpers], refs[helpers:]
@@ -272,8 +273,8 @@
         table[height + at : height + at + proj.shape[0], :] = (proj - high.astype(F32)).astype(BF)
 
     def local_kernel(
-        send_ref, recv_ref, band_ref, e_ref, w1_ref, b1_ref, b2_ref, nb1_ref, nb2_ref, be_ref,
-        sea_ref, pre_ref, place_ref, recv_pick_ref, halo_pick_ref, et_ref, bias_ref, live_ref,
+        send_ref, recv_ref, band_ref, e_ref, ws_ref, wr_ref, b1_ref, b2_ref, nb1_ref, nb2_ref,
+        be_ref, sea_ref, pre_ref, place_ref, recv_pick_ref, halo_pick_ref, et_ref, bias_ref, live_ref,
         sea_diag_ref, table,
     ):
         for i, ref in enumerate((b1_ref, b2_ref, nb1_ref, nb2_ref)):
@@ -292,8 +293,8 @@
         ).astype(BF)
         if b_width > 2 * band:
             table[...] = jnp.zeros_like(table)
-        for at, rows in ((0, slice(0, feat)), (band, slice(feat, 2 * feat))):
-            split_store(table, b_width, at, dot(band_ref[...], w1_ref[rows, :]))
+        for at, weights in ((0, ws_ref[...]), (band, wr_ref[:feat, :])):
+            split_store(table, b_width, at, dot(band_ref[...], weights))
         for i in range(edges // chunk):
             rows = pl.ds(i * chunk, chunk)
             send_cols = chunk_ids(send_ref, i)
@@ -307,7 +308,7 @@
             pick = onehot_rows([send_cols, recv_cols + band], b_width)
             pre = dot(jnp.concatenate([pick, pick], axis=1), table[...])
             e_rows = e_ref[rows, :]
-            pre_ref[rows, :] = pre + dot(e_rows, w1_ref[2 * feat :, :]) + b1_ref[...][None, :]
+            pre_ref[rows, :] = pre + dot(e_rows, wr_ref[feat:, :]) + b1_ref[...][None, :]
             et_ref[:, rows] = e_rows.T
 
     pre_local, place, recv_pick, halo_pick, edge_t, biases, live, sea_diag = call(
@@ -317,7 +318,7 @@
             sds(edges, h_width, BF), sds(feat, edges, BF), sds(4, feat, F32),
             sds(slots, feat, F32), sds(own, own, BF),
         ],
-        [send_ids, recv_ids, band_rows, edge_latent, edge_w1, edge_b1, edge_b2, node_b1, node_b2,
+        [send_ids, recv_ids, band_rows, edge_latent, w1_send, w1_rest, edge_b1, edge_b2, node_b1, node_b2,
          band_edges, sea_mask],
         scratch=[pltpu.VMEM((2 * b_width, feat), BF)],
         flops=4 * unit,
@@ -358,7 +359,7 @@
         forward_kernel,
         [sds(edges, feat, BF), sds(edges, feat, F32), sds(edges, feat, F32), sds(edges, 1, F32),
          sds(band, feat, F32), sds(band + own, feat, BF), sds(2 * halo, feat, BF)],
-        [live, pre_local, place, halo_pick, from_ring, from_core, edge_w1[:feat], edge_w2,
+        [live, pre_local, place, halo_pick, from_ring, from_core, w1_send, edge_w2,
          biases, grad_out_node, sea_diag],
         scratch=[pltpu.VMEM((2 * h_width, feat), BF)],
         flops=3 * unit,
@@ -368,7 +369,7 @@
 
     def backward_kernel(
         live_ref, place_ref, recv_pick_ref, band_ref, halo_ref, et_ref, geo_ref,
-        hid_ref, slope_ref, norm_ref, inv_ref, w1_ref, w2_ref, nw1_ref, nw2_ref, bias_ref,
+        hid_ref, slope_ref, norm_ref, inv_ref, ws_ref, wr_ref, w2_ref, nw1_ref, nw2_ref, bias_ref,
         agg_ref, *refs,
     ):
         parts = refs[:helpers]
@@ -405,7 +406,7 @@
         gb_n1 = jnp.sum(n_dpre, axis=0, keepdims=True) * node_share
         gb_n2 = jnp.sum(n_dz, axis=0, keepdims=True) * node_share
 
-        w1e = w1_ref[2 * feat :, :]
+        w1e = wr_ref[feat:, :]
         gb_1 = jnp.zeros((1, feat), F32)
         gb_2 = jnp.zeros((1, feat), F32)
         gw_1 = jnp.zeros((feat, feat), F32)
@@ -437,8 +438,8 @@
         at_send = sums[:look, :].astype(BF)
         at_recv = sums[look:, :].astype(BF)
         lookup = jnp.concatenate([band_v, halo_ref[...]], axis=0)
-        look_grad = dot_right_t(at_send, w1_ref[:feat, :])
-        recv_grad = dot_right_t(at_recv, w1_ref[feat : 2 * feat, :])
+        look_grad = dot_right_t(at_send, ws_ref[...])
+        recv_grad = dot_right_t(at_recv, wr_ref[:feat, :])
         lg_ref[:band, :] = (look_grad[:band, :] + recv_grad).astype(BF)
         lg_ref[band:, :] = look_grad[band:, :].astype(BF)
         put(0, 0, dot_left_t(lookup, at_send) * edge_scale)
@@ -461,7 +462,7 @@
         [sds(edges, feat, BF), sds(half, feat, F32), sds(half, feat, BF), sds(look, feat, BF),
          sds(band, feat, F32)],
         [live, place, recv_pick, band_rows, halo_rows, edge_t, grad_out_edge,
-         hidden, slope, normed, inv, edge_w1, edge_w2, node_w1, node_w2, biases, agg_own, *swaps],
+         hidden, slope, normed, inv, w1_send, w1_rest, edge_w2, node_w1, node_w2, biases, agg_own, *swaps],
         scratch=[pltpu.VMEM((half * groups.core, feat), F32), pltpu.VMEM((look + band, feat), F32),
                  pltpu.VMEM((band, feat), BF), pltpu.VMEM((edges, feat), BF),
                  pltpu.SemaphoreType.DMA((edges // wide,))],

time: 59.5 us -> 58.3 us (0.980)
  local copies, waits for them, and re-layouts: 3.67 us -> 2.59 us
  waiting for transfers between devices: 19.6 us -> 19 us
    unnamed x34 -> x32, local copies, waits for them, and re-layouts: 2.76 us -> 0.7 us
    slice x1 -> x2, local copies, waits for them, and re-layouts: 0.91 us -> 1.89 us  [on_device(): w1_send, w1_rest = (edge_w1[:feat], edge_w1[feat:])]
  transfers between devices with their start and end apart: 21 -> 21, of which waited for: 9 -> 10; matrix products, arithmetic and copies ran while one was open for 2% -> 3% of each run, Pallas kernels for 7% -> 8%
where the time goes in v3:
time: 58.3 us; the launch traced here: 58.1 us
  starting transfers between devices  25.3 us (43%)
  waiting for transfers between devices  19 us (33%)
  Pallas kernels  10.3 us (18%)
  local copies, waits for them, and re-layouts  2.59 us (4%)
  between operations  0.94 us (2%)
    ppermute x21, starting transfers between devices, permute(): return lax.ppermute(array, AXES, pairs)  25.3 us
    ppermute x21, waiting for transfers between devices, permute(): return lax.ppermute(array, AXES, pairs)  19 us
    pallas_call x8, Pallas kernels, call(): pl.pallas_call(kernel, out_shape=out_shape, in_specs=in_specs, out_specs=...  6.13 us
    pallas_call x4, Pallas kernels, place_call(): pl.pallas_call(kernel, out_shape=node_out + out_shape, in_specs=[vmem] *...  4.15 us
    slice x2, local copies, waits for them, and re-layouts, on_device(): w1_send, w1_rest = (edge_w1[:feat], edge_w1[feat:])  1.89 us
  transfers between devices with their start and end apart: 21, of which 10 were waited for; matrix products, arithmetic and copies ran while one was open for 3% of the time, Pallas kernels for 8%

profile of v3, /device:TPU:0, one launch (start us, length us, event | category | flops | bytes accessed | tf_op | source)
XLA Modules:
  0.0 58.1 jit_solution(13350290674460521925)
XLA Ops:
  0.7 3.0 %collective-permute-start = (bf16[64,256]{1,0:T(8,128)(2,1)}, bf16[64,256]{1,0:T(8,128)(2,1)S(1)}, u32[]{:S(2)}, u32[]{:S(2)}) collective-permute-start(bf16[64,256]{1,0:T(8,128)(2,1)} %refs_0_.1), channel_id=1, source_target_pairs={{0,1},{1,0},{2,3},{3,2},{4,5},{5,4},{6,7},{7,6},{8,9},{9,8},{10,11... | collective-permute-start | bytes 98312 | tf_op jit(solution)/shard_map/ppermute | solution.py:126
  3.7 0.9 %slice.6.ws_ref.w1_ref = bf16[256,256]{1,0:T(8,128)(2,1)S(1)} slice(bf16[768,256]{1,0:T(8,128)(2,1)} %param.26), slice={[0:256], [0:256]} | slice | bytes 262144 | tf_op jit(solution)/shard_map/slice | solution.py:253
  4.6 0.0 copy-start.5
  4.6 0.0 copy-start.6
  4.6 1.0 %slice.7.wr_ref = bf16[512,256]{1,0:T(8,128)(2,1)S(1)} slice(bf16[768,256]{1,0:T(8,128)(2,1)} %param.26), slice={[256:768], [0:256]} | slice | bytes 524288 | tf_op jit(solution)/shard_map/slice | solution.py:253
  5.6 0.2 collective-permute-done.refs_1_
  5.8 0.0 copy-start.12
  5.8 0.0 copy-start.13
  5.8 0.0 copy-start.15
  5.8 0.2 shard_map.240
  6.0 0.0 collective-permute-start.2
  6.0 5.2 %collective-permute-start.1 = (bf16[32,256]{1,0:T(8,128)(2,1)S(1)}, bf16[32,256]{1,0:T(8,128)(2,1)S(1)}, u32[]{:S(2)}, u32[]{:S(2)}) collective-permute-start(bf16[32,256]{1,0:T(8,128)(2,1)S(1)} %get-tuple-element.98), channel_id=1, source_target_pairs={{0,30},{1,31},{2,4},{3,5},{4,2},{5,3},{6,8},{7,9},{8,6},{9,7},{10,... | collective-permute-start | bytes 49160 | tf_op jit(solution)/shard_map/ppermute | solution.py:126
  11.3 0.6 %copy-done.10 = f32[256]{0:T(256)S(1)} copy-done((f32[256]{0:T(256)S(1)}, f32[256]{0:T(256)}, u32[]{:S(2)}) %copy-start.10) | copy-done | bytes 1048
  11.9 1.1 %shard_map.241 = (f32[1024,256]{1,0:T(8,128)S(1)}, bf16[320,1024]{1,0:T(8,128)(2,1)S(1)}, bf16[1024,128]{1,0:T(8,128)(2,1)S(1)}, bf16[1024,128]{1,0:T(8,128)(2,1...) custom-call(s32[8,128]{1,0:T(8,128)S(1)} %bitcast.2, ...), custom_call_target="tpu_custom_call" | custom-call | flops 536870912 | bytes 3768640 | tf_op jit(solution)/shard_map/pallas_call | solution.py:84
  13.0 0.0 collective-permute-done.2.core_ref
  13.0 0.0 collective-permute-done.1.ring_ref
  13.1 0.0 copy-start.1
  13.1 0.0 copy-start.2
  13.1 0.0 copy-start.4
  13.1 1.2 %shard_map.242 = (bf16[1024,256]{1,0:T(8,128)(2,1)S(1)}, f32[1024,256]{1,0:T(8,128)S(1)}, f32[1024,256]{1,0:T(8,128)S(1)}, f32[1024,1]{1,0:T(8,128)S(1)}, f32[12...) custom-call(f32[8,256]{1,0:T(8,128)S(1)} %get-tuple-element.93.live_ref, ...), custom_call_target="tpu_custom_call" | custom-call | flops 402653184 | bytes 5201920 | tf_op jit(solution)/shard_map/pallas_call | solution.py:84
  14.3 1.6 %collective-permute-start.3 = (bf16[192,256]{1,0:T(8,128)(2,1)S(1)}, bf16[192,256]{1,0:T(8,128)(2,1)S(1)}, u32[]{:S(2)}, u32[]{:S(2)}) collective-permute-start(bf16[192,256]{1,0:T(8,128)(2,1)S(1)} %get-tuple-element.108.refs_0_), channel_id=1, source_target_pairs={{0,1},{1,0},{2,3},{3,2},{4,5},{5,4},{6,7},{7,6},{8,9},{9,8},{10,11... | collective-permute-start | bytes 294920 | tf_op jit(solution)/shard_map/ppermute | solution.py:126
  15.9 3.1 %collective-permute-done.3.refs_1_ = bf16[192,256]{1,0:T(8,128)(2,1)S(1)} collective-permute-done((bf16[192,256]{1,0:T(8,128)(2,1)S(1)}, bf16[192,256]{1,0:T(8,128)(2,1)S(1)}, u32[]{:S(2)}, u32[]{:S(2)}) %collective-permute-start.3) | collective-permute-done | bytes 98336 | tf_op jit(solution)/shard_map/ppermute | solution.py:126
  19.0 3.2 %shard_map.243 = (bf16[1024,256]{1,0:T(8,128)(2,1)}, f32[928,256]{1,0:T(8,128)S(1)}, bf16[928,256]{1,0:T(8,128)(2,1)S(1)}, bf16[192,256]{1,0:T(8,128)(2,1)S(1)}, f32[128,256]{1,0:T(8,128)S(1)}) custom-call(f32[8,256]{1,0:T(8,128)S(1)} %get-tuple-element.93.live_ref, bf16[320,1024]{1,0:T(8,128)(2,1)S(1)} %get-tuple-element.94.place_ref, ...), custom_call_target="tpu_custom_call" | custom-call | flops 1073741824 | bytes 8126464 | tf_op jit(solution)/shard_map/pallas_call | solution.py:84
  22.2 0.1 collective-permute-start.4
  22.3 1.8 %collective-permute-done.4.got_ref = bf16[928,256]{1,0:T(8,128)(2,1)S(1)} collective-permute-done((bf16[928,256]{1,0:T(8,128)(2,1)S(1)}, bf16[928,256]{1,0:T(8,128)(2,1)S(1)}, u32[]{:S(2)}, u32[]{:S(2)}) %collective-permute-start.4) | collective-permute-done | bytes 475168 | tf_op jit(solution)/shard_map/ppermute | solution.py:126
  24.1 0.2 shard_map.244
  24.3 1.6 %collective-permute-start.5 = (bf16[232,256]{1,0:T(8,128)(2,1)S(1)}, bf16[232,256]{1,0:T(8,128)(2,1)S(1)}, u32[]{:S(2)}, u32[]{:S(2)}) collective-permute-start(bf16[232,256]{1,0:T(8,128)(2,1)S(1)} %get-tuple-element.112), channel_id=1, source_target_pairs={{0,1},{1,0},{2,10},{3,11},{4,5},{5,4},{6,14},{7,15},{8,9},{9,8},{1... | collective-permute-start | bytes 356360 | tf_op jit(solution)/shard_map/ppermute | solution.py:126
  25.8 0.0 collective-permute-start.6
  25.8 2.0 %collective-permute-start.7 = (bf16[232,256]{1,0:T(8,128)(2,1)S(1)}, bf16[232,256]{1,0:T(8,128)(2,1)S(1)}, u32[]{:S(2)}, u32[]{:S(2)}) collective-permute-start(bf16[232,256]{1,0:T(8,128)(2,1)S(1)} %get-tuple-element.114), channel_id=1, source_target_pairs={{0,5},{1,4},{2,26},{3,27},{4,1},{5,0},{6,30},{7,31},{8,13},{9,12},... | collective-permute-start | bytes 356360 | tf_op jit(solution)/shard_map/ppermute | solution.py:126
  27.8 1.3 %collective-permute-done.5.refs_0_ = bf16[232,256]{1,0:T(8,128)(2,1)S(1)} collective-permute-done((bf16[232,256]{1,0:T(8,128)(2,1)S(1)}, bf16[232,256]{1,0:T(8,128)(2,1)S(1)}, u32[]{:S(2)}, u32[]{:S(2)}) %collective-permute-start.5) | collective-permute-done | bytes 118816 | tf_op jit(solution)/shard_map/ppermute | solution.py:126
  29.2 2.8 %collective-permute-done.6.refs_1_ = bf16[232,256]{1,0:T(8,128)(2,1)S(1)} collective-permute-done((bf16[232,256]{1,0:T(8,128)(2,1)S(1)}, bf16[232,256]{1,0:T(8,128)(2,1)S(1)}, u32[]{:S(2)}, u32[]{:S(2)}) %collective-permute-start.6) | collective-permute-done | bytes 118816 | tf_op jit(solution)/shard_map/ppermute | solution.py:126
  31.9 0.0 collective-permute-done.7.refs_2_
  31.9 0.1 shard_map.245.refs_0_
  32.0 3.1 %collective-permute-start.10 = (bf16[232,256]{1,0:T(8,128)(2,1)S(1)}, bf16[232,256]{1,0:T(8,128)(2,1)S(1)}, u32[]{:S(2)}, u32[]{:S(2)}) collective-permute-start(bf16[232,256]{1,0:T(8,128)(2,1)S(1)} %shard_map.245.refs_0_), channel_id=1, source_target_pairs={{0,24},{1,25},{2,7},{3,6},{4,28},{5,29},{6,3},{7,2},{8,16},{9,17},... | collective-permute-start | bytes 356360 | tf_op jit(solution)/shard_map/ppermute | solution.py:126
  35.1 0.0 collective-permute-start.9
  35.1 1.3 %collective-permute-start.8 = (bf16[232,256]{1,0:T(8,128)(2,1)S(1)}, bf16[232,256]{1,0:T(8,128)(2,1)S(1)}, u32[]{:S(2)}, u32[]{:S(2)}) collective-permute-start(bf16[232,256]{1,0:T(8,128)(2,1)S(1)} %shard_map.245.refs_0_), channel_id=1, source_target_pairs={{0,8},{1,9},{2,3},{3,2},{4,12},{5,13},{6,7},{7,6},{8,0},{9,1},{10,... | collective-permute-start | bytes 356360 | tf_op jit(solution)/shard_map/ppermute | solution.py:126
  36.4 0.5 collective-permute-start.11
  37.0 4.1 %collective-permute-done.11.refs_1_ = bf16[192,256]{1,0:T(8,128)(2,1)S(1)} collective-permute-done((bf16[192,256]{1,0:T(8,128)(2,1)S(1)}, bf16[192,256]{1,0:T(8,128)(2,1)S(1)}, u32[]{:S(2)}, u32[]{:S(2)}) %collective-permute-start.11) | collective-permute-done | bytes 98336 | tf_op jit(solution)/shard_map/ppermute | solution.py:126
  41.1 1.0 %collective-permute-start.12 = (bf16[32,256]{1,0:T(8,128)(2,1)S(1)}, bf16[32,256]{1,0:T(8,128)(2,1)S(1)}, u32[]{:S(2)}, u32[]{:S(2)}) collective-permute-start(bf16[32,256]{1,0:T(8,128)(2,1)S(1)} %get-tuple-element.116), channel_id=1, source_target_pairs={{0,30},{1,31},{2,4},{3,5},{4,2},{5,3},{6,8},{7,9},{8,6},{9,7},{10,... | collective-permute-start | bytes 49160 | tf_op jit(solution)/shard_map/ppermute | solution.py:126
  42.1 0.8 %collective-permute-start.13 = (bf16[32,256]{1,0:T(8,128)(2,1)S(1)}, bf16[32,256]{1,0:T(8,128)(2,1)S(1)}, u32[]{:S(2)}, u32[]{:S(2)}) collective-permute-start(bf16[32,256]{1,0:T(8,128)(2,1)S(1)} %get-tuple-element.117), channel_id=1, source_target_pairs={{0,2},{1,3},{2,0},{3,1},{4,6},{5,7},{6,4},{7,5},{8,10},{9,11},{10,... | collective-permute-start | bytes 49160 | tf_op jit(solution)/shard_map/ppermute | solution.py:126
  42.9 4.1 %collective-permute-done.12.refs_5_ = bf16[32,256]{1,0:T(8,128)(2,1)S(1)} collective-permute-done((bf16[32,256]{1,0:T(8,128)(2,1)S(1)}, bf16[32,256]{1,0:T(8,128)(2,1)S(1)}, u32[]{:S(2)}, u32[]{:S(2)}) %collective-permute-start.12) | collective-permute-done | bytes 16416 | tf_op jit(solution)/shard_map/ppermute | solution.py:126
  47.0 0.0 collective-permute-done.13.refs_6_
  47.0 0.0 collective-permute-done.10.refs_3_
  47.0 0.0 collective-permute-done.9.refs_2_
  47.0 0.0 collective-permute-done.8.refs_1_
  47.0 0.2 shard_map.247
  47.3 0.1 collective-permute-start.14
  47.3 0.1 collective-permute-start.16
  47.4 2.5 %collective-permute-start.15 = (bf16[232,256]{1,0:T(8,128)(2,1)S(1)}, bf16[232,256]{1,0:T(8,128)(2,1)S(1)}, u32[]{:S(2)}, u32[]{:S(2)}) collective-permute-start(bf16[232,256]{1,0:T(8,128)(2,1)S(1)} %get-tuple-element.118.refs_0_), channel_id=1, source_target_pairs={{0,4},{1,5},{2,18},{3,19},{4,0},{5,1},{6,22},{7,23},{8,12},{9,13},... | collective-permute-start | bytes 356360 | tf_op jit(solution)/shard_map/ppermute | solution.py:126
  49.9 1.0 %collective-permute-start.18 = (bf16[232,256]{1,0:T(8,128)(2,1)S(1)}, bf16[232,256]{1,0:T(8,128)(2,1)S(1)}, u32[]{:S(2)}, u32[]{:S(2)}) collective-permute-start(bf16[232,256]{1,0:T(8,128)(2,1)S(1)} %get-tuple-element.118.refs_0_), channel_id=1, source_target_pairs={{0,1},{1,0},{2,10},{3,11},{4,5},{5,4},{6,14},{7,15},{8,9},{9,8},{1... | collective-permute-start | bytes 356360 | tf_op jit(solution)/shard_map/ppermute | solution.py:126
  50.9 0.0 collective-permute-done.14.refs_1_
  50.9 1.5 %shard_map.248 = (f32[64,256]{1,0:T(8,128)}, f32[768,256]{1,0:T(8,128)}, f32[256]{0:T(256)}, f32[256,256]{1,0:T(8,128)}, f32[256]{0:T(256)}, /*index=5*/f32[512,...) custom-call(bf16[232,256]{1,0:T(8,128)(2,1)S(1)} %get-tuple-element.118.refs_0_, ...), custom_call_target="tpu_custom_call" | custom-call | bytes 712704 | tf_op jit(solution)/shard_map/pallas_call | solution.py:602
  52.4 0.8 %collective-permute-done.16.refs_0_ = bf16[232,256]{1,0:T(8,128)(2,1)S(1)} collective-permute-done((bf16[232,256]{1,0:T(8,128)(2,1)S(1)}, bf16[232,256]{1,0:T(8,128)(2,1)S(1)}, u32[]{:S(2)}, u32[]{:S(2)}) %collective-permute-start.16) | collective-permute-done | bytes 118816 | tf_op jit(solution)/shard_map/ppermute | solution.py:126
  53.2 0.3 collective-permute-start.20
  53.5 0.8 %shard_map.249 = (f32[768,256]{1,0:T(8,128)}, f32[256]{0:T(256)}, f32[256,256]{1,0:T(8,128)}, f32[256]{0:T(256)}, f32[512,256]{1,0:T(8,128)}, /*index=5*/f32[256]{0:T(256)}, f32[256,256]{1,0:T(8,128)}, f32[256]{0:T(256)}) custom-call(bf16[232,256]{1,0:T(8,128)(2,1)S(1)} %collective-permute, ...), custom_call_target="tpu_custom_call", output_to_operand_aliasing={{0}: (1, {}), {1}: (2, {}), {2}: (3, {}), {3}: (4, {}), {4}... | custom-call | bytes 356352 | tf_op jit(solution)/shard_map/pallas_call | solution.py:602
  54.3 0.0 collective-permute-done.15.refs_0_
  54.3 0.4 collective-permute-done.18.refs_1_
  54.7 1.1 %collective-permute-start.19 = (bf16[232,256]{1,0:T(8,128)(2,1)S(1)}, bf16[232,256]{1,0:T(8,128)(2,1)S(1)}, u32[]{:S(2)}, u32[]{:S(2)}) collective-permute-start(bf16[232,256]{1,0:T(8,128)(2,1)S(1)} %collective-permute-done.18.refs_1_), channel_id=1, source_target_pairs={{0,2},{1,3},{2,0},{3,1},{4,6},{5,7},{6,4},{7,5},{8,10},{9,11},{10,... | collective-permute-start | bytes 356360 | tf_op jit(solution)/shard_map/ppermute | solution.py:126
  55.9 0.0 collective-permute-start.17
  55.9 0.0 collective-permute-done.20.refs_2_
  55.9 1.0 %shard_map.250 = (f32[768,256]{1,0:T(8,128)}, f32[256]{0:T(256)}, f32[256,256]{1,0:T(8,128)}, f32[256]{0:T(256)}, f32[512,256]{1,0:T(8,128)}, /*index=5*/f32[256]{0:T(256)}, f32[256,256]{1,0:T(8,128)}, f32[256]{0:T(256)}) custom-call(bf16[232,256]{1,0:T(8,128)(2,1)S(1)} %collective-permute, ...), custom_call_target="tpu_custom_call", output_to_operand_aliasing={{0}: (3, {}), {1}: (4, {}), {2}: (5, {}), {3}: (6, {}), {4}... | custom-call | bytes 1069056 | tf_op jit(solution)/shard_map/pallas_call | solution.py:602
  56.9 0.0 collective-permute-done.19.refs_1_
  56.9 0.3 collective-permute-done.17.refs_0_
  57.2 0.9 %shard_map.251 = (f32[768,256]{1,0:T(8,128)}, f32[256]{0:T(256)}, f32[256,256]{1,0:T(8,128)}, f32[256]{0:T(256)}, f32[512,256]{1,0:T(8,128)}, /*index=5*/f32[256]{0:T(256)}, f32[256,256]{1,0:T(8,128)}, f32[256]{0:T(256)}) custom-call(bf16[232,256]{1,0:T(8,128)(2,1)S(1)} %collective-permute, ...), custom_call_target="tpu_custom_call", output_to_operand_aliasing={{0}: (2, {}), {1}: (3, {}), {2}: (4, {}), {3}: (5, {}), {4}... | custom-call | bytes 712704 | tf_op jit(solution)/shard_map/pallas_call | solution.py:602
  (24 shorter events, 0.1 us)
Async XLA Ops:
  0.6 10.6 %copy-start.7 = (bf16[1024,256]{1,0:T(8,128)(2,1)S(1)}, bf16[1024,256]{1,0:T(8,128)(2,1)}, u32[]{:S(2)}) copy-start(bf16[1024,256]{1,0:T(8,128)(2,1)} %e_ref.1) | copy-start | bytes 1572868
  0.7 5.1 %collective-permute-start = (bf16[64,256]{1,0:T(8,128)(2,1)}, bf16[64,256]{1,0:T(8,128)(2,1)S(1)}, u32[]{:S(2)}, u32[]{:S(2)}) collective-permute-start(bf16[64,256]{1,0:T(8,128)(2,1)} %refs_0_.1), channel_id=1, source_target_pairs={{0,1},{1,0},{2,3},{3,2},{4,5},{5,4},{6,7},{7,6},{8,9},{9,8},{10,11... | collective-permute-start | bytes 98312 | tf_op jit(solution)/shard_map/ppermute | solution.py:126
  4.6 1.2 %copy-start.5 = (bf16[64,256]{1,0:T(8,128)(2,1)S(1)}, bf16[64,256]{1,0:T(8,128)(2,1)}, u32[]{:S(2)}) copy-start(bf16[64,256]{1,0:T(8,128)(2,1)} %refs_0_.1) | copy-start | bytes 98308
  4.6 1.2 %copy-start.6 = (s32[1,32]{1,0:T(1,128)S(1)}, s32[1,32]{1,0:T(1,128)}, u32[]{:S(2)}) copy-start(s32[1,32]{1,0:T(1,128)} %refs_4_.1) | copy-start | bytes 388
  5.8 5.4 %copy-start.9 = (s32[1024]{0:T(1024)S(1)}, s32[1024]{0:T(1024)}, u32[]{:S(2)}) copy-start(s32[1024]{0:T(1024)} %param.22) | copy-start | bytes 12292
  5.8 5.4 %copy-start.11 = (f32[256]{0:T(256)S(1)}, f32[256]{0:T(256)}, u32[]{:S(2)}) copy-start(f32[256]{0:T(256)} %b2_ref.1) | copy-start | bytes 3076
  5.8 5.4 %copy-start.12 = (f32[256]{0:T(256)S(1)}, f32[256]{0:T(256)}, u32[]{:S(2)}) copy-start(f32[256]{0:T(256)} %nb1_ref.1) | copy-start | bytes 3076
  5.8 5.4 %copy-start.13 = (f32[256]{0:T(256)S(1)}, f32[256]{0:T(256)}, u32[]{:S(2)}) copy-start(f32[256]{0:T(256)} %nb2_ref.1) | copy-start | bytes 3076
  5.8 5.4 %copy-start.15 = (s32[64]{0:T(128)S(1)}, s32[64]{0:T(128)}, u32[]{:S(2)}) copy-start(s32[64]{0:T(128)} %sea_ref.1) | copy-start | bytes 772
  6.0 5.3 %copy-start.8 = (s32[1024]{0:T(1024)S(1)}, s32[1024]{0:T(1024)}, u32[]{:S(2)}) copy-start(s32[1024]{0:T(1024)} %param.21) | copy-start | bytes 12292
  6.0 7.0 %collective-permute-start.2 = (bf16[32,256]{1,0:T(8,128)(2,1)S(1)}, bf16[32,256]{1,0:T(8,128)(2,1)S(1)}, u32[]{:S(2)}, u32[]{:S(2)}) collective-permute-start(bf16[32,256]{1,0:T(8,128)(2,1)S(1)} %get-tuple-element.98), channel_id=1, source_target_pairs={{0,2},{1,3},{2,0},{3,1},{4,6},{5,7},{6,4},{7,5},{8,10},{9,11},{10,... | collective-permute-start | bytes 49160 | tf_op jit(solution)/shard_map/ppermute | solution.py:126
  6.0 7.0 %collective-permute-start.1 = (bf16[32,256]{1,0:T(8,128)(2,1)S(1)}, bf16[32,256]{1,0:T(8,128)(2,1)S(1)}, u32[]{:S(2)}, u32[]{:S(2)}) collective-permute-start(bf16[32,256]{1,0:T(8,128)(2,1)S(1)} %get-tuple-element.98), channel_id=1, source_target_pairs={{0,30},{1,31},{2,4},{3,5},{4,2},{5,3},{6,8},{7,9},{8,6},{9,7},{10,... | collective-permute-start | bytes 49160 | tf_op jit(solution)/shard_map/ppermute | solution.py:126
  11.2 0.7 %copy-start.10 = (f32[256]{0:T(256)S(1)}, f32[256]{0:T(256)}, u32[]{:S(2)}) copy-start(f32[256]{0:T(256)} %b1_ref.1) | copy-start | bytes 3076
  11.2 0.7 %copy-start.14 = (s32[16]{0:T(128)S(1)}, s32[16]{0:T(128)}, u32[]{:S(2)}) copy-start(s32[16]{0:T(128)} %be_ref.1) | copy-start | bytes 196
  11.9 1.2 %copy-start = (bf16[256,256]{1,0:T(8,128)(2,1)S(1)}, bf16[256,256]{1,0:T(8,128)(2,1)}, u32[]{:S(2)}) copy-start(bf16[256,256]{1,0:T(8,128)(2,1)} %w2_ref.3) | copy-start | bytes 393220
  11.9 1.2 %copy-start.3 = (bf16[64,256]{1,0:T(8,128)(2,1)S(1)}, bf16[64,256]{1,0:T(8,128)(2,1)}, u32[]{:S(2)}) copy-start(bf16[64,256]{1,0:T(8,128)(2,1)} %refs_5_.1) | copy-start | bytes 98308
  13.1 5.9 %copy-start.1 = (bf16[1024,256]{1,0:T(8,128)(2,1)S(1)}, bf16[1024,256]{1,0:T(8,128)(2,1)}, u32[]{:S(2)}) copy-start(bf16[1024,256]{1,0:T(8,128)(2,1)} %geo_ref.1) | copy-start | bytes 1572868
  13.1 5.9 %copy-start.2 = (bf16[512,256]{1,0:T(8,128)(2,1)S(1)}, bf16[512,256]{1,0:T(8,128)(2,1)}, u32[]{:S(2)}) copy-start(bf16[512,256]{1,0:T(8,128)(2,1)} %nw1_ref.1) | copy-start | bytes 786436
  13.1 5.9 %copy-start.4 = (bf16[256,256]{1,0:T(8,128)(2,1)S(1)}, bf16[256,256]{1,0:T(8,128)(2,1)}, u32[]{:S(2)}) copy-start(bf16[256,256]{1,0:T(8,128)(2,1)} %nw2_ref.1) | copy-start | bytes 393220
  14.3 4.7 %collective-permute-start.3 = (bf16[192,256]{1,0:T(8,128)(2,1)S(1)}, bf16[192,256]{1,0:T(8,128)(2,1)S(1)}, u32[]{:S(2)}, u32[]{:S(2)}) collective-permute-start(bf16[192,256]{1,0:T(8,128)(2,1)S(1)} %get-tuple-element.108.refs_0_), channel_id=1, source_target_pairs={{0,1},{1,0},{2,3},{3,2},{4,5},{5,4},{6,7},{7,6},{8,9},{9,8},{10,11... | collective-permute-start | bytes 294920 | tf_op jit(solution)/shard_map/ppermute | solution.py:126
  22.2 1.9 %collective-permute-start.4 = (bf16[928,256]{1,0:T(8,128)(2,1)S(1)}, bf16[928,256]{1,0:T(8,128)(2,1)S(1)}, u32[]{:S(2)}, u32[]{:S(2)}) collective-permute-start(bf16[928,256]{1,0:T(8,128)(2,1)S(1)} %get-tuple-element.110), channel_id=1, source_target_pairs={{0,2},{1,3},{2,0},{3,1},{4,6},{5,7},{6,4},{7,5},{8,10},{9,11},{10,... | collective-permute-start | bytes 1425416 | tf_op jit(solution)/shard_map/ppermute | solution.py:126
  24.3 4.9 %collective-permute-start.5 = (bf16[232,256]{1,0:T(8,128)(2,1)S(1)}, bf16[232,256]{1,0:T(8,128)(2,1)S(1)}, u32[]{:S(2)}, u32[]{:S(2)}) collective-permute-start(bf16[232,256]{1,0:T(8,128)(2,1)S(1)} %get-tuple-element.112), channel_id=1, source_target_pairs={{0,1},{1,0},{2,10},{3,11},{4,5},{5,4},{6,14},{7,15},{8,9},{9,8},{1... | collective-permute-start | bytes 356360 | tf_op jit(solution)/shard_map/ppermute | solution.py:126
  25.8 6.1 %collective-permute-start.6 = (bf16[232,256]{1,0:T(8,128)(2,1)S(1)}, bf16[232,256]{1,0:T(8,128)(2,1)S(1)}, u32[]{:S(2)}, u32[]{:S(2)}) collective-permute-start(bf16[232,256]{1,0:T(8,128)(2,1)S(1)} %get-tuple-element.113), channel_id=1, source_target_pairs={{0,4},{1,5},{2,18},{3,19},{4,0},{5,1},{6,22},{7,23},{8,12},{9,13},... | collective-permute-start | bytes 356360 | tf_op jit(solution)/shard_map/ppermute | solution.py:126
  25.8 6.1 %collective-permute-start.7 = (bf16[232,256]{1,0:T(8,128)(2,1)S(1)}, bf16[232,256]{1,0:T(8,128)(2,1)S(1)}, u32[]{:S(2)}, u32[]{:S(2)}) collective-permute-start(bf16[232,256]{1,0:T(8,128)(2,1)S(1)} %get-tuple-element.114), channel_id=1, source_target_pairs={{0,5},{1,4},{2,26},{3,27},{4,1},{5,0},{6,30},{7,31},{8,13},{9,12},... | collective-permute-start | bytes 356360 | tf_op jit(solution)/shard_map/ppermute | solution.py:126
  32.0 15.0 %collective-permute-start.10 = (bf16[232,256]{1,0:T(8,128)(2,1)S(1)}, bf16[232,256]{1,0:T(8,128)(2,1)S(1)}, u32[]{:S(2)}, u32[]{:S(2)}) collective-permute-start(bf16[232,256]{1,0:T(8,128)(2,1)S(1)} %shard_map.245.refs_0_), channel_id=1, source_target_pairs={{0,24},{1,25},{2,7},{3,6},{4,28},{5,29},{6,3},{7,2},{8,16},{9,17},... | collective-permute-start | bytes 356360 | tf_op jit(solution)/shard_map/ppermute | solution.py:126
  35.1 11.9 %collective-permute-start.9 = (bf16[232,256]{1,0:T(8,128)(2,1)S(1)}, bf16[232,256]{1,0:T(8,128)(2,1)S(1)}, u32[]{:S(2)}, u32[]{:S(2)}) collective-permute-start(bf16[232,256]{1,0:T(8,128)(2,1)S(1)} %shard_map.245.refs_0_), channel_id=1, source_target_pairs={{0,16},{1,17},{2,6},{3,7},{4,20},{5,21},{6,2},{7,3},{8,24},{9,25},... | collective-permute-start | bytes 356360 | tf_op jit(solution)/shard_map/ppermute | solution.py:126
  35.1 11.9 %collective-permute-start.8 = (bf16[232,256]{1,0:T(8,128)(2,1)S(1)}, bf16[232,256]{1,0:T(8,128)(2,1)S(1)}, u32[]{:S(2)}, u32[]{:S(2)}) collective-permute-start(bf16[232,256]{1,0:T(8,128)(2,1)S(1)} %shard_map.245.refs_0_), channel_id=1, source_target_pairs={{0,8},{1,9},{2,3},{3,2},{4,12},{5,13},{6,7},{7,6},{8,0},{9,1},{10,... | collective-permute-start | bytes 356360 | tf_op jit(solution)/shard_map/ppermute | solution.py:126
  36.4 4.6 %collective-permute-start.11 = (bf16[192,256]{1,0:T(8,128)(2,1)S(1)}, bf16[192,256]{1,0:T(8,128)(2,1)S(1)}, u32[]{:S(2)}, u32[]{:S(2)}) collective-permute-start(bf16[192,256]{1,0:T(8,128)(2,1)S(1)} %get-tuple-element.115.refs_0_), channel_id=1, source_target_pairs={{0,1},{1,0},{2,3},{3,2},{4,5},{5,4},{6,7},{7,6},{8,9},{9,8},{10,11... | collective-permute-start | bytes 294920 | tf_op jit(solution)/shard_map/ppermute | solution.py:126
  41.1 5.9 %collective-permute-start.12 = (bf16[32,256]{1,0:T(8,128)(2,1)S(1)}, bf16[32,256]{1,0:T(8,128)(2,1)S(1)}, u32[]{:S(2)}, u32[]{:S(2)}) collective-permute-start(bf16[32,256]{1,0:T(8,128)(2,1)S(1)} %get-tuple-element.116), channel_id=1, source_target_pairs={{0,30},{1,31},{2,4},{3,5},{4,2},{5,3},{6,8},{7,9},{8,6},{9,7},{10,... | collective-permute-start | bytes 49160 | tf_op jit(solution)/shard_map/ppermute | solution.py:126
  42.1 4.9 %collective-permute-start.13 = (bf16[32,256]{1,0:T(8,128)(2,1)S(1)}, bf16[32,256]{1,0:T(8,128)(2,1)S(1)}, u32[]{:S(2)}, u32[]{:S(2)}) collective-permute-start(bf16[32,256]{1,0:T(8,128)(2,1)S(1)} %get-tuple-element.117), channel_id=1, source_target_pairs={{0,2},{1,3},{2,0},{3,1},{4,6},{5,7},{6,4},{7,5},{8,10},{9,11},{10,... | collective-permute-start | bytes 49160 | tf_op jit(solution)/shard_map/ppermute | solution.py:126
  47.3 3.6 %collective-permute-start.14 = (bf16[232,256]{1,0:T(8,128)(2,1)S(1)}, bf16[232,256]{1,0:T(8,128)(2,1)S(1)}, u32[]{:S(2)}, u32[]{:S(2)}) collective-permute-start(bf16[232,256]{1,0:T(8,128)(2,1)S(1)} %get-tuple-element.118.refs_0_), channel_id=1, source_target_pairs={{0,2},{1,3},{2,0},{3,1},{4,6},{5,7},{6,4},{7,5},{8,10},{9,11},{10,... | collective-permute-start | bytes 356360 | tf_op jit(solution)/shard_map/ppermute | solution.py:126
  47.3 5.9 %collective-permute-start.16 = (bf16[232,256]{1,0:T(8,128)(2,1)S(1)}, bf16[232,256]{1,0:T(8,128)(2,1)S(1)}, u32[]{:S(2)}, u32[]{:S(2)}) collective-permute-start(bf16[232,256]{1,0:T(8,128)(2,1)S(1)} %get-tuple-element.118.refs_0_), channel_id=1, source_target_pairs={{0,5},{1,4},{2,26},{3,27},{4,1},{5,0},{6,30},{7,31},{8,13},{9,12},... | collective-permute-start | bytes 356360 | tf_op jit(solution)/shard_map/ppermute | solution.py:126
  47.4 6.9 %collective-permute-start.15 = (bf16[232,256]{1,0:T(8,128)(2,1)S(1)}, bf16[232,256]{1,0:T(8,128)(2,1)S(1)}, u32[]{:S(2)}, u32[]{:S(2)}) collective-permute-start(bf16[232,256]{1,0:T(8,128)(2,1)S(1)} %get-tuple-element.118.refs_0_), channel_id=1, source_target_pairs={{0,4},{1,5},{2,18},{3,19},{4,0},{5,1},{6,22},{7,23},{8,12},{9,13},... | collective-permute-start | bytes 356360 | tf_op jit(solution)/shard_map/ppermute | solution.py:126
  49.9 4.8 %collective-permute-start.18 = (bf16[232,256]{1,0:T(8,128)(2,1)S(1)}, bf16[232,256]{1,0:T(8,128)(2,1)S(1)}, u32[]{:S(2)}, u32[]{:S(2)}) collective-permute-start(bf16[232,256]{1,0:T(8,128)(2,1)S(1)} %get-tuple-element.118.refs_0_), channel_id=1, source_target_pairs={{0,1},{1,0},{2,10},{3,11},{4,5},{5,4},{6,14},{7,15},{8,9},{9,8},{1... | collective-permute-start | bytes 356360 | tf_op jit(solution)/shard_map/ppermute | solution.py:126
  53.2 2.6 %collective-permute-start.20 = (bf16[232,256]{1,0:T(8,128)(2,1)S(1)}, bf16[232,256]{1,0:T(8,128)(2,1)S(1)}, u32[]{:S(2)}, u32[]{:S(2)}) collective-permute-start(bf16[232,256]{1,0:T(8,128)(2,1)S(1)} %collective-permute-done.16.refs_0_), channel_id=1, source_target_pairs={{0,2},{1,3},{2,0},{3,1},{4,6},{5,7},{6,4},{7,5},{8,10},{9,11},{10,... | collective-permute-start | bytes 356360 | tf_op jit(solution)/shard_map/ppermute | solution.py:126
  54.7 2.2 %collective-permute-start.19 = (bf16[232,256]{1,0:T(8,128)(2,1)S(1)}, bf16[232,256]{1,0:T(8,128)(2,1)S(1)}, u32[]{:S(2)}, u32[]{:S(2)}) collective-permute-start(bf16[232,256]{1,0:T(8,128)(2,1)S(1)} %collective-permute-done.18.refs_1_), channel_id=1, source_target_pairs={{0,2},{1,3},{2,0},{3,1},{4,6},{5,7},{6,4},{7,5},{8,10},{9,11},{10,... | collective-permute-start | bytes 356360 | tf_op jit(solution)/shard_map/ppermute | solution.py:126
  55.9 1.3 %collective-permute-start.17 = (bf16[232,256]{1,0:T(8,128)(2,1)S(1)}, bf16[232,256]{1,0:T(8,128)(2,1)S(1)}, u32[]{:S(2)}, u32[]{:S(2)}) collective-permute-start(bf16[232,256]{1,0:T(8,128)(2,1)S(1)} %collective-permute-done.15.refs_0_), channel_id=1, source_target_pairs={{0,2},{1,3},{2,0},{3,1},{4,6},{5,7},{6,4},{7,5},{8,10},{9,11},{10,... | collective-permute-start | bytes 356360 | tf_op jit(solution)/shard_map/ppermute | solution.py:126
